TPU v7x, 32 devices: a whole 2x2x4 slice. The times are simulated.
32 devices in a mesh: coef: 16 (over z, y, x), rot: 2 (over core).
Axes of the slice: x: 2, y: 2, z: 4, core: 2. Of those that a mesh axis runs over, the one named last changes fastest.
Arguments:
- features: float32 [256, 47872], P(None, 'coef'), may hold values from -200 to 200
- table: float32 [2048, 47872], P('rot', 'coef'), may hold values from -16 to 16
- targets: float32 [256, 2048], P('coef', 'rot'), may hold values from 0 to 1
Outputs:
- grad_features: float32 [256, 47872], P('rot', 'coef')
- grad_table: float32 [2048, 47872], P('rot', 'coef')
All inputs are finite; a program needn't handle non-finite values.
Results may differ from a plain program's by a relative error of at most 0.0003.
Values sent between devices are 32-bit elements; how exact they have to be, the bound alone decides.
No kernel may reach another device: no remote copies, remote signals or barrier semaphores. Data moves between devices by JAX's collectives and lax.ppermute only.
A program may use at most 64 MiB of HBM per device.

v0:
```python
import math

import jax
import jax.numpy as jnp
from jax import lax
from jax.sharding import PartitionSpec as P

K = 47872


logit_gain = 4.0
loss_scale = 64.0


def on_device(features, table, targets):
    scale = logit_gain / math.sqrt(K)
    partial_value = lax.dot_general(
        features,
        table,
        (((1,), (1,)), ((), ())),
        precision=lax.Precision.HIGHEST,
        preferred_element_type=jnp.float32,
    )
    summed = lax.psum_scatter(partial_value, "coef", scatter_dimension=0, tiled=True)
    scores = scale * summed
    local_max = jnp.max(scores, axis=1)
    row_max = lax.pmax(local_max, "rot")
    expo = jnp.exp(scores - row_max[:, None])
    row_total = lax.psum(jnp.sum(expo, axis=1), "rot")
    probs = expo / row_total[:, None]
    grad_scores = loss_scale * (probs - targets)
    piece = lax.all_gather(grad_scores, "coef", axis=0, tiled=True)
    table_part = lax.dot_general(
        piece,
        features,
        (((0,), (0,)), ((), ())),
        precision=lax.Precision.HIGHEST,
        preferred_element_type=jnp.float32,
    )
    feature_part = jnp.dot(
        piece, table, precision=lax.Precision.HIGHEST, preferred_element_type=jnp.float32
    )
    grad_features = scale * lax.psum_scatter(feature_part, "rot", scatter_dimension=0, tiled=True)
    grad_table = scale * table_part
    return (grad_features, grad_table)


def solution(mesh):
    return jax.shard_map(
        on_device,
        mesh=mesh,
        in_specs=(P(None, "coef"), P("rot", "coef"), P("coef", "rot")),
        out_specs=(P("rot", "coef"), P("rot", "coef")),
        check_vma=False,
    )
```

profile of v0, /device:TPU:0, one launch (start us, length us, event | category | flops | bytes accessed | tf_op | source)
XLA Modules:
  0.0 202.1 jit_solution(17302437431089537872)
XLA Ops:
  7.2 0.0 copy-start
  7.2 0.0 copy-start.1
  7.2 0.0 reduce-scatter.3.cloned.1.call-start
  7.2 1.8 copy-done
  9.0 14.6 %fusion.1 = f32[256,1024]{1,0:T(8,128)} fusion(f32[256,2992]{0,1:T(8,128)S(1)} %copy-done, f32[1024,2992]{0,1:T(8,128)} %param.4), kind=kOutput, calls=%fused_computation.6 | convolution fusion | flops 9412018176 | bytes 16367616 | tf_op jit(solution)/shard_map/dot_general | solution.py:17
  23.6 0.0 reduce-scatter.3.cloned.1.call-update
  23.7 0.0 all-gather.2.cloned.1.call-start
  23.7 81.6 %reduce-scatter.3.cloned.1.call-done = f32[16,1024]{1,0:T(8,128)} async-done(((f32[256,1024]{1,0:T(8,128)}), f32[16,1024]{1,0:T(8,128)}) %reduce-scatter.3.cloned.1.call-update) | async-done | bytes 65552 | tf_op jit(solution)/shard_map/reduce_scatter | solution.py:24
  105.3 1.0 multiply_reduce_fusion
  106.3 2.5 %pmax.7 = f32[16]{0:T(128)S(1)} all-reduce(f32[16]{0:T(128)S(1)} %multiply_reduce_fusion), channel_id=1, replica_groups=mesh['coef'=16,'rot'=2] {'rot'}, use_global_device_ids=true, to_apply=%region_2.0 | all-reduce | flops 16 | bytes 128 | tf_op jit(solution)/shard_map/pmax | solution.py:27
  108.8 1.0 fusion
  109.8 2.5 %psum.7 = f32[16]{0:T(128)S(1)} all-reduce(f32[16]{0:T(128)S(1)} %fusion), channel_id=1, replica_groups=mesh['coef'=16,'rot'=2] {'rot'}, use_global_device_ids=true, to_apply=%region_4.0 | all-reduce | flops 16 | bytes 128 | tf_op jit(solution)/shard_map/psum | solution.py:29
  112.3 0.0 copy-done.1
  112.3 1.6 subtract_multiply_fusion
  113.8 0.0 all-gather.2.cloned.1.call-update
  113.8 0.2 reduce-scatter.5.cloned.1.call-start
  114.1 51.3 %all-gather.2.cloned.1.call-done = f32[256,1024]{1,0:T(8,128)} async-done(((f32[16,1024]{1,0:T(8,128)}), f32[256,1024]{1,0:T(8,128)}) %all-gather.2.cloned.1.call-update) | async-done | bytes 1048592 | tf_op jit(solution)/shard_map/all_gather | solution.py:32
  165.4 13.5 %fusion.2 = f32[256,2992]{0,1:T(8,128)} fusion(f32[256,1024]{1,0:T(8,128)} %all-gather.2.cloned.1.call-done, f32[1024,2992]{0,1:T(8,128)} %param.4), kind=kOutput, calls=%fused_computation.7 | convolution fusion | flops 9412018176 | bytes 16367616 | tf_op jit(solution)/shard_map/dot_general | solution.py:40
  178.9 0.0 reduce-scatter.5.cloned.1.call-update
  178.9 14.0 %convolution_multiply_fusion = f32[1024,2992]{0,1:T(8,128)} fusion(f32[256,1024]{1,0:T(8,128)} %all-gather.2.cloned.1.call-done, f32[256,2992]{0,1:T(8,128)S(1)} %copy-done), kind=kOutput, calls=%fused_computation | convolution fusion | flops 9415081984 | bytes 16367616 | tf_op jit(solution)/shard_map/dot_general | solution.py:33
  192.9 0.0 reduce-scatter.5.cloned.1.call-done
  192.9 2.7 %broadcast_multiply_fusion = f32[128,2992]{0,1:T(8,128)} fusion(f32[128,2992]{0,1:T(8,128)} %reduce-scatter.5.cloned.1.call-done), kind=kLoop, calls=%fused_computation.1 | loop fusion | flops 382976 | bytes 3063808 | tf_op jit(solution)/shard_map/mul | solution.py:43
Async XLA Ops:
  7.2 1.9 copy-start
  7.2 105.1 %copy-start.1 = (f32[16,1024]{1,0:T(8,128)S(1)}, f32[16,1024]{1,0:T(8,128)}, u32[]{:S(2)}) copy-start(f32[16,1024]{1,0:T(8,128)} %param.5) | copy-start | bytes 196612
  7.2 98.1 %reduce-scatter.3.cloned.1.call-start = ((), (), s32[]{:S(2)}) async-start(), calls=%async_computation.2 | async-start | bytes 1114112 | tf_op jit(solution)/shard_map/reduce_scatter | solution.py:24
  23.7 141.8 %all-gather.2.cloned.1.call-start = ((), (), s32[]{:S(2)}) async-start(), calls=%async_computation.3 | async-start | bytes 1114112 | tf_op jit(solution)/shard_map/all_gather | solution.py:32
  113.8 79.1 %reduce-scatter.5.cloned.1.call-start = ((), (), s32[]{:S(2)}) async-start(), calls=%async_computation.4 | async-start | bytes 4595712 | tf_op jit(solution)/shard_map/reduce_scatter | solution.py:43
Sparse Core Ops, SparseCore 0:
  23.8 81.4 reduce-scatter.2
  114.0 51.4 all-gather.1
  179.0 9.6 reduce-scatter.4
where the time goes:
time: 202 us
  waiting for transfers between devices  133 us (66%)
  matrix products  42.1 us (21%)
  between operations  13.8 us (7%)
  other arithmetic  6.2 us (3%)
  blocking collectives  4.93 us (2%)
    reduce_scatter x1, waiting for transfers between devices, on_device(): lax.psum_scatter(partial_value, 'coef', scatter_dimension=0, tiled=True)  81.6 us
    all_gather x1, waiting for transfers between devices, on_device(): piece = lax.all_gather(grad_scores, 'coef', axis=0, tiled=True)  51.3 us
    dot_general x1, matrix products, on_device(): lax.dot_general(features, table, (((1,), (1,)), ((), ())), precision=lax....  14.6 us
    dot_general x1, matrix products, on_device(): lax.dot_general(piece, features, (((0,), (0,)), ((), ())), precision=lax....  14 us
    dot_general x1, matrix products, on_device(): jnp.dot(piece, table, precision=lax.Precision.HIGHEST, preferred_element_...  13.5 us
  transfers between devices with their start and end apart: 3, of which 2 were waited for; matrix products, arithmetic and copies ran while one was open for 7% of the time, Pallas kernels for 0%

commit v1 on v0

v1 whole, which is shorter than its diff:
```python
import math

import jax
import jax.numpy as jnp
from jax import lax
from jax.sharding import PartitionSpec as P

logit_gain = 4.0
loss_scale = 64.0


def solution(mesh):
    n = mesh.shape["coef"]
    r = mesh.shape["rot"]
    g = math.gcd(n, 8)
    m = n // g
    inner = [[a * g + b for b in range(g)] for a in range(m)]
    outer = [[a * g + b for a in range(m)] for b in range(g)]
    swap = [(i, (i + g) % n) for i in range(n)]
    rot_swap = [(0, 1), (1, 0)]

    def add_cubes(x):
        if m == 1:
            return x
        if m == 2:
            return x + lax.ppermute(x, "coef", swap)
        return lax.psum(x, "coef", axis_index_groups=outer)

    def join_cubes(x):
        if m == 1:
            return x[None]
        if m == 2:
            other = lax.ppermute(x, "coef", swap)
            first = lax.axis_index("coef") < g
            return jnp.where(first, jnp.stack([x, other]), jnp.stack([other, x]))
        return lax.all_gather(x, "coef", axis_index_groups=outer)

    def on_device(features, table, targets):
        imgs, k = features.shape
        rots = table.shape[0]
        rows = imgs // n
        scale = logit_gain / math.sqrt(k * n)
        high = dict(precision=lax.Precision.HIGH, preferred_element_type=jnp.float32)
        goal = join_cubes(targets)

        partial = lax.dot_general(features, table, (((1,), (1,)), ((), ())), **high)
        blocks = partial.reshape(m, g, rows, rots).transpose(1, 0, 2, 3)
        blocks = lax.all_to_all(blocks, "coef", 0, 0, axis_index_groups=inner, tiled=True)
        scores = scale * add_cubes(jnp.sum(blocks, axis=0))

        top = jnp.max(scores, axis=2, keepdims=True)
        expo = jnp.exp(scores - top)
        total = jnp.sum(expo, axis=2, keepdims=True)
        if r == 2:
            both = jnp.concatenate([top, total], axis=2)
            far = lax.ppermute(both, "rot", rot_swap)
            far_top, far_total = far[:, :, :1], far[:, :, 1:]
            row_max = jnp.maximum(top, far_top)
            ours = jnp.exp(top - row_max)
            row_sum = total * ours + far_total * jnp.exp(far_top - row_max)
        else:
            row_max = lax.pmax(top, "rot")
            ours = jnp.exp(top - row_max)
            row_sum = lax.psum(total * ours, "rot")
        probs = expo * (ours / row_sum)
        grad = (scale * loss_scale) * (probs - goal)

        wide = jnp.broadcast_to(grad[None], (g,) + grad.shape)
        piece = lax.all_to_all(wide, "coef", 0, 0, axis_index_groups=inner, tiled=True)
        piece = piece.transpose(1, 0, 2, 3).reshape(imgs, rots)

        feature_part = jnp.dot(piece, table, **high)
        if r == 2:
            half = imgs // 2
            me = lax.axis_index("rot")
            send = lax.dynamic_slice_in_dim(feature_part, (1 - me) * half, half)
            keep = lax.dynamic_slice_in_dim(feature_part, me * half, half)
            grad_features = keep + lax.ppermute(send, "rot", rot_swap)
        else:
            grad_features = lax.psum_scatter(feature_part, "rot", scatter_dimension=0, tiled=True)
        grad_table = lax.dot_general(piece, features, (((0,), (0,)), ((), ())), **high)
        return (grad_features, grad_table)

    return jax.shard_map(
        on_device,
        mesh=mesh,
        in_specs=(P(None, "coef"), P("rot", "coef"), P("coef", "rot")),
        out_specs=(P("rot", "coef"), P("rot", "coef")),
        check_vma=False,
    )
```

time: 202 us -> 90 us (0.45)
  waiting for transfers between devices: 133 us -> 23 us
  matrix products: 42.1 us -> 25.8 us
  blocking collectives: 4.93 us -> 21.2 us
  between operations: 13.8 us -> 0.75 us
  starting transfers between devices: 0.3 us -> 7.3 us
  local copies, waits for them, and re-layouts: 1.81 us -> 7.26 us
    reduce_scatter x2 -> x0, waiting for transfers between devices: 81.6 us -> none  [the longest x1 81.6 us: on_device(): lax.psum_scatter(partial_value, 'coef', scatter_dimension=0, tiled=True)]
    all_gather x1 -> x0, waiting for transfers between devices: 51.3 us -> none  [on_device(): piece = lax.all_gather(grad_scores, 'coef', axis=0, tiled=True)]
    all_to_all x0 -> x1, blocking collectives: none -> 21.2 us  [on_device(): lax.all_to_all(blocks, 'coef', 0, 0, axis_index_groups=inner, tiled=True)]
    dot_general x3, matrix products: 42.1 us -> 25.8 us  [the longest x1 9.21 us: on_device(): lax.dot_general(piece, features, (((0,), (0,)), ((), ())), **high)]
    all_to_all x0 -> x1, waiting for transfers between devices: none -> 15.2 us  [on_device(): lax.all_to_all(wide, 'coef', 0, 0, axis_index_groups=inner, tiled=True)]
    ppermute x0 -> x4, waiting for transfers between devices: none -> 7.78 us  [the longest x1 6.63 us: add_cubes(): return x + lax.ppermute(x, 'coef', swap)]
    all_to_all x0 -> x1, starting transfers between devices: none -> 4.24 us  [on_device(): lax.all_to_all(wide, 'coef', 0, 0, axis_index_groups=inner, tiled=True)]
    mul x2, other arithmetic: 4.21 us -> 0.11 us  [the longest x1 0.1 us: on_device(): grad = scale * loss_scale * (probs - goal)]
  transfers between devices with their start and end apart: 3 -> 5, of which waited for: 2 -> 3; matrix products, arithmetic and copies ran while one was open for 7% -> 11% of each run, Pallas kernels for 0% -> 0%
where the time goes in v1:
time: 90 us; the launch traced here: 89.7 us
  matrix products  25.8 us (29%)
  waiting for transfers between devices  23 us (26%)
  blocking collectives  21.2 us (24%)
  starting transfers between devices  7.3 us (8%)
  local copies, waits for them, and re-layouts  7.26 us (8%)
  other arithmetic  4.41 us (5%)
    all_to_all x1, blocking collectives, on_device(): lax.all_to_all(blocks, 'coef', 0, 0, axis_index_groups=inner, tiled=True)  21.2 us
    all_to_all x1, waiting for transfers between devices, on_device(): lax.all_to_all(wide, 'coef', 0, 0, axis_index_groups=inner, tiled=True)  15.2 us
    dot_general x1, matrix products, on_device(): lax.dot_general(piece, features, (((0,), (0,)), ((), ())), **high)  9.21 us
    dot_general x1, matrix products, on_device(): feature_part = jnp.dot(piece, table, **high)  8.46 us
    dot_general x1, matrix products, on_device(): partial = lax.dot_general(features, table, (((1,), (1,)), ((), ())), **high)  8.15 us
    ppermute x1, waiting for transfers between devices, add_cubes(): return x + lax.ppermute(x, 'coef', swap)  6.63 us
    all_to_all x1, starting transfers between devices, on_device(): lax.all_to_all(wide, 'coef', 0, 0, axis_index_groups=inner, tiled=True)  4.24 us
    unnamed x10, local copies, waits for them, and re-layouts  3.52 us
  transfers between devices with their start and end apart: 5, of which 3 were waited for; matrix products, arithmetic and copies ran while one was open for 11% of the time, Pallas kernels for 0%

profile of v1, /device:TPU:0, one launch (start us, length us, event | category | flops | bytes accessed | tf_op | source)
XLA Modules:
  0.0 89.7 jit_solution(16654040654146555134)
XLA Ops:
  0.6 0.0 copy-start
  0.6 1.9 %copy-done = f32[256,2992]{0,1:T(8,128)S(1)} copy-done((f32[256,2992]{0,1:T(8,128)S(1)}, f32[256,2992]{0,1:T(8,128)}, u32[]{:S(2)}) %copy-start) | copy-done | bytes 3063832
  2.5 8.1 %fusion.10 = f32[256,1024]{1,0:T(8,128)S(1)} fusion(f32[256,2992]{0,1:T(8,128)S(1)} %copy-done, f32[1024,2992]{0,1:T(8,128)} %param.4), kind=kOutput, calls=%fused_computation.19 | convolution fusion | flops 4706009088 | bytes 16367616 | tf_op jit(solution)/shard_map/dot_general | solution.py:46
  10.7 0.0 copy-start.4
  10.7 0.1 copy.8
  10.8 21.2 %all_to_all.10 = f32[8,2,16,1024]{3,2,1,0:T(8,128)} all-to-all(f32[8,2,16,1024]{3,2,1,0:T(8,128)S(1)} %bitcast.24), channel_id=1, replica_groups={{0,2,4,6,8,10,12,14},{16,18,20,22,24,26,28,30},{1,3,5,7,9,11,13,15},{17..., dimensions={0} | all-to-all | bytes 2097152 | tf_op jit(solution)/shard_map/all_to_all | solution.py:48
  31.9 1.3 %reduce_sum.18 = f32[2,16,1024]{2,1,0:T(8,128)S(1)} reduce(f32[8,2,16,1024]{3,2,1,0:T(8,128)} %all_to_all.10, f32[]{:T(128)} %constant.11.clone.1), dimensions={0}, to_apply=%region_0.1 | reduce | flops 229376 | bytes 1179652 | tf_op jit(solution)/shard_map/reduce_sum | solution.py:49
  33.2 2.7 %collective-permute-start = (f32[2,16,1024]{2,1,0:T(8,128)S(1)}, f32[2,16,1024]{2,1,0:T(8,128)S(1)}, u32[]{:S(2)}, u32[]{:S(2)}) collective-permute-start(f32[2,16,1024]{2,1,0:T(8,128)S(1)} %reduce_sum.18), channel_id=1, source_target_pairs={{0,16},{2,18},{4,20},{6,22},{8,24},{10,26},{12,28},{14,30},{16,0},... | collective-permute-start | bytes 393224 | tf_op jit(solution)/shard_map/ppermute | solution.py:26
  35.9 0.0 copy-done.4
  35.9 0.3 collective-permute-start.2
  36.2 6.6 %collective-permute-done = f32[2,16,1024]{2,1,0:T(8,128)S(1)} collective-permute-done((f32[2,16,1024]{2,1,0:T(8,128)S(1)}, f32[2,16,1024]{2,1,0:T(8,128)S(1)}, u32[]{:S(2)}, u32[]{:S(2)}) %collective-permute-start) | collective-permute-done | bytes 131104 | tf_op jit(solution)/shard_map/ppermute | solution.py:26
  42.8 0.1 fusion.9
  42.9 0.2 fusion.2
  43.1 0.1 collective-permute-start.1
  43.2 1.1 %collective-permute-done.1 = f32[2,16,2]{1,0,2:T(2,128)S(1)} collective-permute-done((f32[2,16,2]{1,0,2:T(2,128)S(1)}, f32[2,16,2]{1,0,2:T(2,128)S(1)}, u32[]{:S(2)}, u32[]{:S(2)}) %collective-permute-start.1) | collective-permute-done | bytes 288 | tf_op jit(solution)/shard_map/ppermute | solution.py:56
  44.4 0.0 collective-permute-done.2
  44.4 0.1 fusion.1
  44.5 1.1 %broadcast_in_dim.14 = f32[8,2,16,1024]{3,2,1,0:T(8,128)} broadcast(f32[2,16,1024]{2,1,0:T(8,128)S(1)} %fusion.1), dimensions={1,2,3} | broadcast | bytes 1179648 | tf_op jit(solution)/shard_map/broadcast_in_dim | solution.py:68
  45.6 4.2 %all-to-all-start.1 = ((f32[8,2,16,1024]{3,2,1,0:T(8,128)}), f32[8,2,16,1024]{3,2,1,0:T(8,128)}, u32[]{:S(2)}, u32[]{:S(2)}) async-start(f32[8,2,16,1024]{3,2,1,0:T(8,128)} %broadcast_in_dim.14), calls=%async_computation.1 | async-start | bytes 2097152 | tf_op jit(solution)/shard_map/all_to_all | solution.py:69
  49.8 15.2 %all-to-all-done.1 = f32[8,2,16,1024]{3,2,1,0:T(8,128)} async-done(((f32[8,2,16,1024]{3,2,1,0:T(8,128)}), f32[8,2,16,1024]{3,2,1,0:T(8,128)}, u32[]{:S(2)}, u32[]{:S(2)}) %all-to-all-start.1) | async-done | bytes 1048608 | tf_op jit(solution)/shard_map/all_to_all | solution.py:69
  65.0 1.3 %copy.6 = f32[8,2,16,1024]{3,2,0,1:T(8,128)S(1)} copy(f32[8,2,16,1024]{3,2,1,0:T(8,128)} %all-to-all-done.1) | data formatting | bytes 2097152 | tf_op jit(solution)/shard_map/all_to_all | solution.py:69
  66.4 0.0 copy-start.3
  66.4 8.5 %fusion.11 = f32[256,2992]{0,1:T(8,128)S(1)} fusion(f32[256,1024]{1,0:T(8,128)S(1)} %bitcast.21, f32[1024,2992]{0,1:T(8,128)} %param.4), kind=kOutput, calls=%fused_computation.20 | convolution fusion | flops 4706009088 | bytes 16367616 | tf_op jit(solution)/shard_map/dot_general | solution.py:72
  74.8 0.0 copy-done.3
  74.8 0.0 copy-start.1
  74.9 1.6 %copy-done.1 = f32[256,2992]{0,1:T(8,128)} copy-done((f32[256,2992]{0,1:T(8,128)}, f32[256,2992]{0,1:T(8,128)S(1)}, u32[]{:S(2)}) %copy-start.1) | copy-done | bytes 3063832
  76.5 1.2 %constant_dynamic-slice_fusion = f32[128,2992]{0,1:T(8,128)} fusion(f32[256,2992]{0,1:T(8,128)S(1)} %fusion.11, s32[]{:T(128)S(6)} %select_n.17), kind=kLoop, calls=%fused_computation.17 | loop fusion | bytes 3063812 | tf_op jit(solution)/shard_map/dynamic_slice | solution.py:76
  77.7 0.0 collective-permute-start.3
  77.7 9.2 %fusion.12 = f32[1024,2992]{0,1:T(8,128)} fusion(f32[256,1024]{1,0:T(8,128)} %bitcast.22, f32[256,2992]{0,1:T(8,128)S(1)} %copy-done), kind=kOutput, calls=%fused_computation.21 | convolution fusion | flops 4706009088 | bytes 16367616 | tf_op jit(solution)/shard_map/dot_general | solution.py:81
  86.9 0.0 collective-permute-done.3
  86.9 0.0 copy-done.2
  86.9 2.7 %dynamic-slice_add_fusion = f32[128,2992]{0,1:T(8,128)} fusion(f32[128,2992]{0,1:T(8,128)} %collective-permute-done.3, f32[256,2992]{0,1:T(8,128)S(1)} %copy-done.2, s32[]{:T(128)S(6)} %select_n.16), kind=kLoop, calls=%fused_computation | loop fusion | flops 382976 | bytes 4595716 | tf_op jit(solution)/shard_map/add | solution.py:78
  (3 shorter events, 0.0 us)
Async XLA Ops:
  0.6 1.9 %copy-start = (f32[256,2992]{0,1:T(8,128)S(1)}, f32[256,2992]{0,1:T(8,128)}, u32[]{:S(2)}) copy-start(f32[256,2992]{0,1:T(8,128)} %param.3) | copy-start | bytes 9191428
  10.7 25.2 %copy-start.4 = (f32[16,1024]{1,0:T(8,128)S(1)}, f32[16,1024]{1,0:T(8,128)}, u32[]{:S(2)}) copy-start(f32[16,1024]{1,0:T(8,128)} %param.5) | copy-start | bytes 196612
  33.2 9.6 %collective-permute-start = (f32[2,16,1024]{2,1,0:T(8,128)S(1)}, f32[2,16,1024]{2,1,0:T(8,128)S(1)}, u32[]{:S(2)}, u32[]{:S(2)}) collective-permute-start(f32[2,16,1024]{2,1,0:T(8,128)S(1)} %reduce_sum.18), channel_id=1, source_target_pairs={{0,16},{2,18},{4,20},{6,22},{8,24},{10,26},{12,28},{14,30},{16,0},... | collective-permute-start | bytes 393224 | tf_op jit(solution)/shard_map/ppermute | solution.py:26
  35.9 8.5 %collective-permute-start.2 = (f32[16,1024]{1,0:T(8,128)S(1)}, f32[16,1024]{1,0:T(8,128)S(1)}, u32[]{:S(2)}, u32[]{:S(2)}) collective-permute-start(f32[16,1024]{1,0:T(8,128)S(1)} %copy-done.4), channel_id=1, source_target_pairs={{0,16},{2,18},{4,20},{6,22},{8,24},{10,26},{12,28},{14,30},{16,0},... | collective-permute-start | bytes 196616 | tf_op jit(solution)/shard_map/ppermute | solution.py:33
  43.1 1.2 %collective-permute-start.1 = (f32[2,16,2]{1,0,2:T(2,128)S(1)}, f32[2,16,2]{1,0,2:T(2,128)S(1)}, u32[]{:S(2)}, u32[]{:S(2)}) collective-permute-start(f32[2,16,2]{1,0,2:T(2,128)S(1)} %pad_maximum_fusion), channel_id=1, source_target_pairs={{0,1},{1,0},{2,3},{3,2},{4,5},{5,4},{6,7},{7,6},{8,9},{9,8},{10,11... | collective-permute-start | bytes 776 | tf_op jit(solution)/shard_map/ppermute | solution.py:56
  45.6 19.4 %all-to-all-start.1 = ((f32[8,2,16,1024]{3,2,1,0:T(8,128)}), f32[8,2,16,1024]{3,2,1,0:T(8,128)}, u32[]{:S(2)}, u32[]{:S(2)}) async-start(f32[8,2,16,1024]{3,2,1,0:T(8,128)} %broadcast_in_dim.14), calls=%async_computation.1 | async-start | bytes 2097152 | tf_op jit(solution)/shard_map/all_to_all | solution.py:69
  66.4 8.5 %copy-start.3 = (f32[8,2,16,1024]{3,2,0,1:T(8,128)}, f32[8,2,16,1024]{3,2,0,1:T(8,128)S(1)}, u32[]{:S(2)}) copy-start(f32[8,2,16,1024]{3,2,0,1:T(8,128)S(1)} %copy.6) | copy-start | bytes 3145732
  74.8 1.7 %copy-start.1 = (f32[256,2992]{0,1:T(8,128)}, f32[256,2992]{0,1:T(8,128)S(1)}, u32[]{:S(2)}) copy-start(f32[256,2992]{0,1:T(8,128)S(1)} %fusion.11) | copy-start | bytes 9191428
  77.7 9.2 %collective-permute-start.3 = (f32[128,2992]{0,1:T(8,128)}, f32[128,2992]{0,1:T(8,128)}, u32[]{:S(2)}, u32[]{:S(2)}) collective-permute-start(f32[128,2992]{0,1:T(8,128)} %constant_dynamic-slice_fusion), channel_id=1, source_target_pairs={{0,1},{1,0},{2,3},{3,2},{4,5},{5,4},{6,7},{7,6},{8,9},{9,8},{10,11... | collective-permute-start | bytes 4595720 | tf_op jit(solution)/shard_map/ppermute | solution.py:78
  77.7 9.2 %copy-start.2 = (f32[256,2992]{0,1:T(8,128)S(1)}, f32[256,2992]{0,1:T(8,128)}, u32[]{:S(2)}) copy-start(f32[256,2992]{0,1:T(8,128)} %copy-done.1) | copy-start | bytes 9191428

commit v2 on v1

v2 whole, which is shorter than its diff:
```python
import functools
import math

import jax
import jax.numpy as jnp
from jax import lax
from jax.experimental import pallas as pl
from jax.experimental.pallas import tpu as pltpu
from jax.sharding import PartitionSpec as P

logit_gain = 4.0
loss_scale = 64.0

F32, BF16 = jnp.float32, jnp.bfloat16
HBM = pl.BlockSpec(memory_space=pltpu.HBM)
VMEM = pl.BlockSpec(memory_space=pltpu.VMEM)
CHUNKS = 2


def split(x):
    hi = x.astype(BF16)
    return hi, (x - hi.astype(F32)).astype(BF16)


def product(a, b, da, db):
    return lax.dot_general(a, b, (((da,), (db,)), ((), ())), preferred_element_type=F32)


def cuts_of(k, most):
    return [(a, min(most, k - a)) for a in range(0, k, most)]


def masks_of(g, odd):
    bits = [1 << b for b in range(g.bit_length() - 1)]
    if odd and len(bits) > 1:
        bits[0], bits[1] = bits[1], bits[0]
    return bits


def blocks(g, m):
    me, core = lax.axis_index("coef"), lax.axis_index("rot")
    odd = lax.rem(core, 2)
    inner = lax.rem(me, g)
    found = []
    for q in range(g):
        far = []
        for order in (0, 1):
            steps = masks_of(g, order)
            far.append(sum(bit for s, bit in enumerate(reversed(steps)) if q >> s & 1))
        flip = jnp.where(odd == 1, far[1], far[0])
        for a in range(m):
            found.append(a * g + jnp.bitwise_xor(inner, flip))
    return found


def scores_kernel(g, m, cuts, first, *refs):
    if first:
        feat, table, out, t_hi, t_lo, f_hi, f_lo, feat_v, table_v, acc, sems = refs
    else:
        table, f_hi, f_lo, out, t_hi, t_lo, table_v, acc, sems = refs
    chunk = 0 if first else 1
    width = t_hi.shape[1]
    columns = pl.ds(chunk * width, width)
    copies = []
    for i, (at, size) in enumerate(cuts):
        s = pl.ds(at, size)
        pair = [pltpu.make_async_copy(table.at[s, columns], table_v.at[s], sems.at[0, i])]
        if first:
            pair.append(pltpu.make_async_copy(feat.at[s], feat_v.at[s], sems.at[1, i]))
        for c in pair:
            c.start()
        copies.append(pair)
    for i, (at, size) in enumerate(cuts):
        for c in copies[i]:
            c.wait()
        s = slice(at, at + size)
        if first:
            a_hi, a_lo = split(feat_v[s])
            f_hi[s], f_lo[s] = a_hi, a_lo
        else:
            a_hi, a_lo = f_hi[s], f_lo[s]
        b_hi, b_lo = split(table_v[s])
        t_hi[s], t_lo[s] = b_hi, b_lo
        left = jnp.concatenate([a_hi, a_hi, a_lo], axis=0)
        right = jnp.concatenate([b_hi, b_lo, b_hi], axis=0)
        got = product(left, right, 0, 0)
        if i == 0:
            acc[...] = got
        else:
            acc[...] += got
    rows = acc.shape[0] // (g * m)
    for p, block in enumerate(blocks(g, m)):
        out[p * rows:(p + 1) * rows] = acc[pl.ds(pl.multiple_of(block * rows, rows), rows)]


def scores_call(g, m, table, feat=None, halves=None, depth=512):
    k, rots = table.shape
    first = halves is None
    imgs = (feat if first else halves[0]).shape[1]
    width = rots // CHUNKS
    cuts = cuts_of(k, depth)
    outs = [jax.ShapeDtypeStruct((imgs, width), F32)] + [jax.ShapeDtypeStruct((k, width), BF16)] * 2
    scratch = [pltpu.VMEM((k, width), F32), pltpu.VMEM((imgs, width), F32), pltpu.SemaphoreType.DMA((2, len(cuts)))]
    if first:
        outs += [jax.ShapeDtypeStruct((k, imgs), BF16)] * 2
        scratch = [pltpu.VMEM((k, imgs), F32)] + scratch
    return pl.pallas_call(
        functools.partial(scores_kernel, g, m, cuts, first),
        out_shape=outs,
        in_specs=[HBM, HBM] if first else [HBM, VMEM, VMEM],
        out_specs=[VMEM] * len(outs),
        scratch_shapes=scratch,
        cost_estimate=pl.CostEstimate(flops=6 * k * imgs * width, bytes_accessed=4 * k * width, transcendentals=0),
        compiler_params=pltpu.CompilerParams(vmem_limit_bytes=32 << 20),
        name="scores",
    )(*([feat, table] if first else [table, *halves]))


def table_kernel(g, m, cuts, chunk, *refs):
    f_hi, f_lo, mine, far = refs[:4]
    out, out_v, rhs, sems = refs[-4:]
    imgs, width = rhs.shape[0] // 3, rhs.shape[1]
    n = g * m
    rows = imgs // n
    for p, block in enumerate(blocks(g, m)):
        src, q = (mine, p) if p < n // 2 else (far, p - n // 2)
        hi, lo = split(src[q * rows:(q + 1) * rows])
        for j, part in enumerate((hi, lo, hi)):
            rhs[pl.ds(pl.multiple_of(block * rows + j * imgs, rows), rows)] = part
    copies = []
    for i, (at, size) in enumerate(cuts):
        s = slice(at, at + size)
        a_hi = f_hi[s]
        out_v[s] = product(jnp.concatenate([a_hi, a_hi, f_lo[s]], axis=1), rhs[...], 1, 0)
        copy = pltpu.make_async_copy(
            out_v.at[pl.ds(at, size)],
            out.at[pl.ds(at, size), pl.ds(chunk * width, width)],
            sems.at[i],
        )
        copy.start()
        copies.append(copy)
    for copy in copies:
        copy.wait()


def table_call(g, m, f_hi, f_lo, piece, chunk, onto=None, depth=752):
    k, imgs = f_hi.shape
    width = piece[0].shape[1]
    cuts = cuts_of(k, depth)
    extra = [] if onto is None else [onto]
    return pl.pallas_call(
        functools.partial(table_kernel, g, m, cuts, chunk),
        out_shape=jax.ShapeDtypeStruct((k, width * CHUNKS), F32),
        in_specs=[VMEM] * 4 + [HBM] * len(extra),
        out_specs=HBM,
        scratch_shapes=[
            pltpu.VMEM((k, width), F32),
            pltpu.VMEM((3 * imgs, width), BF16),
            pltpu.SemaphoreType.DMA((len(cuts),)),
        ],
        input_output_aliases={4: 0} if extra else {},
        cost_estimate=pl.CostEstimate(flops=6 * k * imgs * width, bytes_accessed=4 * k * width, transcendentals=0),
        compiler_params=pltpu.CompilerParams(vmem_limit_bytes=24 << 20),
        name="grad_table",
    )(f_hi, f_lo, *piece, *extra)


def features_kernel(g, m, parts, *refs):
    tables, pieces = refs[:2 * CHUNKS], refs[2 * CHUNKS:4 * CHUNKS]
    outs, (rows_v, rhs) = refs[4 * CHUNKS:-2], refs[-2:]
    n = g * m
    imgs, width = rows_v.shape
    rows = imgs // n
    shift = 0 if parts == 1 else (1 - lax.axis_index("rot")) * (n // 2)
    for c in range(CHUNKS):
        mine, far = pieces[2 * c:2 * c + 2]
        for p, block in enumerate(blocks(g, m)):
            src, q = (mine, p) if p < n // 2 else (far, p - n // 2)
            place = lax.rem(block + shift, n)
            rows_v[pl.ds(pl.multiple_of(place * rows, rows), rows)] = src[q * rows:(q + 1) * rows]
        hi, lo = split(rows_v[...].T)
        for j, part in enumerate((hi, lo, hi)):
            rhs[(3 * c + j) * width:(3 * c + j + 1) * width] = part
    left = []
    for c in range(CHUNKS):
        hi, lo = tables[2 * c][...], tables[2 * c + 1][...]
        left += [hi, hi, lo]
    got = product(jnp.concatenate(left, axis=1), rhs[...], 1, 0)
    share = imgs // parts
    for i, out in enumerate(outs):
        out[...] = got[:, i * share:(i + 1) * share]


def features_call(g, m, tables, pieces, parts):
    k, width = tables[0].shape
    imgs = 2 * pieces[0].shape[0]
    return pl.pallas_call(
        functools.partial(features_kernel, g, m, parts),
        out_shape=[jax.ShapeDtypeStruct((k, imgs // parts), F32)] * parts,
        in_specs=[VMEM] * (len(tables) + len(pieces)),
        out_specs=[VMEM] * parts,
        scratch_shapes=[pltpu.VMEM((imgs, width), F32), pltpu.VMEM((3 * CHUNKS * width, imgs), BF16)],
        cost_estimate=pl.CostEstimate(
            flops=6 * k * imgs * width * CHUNKS, bytes_accessed=4 * k * width * CHUNKS, transcendentals=0
        ),
        compiler_params=pltpu.CompilerParams(vmem_limit_bytes=24 << 20),
        name="grad_features",
    )(*tables, *pieces)


def solution(mesh):
    n = mesh.shape["coef"]
    r = mesh.shape["rot"]
    g = math.gcd(n, 8)
    m = n // g
    outer = [[a * g + b for a in range(m)] for b in range(g)]
    swap = [(i, (i + g) % n) for i in range(n)]
    rot_swap = [(0, 1), (1, 0)]
    steps = g.bit_length() - 1

    def exchange(x, step):
        perm = [(i * r + c, (i ^ masks_of(g, c % 2)[step]) * r + c) for i in range(n) for c in range(r)]
        return lax.ppermute(x, ("coef", "rot"), perm)

    def add_cubes(x):
        if m == 1:
            return x
        if m == 2:
            return x + lax.ppermute(x, "coef", swap)
        return lax.psum(x, "coef", axis_index_groups=outer)

    def join_cubes(x):
        if m == 1:
            return x
        if m == 2:
            other = lax.ppermute(x, "coef", swap)
            first = lax.axis_index("coef") < g
            return jnp.where(first, jnp.concatenate([x, other]), jnp.concatenate([other, x]))
        return lax.all_gather(x, "coef", axis_index_groups=outer, tiled=True)

    def reduce(x):
        for step in range(steps):
            half = x.shape[0] // 2
            x = x[:half] + exchange(x[half:], step)
        return add_cubes(x)

    def gather(x):
        for step in reversed(range(1, steps)):
            x = jnp.concatenate([x, exchange(x, step)])
        return x, exchange(x, 0)

    def on_device(features, table, targets):
        imgs, k = features.shape
        rots = table.shape[0]
        width = rots // CHUNKS
        scale = logit_gain / math.sqrt(k * n)
        features, table = features.T, table.T
        goal = join_cubes(targets)

        first, *rest = scores_call(g, m, table, feat=features)
        tables, halves = rest[:2], rest[2:]
        second, *more = scores_call(g, m, table, halves=halves)
        tables = tables + more
        scores = [scale * reduce(part) for part in (first, second)]

        top = functools.reduce(jnp.maximum, [jnp.max(s, axis=1, keepdims=True) for s in scores])
        expo = [jnp.exp(s - top) for s in scores]
        total = sum(jnp.sum(e, axis=1, keepdims=True) for e in expo)
        if r == 2:
            both = jnp.concatenate([top, total], axis=1)
            far = lax.ppermute(both, "rot", rot_swap)
            far_top, far_total = far[:, :1], far[:, 1:]
            row_max = jnp.maximum(top, far_top)
            ours = jnp.exp(top - row_max)
            row_sum = total * ours + far_total * jnp.exp(far_top - row_max)
        else:
            row_max = lax.pmax(top, "rot")
            ours = jnp.exp(top - row_max)
            row_sum = lax.psum(total * ours, "rot")
        norm = ours / row_sum
        pieces = []
        for c, e in enumerate(expo):
            grad = (scale * loss_scale) * (e * norm - goal[:, c * width:(c + 1) * width])
            pieces.append(gather(grad))

        grad_table = table_call(g, m, *halves, pieces[0], 0)
        flat = [x for piece in pieces for x in piece]
        if r == 2:
            send, keep = features_call(g, m, tables, flat, 2)
            grad_features = keep + lax.ppermute(send, "rot", rot_swap)
        else:
            (whole,) = features_call(g, m, tables, flat, 1)
            grad_features = lax.psum_scatter(whole, "rot", scatter_dimension=1, tiled=True)
        grad_table = table_call(g, m, *halves, pieces[1], 1, grad_table)
        return (grad_features.T, grad_table.T)

    return jax.shard_map(
        on_device,
        mesh=mesh,
        in_specs=(P(None, "coef"), P("rot", "coef"), P("coef", "rot")),
        out_specs=(P("rot", "coef"), P("rot", "coef")),
        check_vma=False,
    )
```

time: 90 us -> 91 us (1.011)
  matrix products: 25.8 us -> 0 us
  Pallas kernels: 0 us -> 22.1 us
  blocking collectives: 21.2 us -> 0 us
  starting transfers between devices: 7.3 us -> 25.1 us
  local copies, waits for them, and re-layouts: 7.26 us -> 19 us
  waiting for transfers between devices: 23 us -> 19.5 us
    dot_general x3 -> x0, matrix products: 25.8 us -> none  [the longest x1 9.21 us: on_device(): lax.dot_general(piece, features, (((0,), (0,)), ((), ())), **high)]
    pallas_call x0 -> x5, Pallas kernels: none -> 22.1 us  [the longest x2 9.27 us: scores_call(): pl.pallas_call(functools.partial(scores_kernel, g, m, cuts, first), out_s...]
    all_to_all x1 -> x0, blocking collectives: 21.2 us -> none  [on_device(): lax.all_to_all(blocks, 'coef', 0, 0, axis_index_groups=inner, tiled=True)]
    ppermute x0 -> x12, waiting for transfers between devices: none -> 15.9 us  [exchange(): return lax.ppermute(x, ('coef', 'rot'), perm)]
    ppermute x0 -> x12, starting transfers between devices: none -> 15.8 us  [exchange(): return lax.ppermute(x, ('coef', 'rot'), perm)]
    all_to_all x1 -> x0, waiting for transfers between devices: 15.2 us -> none  [on_device(): lax.all_to_all(wide, 'coef', 0, 0, axis_index_groups=inner, tiled=True)]
    unnamed x10 -> x26, local copies, waits for them, and re-layouts: 3.52 us -> 17.5 us
    all_to_all x1 -> x0, starting transfers between devices: 4.24 us -> none  [on_device(): lax.all_to_all(wide, 'coef', 0, 0, axis_index_groups=inner, tiled=True)]
  transfers between devices with their start and end apart: 5 -> 17, of which waited for: 3 -> 9; matrix products, arithmetic and copies ran while one was open for 11% -> 4% of each run, Pallas kernels for 0% -> 13%
where the time goes in v2:
time: 91 us; the launch traced here: 90.7 us
  starting transfers between devices  25.1 us (28%)
  Pallas kernels  22.1 us (24%)
  waiting for transfers between devices  19.5 us (21%)
  local copies, waits for them, and re-layouts  19 us (21%)
  other arithmetic  4.23 us (5%)
    unnamed x26, local copies, waits for them, and re-layouts  17.5 us
    ppermute x12, waiting for transfers between devices, exchange(): return lax.ppermute(x, ('coef', 'rot'), perm)  15.9 us
    ppermute x12, starting transfers between devices, exchange(): return lax.ppermute(x, ('coef', 'rot'), perm)  15.8 us
    pallas_call x2, Pallas kernels, scores_call(): pl.pallas_call(functools.partial(scores_kernel, g, m, cuts, first), out_s...  9.27 us
    pallas_call x2, Pallas kernels, table_call(): pl.pallas_call(functools.partial(table_kernel, g, m, cuts, chunk), out_sh...  7.54 us
    ppermute x2, starting transfers between devices, add_cubes(): return x + lax.ppermute(x, 'coef', swap)  6.12 us
    pallas_call x1, Pallas kernels, features_call(): pl.pallas_call(functools.partial(features_kernel, g, m, parts), out_shape...  5.24 us
    ppermute x1, starting transfers between devices, join_cubes(): other = lax.ppermute(x, 'coef', swap)  3.01 us
  transfers between devices with their start and end apart: 17, of which 9 were waited for; matrix products, arithmetic and copies ran while one was open for 4% of the time, Pallas kernels for 13%

profile of v2, /device:TPU:0, one launch (start us, length us, event | category | flops | bytes accessed | tf_op | source)
XLA Modules:
  0.0 90.7 jit_solution(11831261096009830801)
XLA Ops:
  0.6 1.9 %copy-done.1 = f32[256,2992]{0,1:T(8,128)S(1)} copy-done((f32[256,2992]{0,1:T(8,128)S(1)}, f32[256,2992]{0,1:T(8,128)}, u32[]{:S(2)}) %copy-start.1) | copy-done | bytes 3063832
  2.5 4.7 %scores.2 = (f32[256,512]{1,0:T(8,128)S(1)}, bf16[2992,512]{1,0:T(8,128)(2,1)S(1)}, bf16[2992,512]{1,0:T(8,128)(2,1)S(1)}, bf16[2992,256]{1,0:T(8,128)(2,1)S(1)}, bf16[2992,256]{1,0:T(8,128)(2,1)S(1)}) custom-call(f32[2992,256]{1,0:T(8,128)S(1)} %bitcast.13, f32[2992,1024]{1,0:T(8,128)} %bitcast.11), custom_call_target="tpu_custom_call" | custom-call | flops 2353004544 | bytes 6127616 | tf_op jit(solution)/shard_map/scores/pallas_call | solution.py:107
  7.2 1.6 %copy-done.4 = bf16[2992,512]{1,0:T(8,128)(2,1)} copy-done((bf16[2992,512]{1,0:T(8,128)(2,1)}, bf16[2992,512]{1,0:T(8,128)(2,1)S(1)}, u32[]{:S(2)}) %copy-start.4) | copy-done | bytes 3063832
  8.9 1.6 %copy-done.6 = bf16[2992,512]{1,0:T(8,128)(2,1)} copy-done((bf16[2992,512]{1,0:T(8,128)(2,1)}, bf16[2992,512]{1,0:T(8,128)(2,1)S(1)}, u32[]{:S(2)}) %copy-start.6) | copy-done | bytes 3063832
  11.2 3.0 %collective-permute-start = (f32[128,512]{1,0:T(8,128)}, f32[128,512]{1,0:T(8,128)}, u32[]{:S(2)}, u32[]{:S(2)}) collective-permute-start(f32[128,512]{1,0:T(8,128)} %slice.49), channel_id=1, source_target_pairs={{0,2},{1,5},{2,0},{3,7},{4,6},{5,1},{6,4},{7,3},{8,10},{9,13},{10,... | collective-permute-start | bytes 786440 | tf_op jit(solution)/shard_map/ppermute | solution.py:223
  14.2 4.5 %copy-done = f32[1024,2992]{0,1:T(8,128)S(1)} copy-done((f32[1024,2992]{0,1:T(8,128)S(1)}, f32[1024,2992]{0,1:T(8,128)}, u32[]{:S(2)}) %copy-start) | copy-done | bytes 12255256
  18.7 4.6 %scores.3 = (f32[256,512]{1,0:T(8,128)S(1)}, bf16[2992,512]{1,0:T(8,128)(2,1)S(1)}, bf16[2992,512]{1,0:T(8,128)(2,1)S(1)}) custom-call(f32[2992,1024]{1,0:T(8,128)S(1)} %bitcast.12, bf16[2992,256]{1,0:T(8,128)(2,1)S(1)} %get-tuple-element.14.refs_1_.refs_0_, bf16[2992,256]{1,0:T(8,128)(2,1)S(1)} %get-tuple-element.15.refs_2_.refs_1_), custom_call_target="tpu_custom_call" | custom-call | flops 2353004544 | bytes 6127616 | tf_op jit(solution)/shard_map/scores/pallas_call | solution.py:107
  23.3 1.6 %copy-done.8 = bf16[2992,512]{1,0:T(8,128)(2,1)} copy-done((bf16[2992,512]{1,0:T(8,128)(2,1)}, bf16[2992,512]{1,0:T(8,128)(2,1)S(1)}, u32[]{:S(2)}) %copy-start.8) | copy-done | bytes 3063832
  24.9 1.7 %copy-done.10 = bf16[2992,512]{1,0:T(8,128)(2,1)} copy-done((bf16[2992,512]{1,0:T(8,128)(2,1)}, bf16[2992,512]{1,0:T(8,128)(2,1)S(1)}, u32[]{:S(2)}) %copy-start.10) | copy-done | bytes 3063832
  28.2 3.0 %collective-permute-start.9 = (f32[16,1024]{1,0:T(8,128)S(1)}, f32[16,1024]{1,0:T(8,128)S(1)}, u32[]{:S(2)}, u32[]{:S(2)}) collective-permute-start(f32[16,1024]{1,0:T(8,128)S(1)} %copy-done.12), channel_id=1, source_target_pairs={{0,16},{2,18},{4,20},{6,22},{8,24},{10,26},{12,28},{14,30},{16,0},... | collective-permute-start | bytes 196616 | tf_op jit(solution)/shard_map/ppermute | solution.py:236
  31.3 1.2 %slice_add_fusion.1 = f32[128,512]{1,0:T(8,128)S(1)} fusion(f32[128,512]{1,0:T(8,128)} %collective-permute-done, f32[256,512]{1,0:T(8,128)} %copy-done.3), kind=kLoop, calls=%fused_computation.4 | loop fusion | flops 65536 | bytes 786432 | tf_op jit(solution)/shard_map/add | solution.py:244
  32.5 1.6 %collective-permute-start.1 = (f32[64,512]{1,0:T(8,128)S(1)}, f32[64,512]{1,0:T(8,128)S(1)}, u32[]{:S(2)}, u32[]{:S(2)}) collective-permute-start(f32[64,512]{1,0:T(8,128)S(1)} %slice.65), channel_id=1, source_target_pairs={{0,4},{1,3},{2,6},{3,1},{4,0},{5,7},{6,2},{7,5},{8,12},{9,11},{10,... | collective-permute-start | bytes 393224 | tf_op jit(solution)/shard_map/ppermute | solution.py:223
  36.3 1.6 %collective-permute-start.5 = (f32[64,512]{1,0:T(8,128)S(1)}, f32[64,512]{1,0:T(8,128)S(1)}, u32[]{:S(2)}, u32[]{:S(2)}) collective-permute-start(f32[64,512]{1,0:T(8,128)S(1)} %slice.69), channel_id=1, source_target_pairs={{0,4},{1,3},{2,6},{3,1},{4,0},{5,7},{6,2},{7,5},{8,12},{9,11},{10,... | collective-permute-start | bytes 393224 | tf_op jit(solution)/shard_map/ppermute | solution.py:223
  37.9 1.6 %collective-permute-start.2 = (f32[32,512]{1,0:T(8,128)S(1)}, f32[32,512]{1,0:T(8,128)S(1)}, u32[]{:S(2)}, u32[]{:S(2)}) collective-permute-start(f32[32,512]{1,0:T(8,128)S(1)} %slice.67), channel_id=1, source_target_pairs={{0,8},{1,9},{2,10},{3,11},{4,12},{5,13},{6,14},{7,15},{8,0},{9,1},... | collective-permute-start | bytes 196616 | tf_op jit(solution)/shard_map/ppermute | solution.py:223
  39.5 1.8 %collective-permute-done.5 = f32[64,512]{1,0:T(8,128)S(1)} collective-permute-done((f32[64,512]{1,0:T(8,128)S(1)}, f32[64,512]{1,0:T(8,128)S(1)}, u32[]{:S(2)}, u32[]{:S(2)}) %collective-permute-start.5) | collective-permute-done | bytes 131104 | tf_op jit(solution)/shard_map/ppermute | solution.py:223
  41.3 1.6 %collective-permute-start.6 = (f32[32,512]{1,0:T(8,128)S(1)}, f32[32,512]{1,0:T(8,128)S(1)}, u32[]{:S(2)}, u32[]{:S(2)}) collective-permute-start(f32[32,512]{1,0:T(8,128)S(1)} %slice.71), channel_id=1, source_target_pairs={{0,8},{1,9},{2,10},{3,11},{4,12},{5,13},{6,14},{7,15},{8,0},{9,1},... | collective-permute-start | bytes 196616 | tf_op jit(solution)/shard_map/ppermute | solution.py:223
  43.0 3.5 %collective-permute-start.3 = (f32[32,512]{1,0:T(8,128)S(1)}, f32[32,512]{1,0:T(8,128)S(1)}, u32[]{:S(2)}, u32[]{:S(2)}) collective-permute-start(f32[32,512]{1,0:T(8,128)S(1)} %slice_add_fusion.5), channel_id=1, source_target_pairs={{0,16},{2,18},{4,20},{6,22},{8,24},{10,26},{12,28},{14,30},{16,0},... | collective-permute-start | bytes 196616 | tf_op jit(solution)/shard_map/ppermute | solution.py:229
  46.5 2.6 %collective-permute-start.7 = (f32[32,512]{1,0:T(8,128)S(1)}, f32[32,512]{1,0:T(8,128)S(1)}, u32[]{:S(2)}, u32[]{:S(2)}) collective-permute-start(f32[32,512]{1,0:T(8,128)S(1)} %slice_add_fusion.4), channel_id=1, source_target_pairs={{0,16},{2,18},{4,20},{6,22},{8,24},{10,26},{12,28},{14,30},{16,0},... | collective-permute-start | bytes 196616 | tf_op jit(solution)/shard_map/ppermute | solution.py:229
  49.3 2.5 %collective-permute-done.7 = f32[32,512]{1,0:T(8,128)S(1)} collective-permute-done((f32[32,512]{1,0:T(8,128)S(1)}, f32[32,512]{1,0:T(8,128)S(1)}, u32[]{:S(2)}, u32[]{:S(2)}) %collective-permute-start.7) | collective-permute-done | bytes 65568 | tf_op jit(solution)/shard_map/ppermute | solution.py:229
  53.5 1.8 %collective-permute-start.10 = (f32[32,512]{1,0:T(8,128)S(1)}, f32[32,512]{1,0:T(8,128)S(1)}, u32[]{:S(2)}, u32[]{:S(2)}) collective-permute-start(f32[32,512]{1,0:T(8,128)S(1)} %get-tuple-element.25), channel_id=1, source_target_pairs={{0,8},{1,9},{2,10},{3,11},{4,12},{5,13},{6,14},{7,15},{8,0},{9,1},... | collective-permute-start | bytes 196616 | tf_op jit(solution)/shard_map/ppermute | solution.py:223
  55.6 2.2 %collective-permute-done.10 = f32[32,512]{1,0:T(8,128)S(1)} collective-permute-done((f32[32,512]{1,0:T(8,128)S(1)}, f32[32,512]{1,0:T(8,128)S(1)}, u32[]{:S(2)}, u32[]{:S(2)}) %collective-permute-start.10) | collective-permute-done | bytes 65568 | tf_op jit(solution)/shard_map/ppermute | solution.py:223
  57.8 2.0 %collective-permute-start.11 = (f32[64,512]{1,0:T(8,128)S(1)}, f32[64,512]{1,0:T(8,128)S(1)}, u32[]{:S(2)}, u32[]{:S(2)}) collective-permute-start(f32[64,512]{1,0:T(8,128)S(1)} %pad_maximum_fusion.2), channel_id=1, source_target_pairs={{0,4},{1,3},{2,6},{3,1},{4,0},{5,7},{6,2},{7,5},{8,12},{9,11},{10,... | collective-permute-start | bytes 393224 | tf_op jit(solution)/shard_map/ppermute | solution.py:223
  60.8 2.0 %collective-permute-done.11 = f32[64,512]{1,0:T(8,128)S(1)} collective-permute-done((f32[64,512]{1,0:T(8,128)S(1)}, f32[64,512]{1,0:T(8,128)S(1)}, u32[]{:S(2)}, u32[]{:S(2)}) %collective-permute-start.11) | collective-permute-done | bytes 131104 | tf_op jit(solution)/shard_map/ppermute | solution.py:223
  64.0 2.3 %collective-permute-done.14 = f32[64,512]{1,0:T(8,128)S(1)} collective-permute-done((f32[64,512]{1,0:T(8,128)S(1)}, f32[64,512]{1,0:T(8,128)S(1)}, u32[]{:S(2)}, u32[]{:S(2)}) %collective-permute-start.14) | collective-permute-done | bytes 131104 | tf_op jit(solution)/shard_map/ppermute | solution.py:223
  66.4 2.9 %collective-permute-done.12.refs_5_.refs_3_ = f32[128,512]{1,0:T(8,128)S(1)} collective-permute-done((f32[128,512]{1,0:T(8,128)S(1)}, f32[128,512]{1,0:T(8,128)S(1)}, u32[]{:S(2)}, u32[]{:S(2)}) %collective-permute-start.12) | collective-permute-done | bytes 262176 | tf_op jit(solution)/shard_map/ppermute | solution.py:223
  69.3 3.4 %collective-permute-done.15.refs_7_.refs_3_ = f32[128,512]{1,0:T(8,128)S(1)} collective-permute-done((f32[128,512]{1,0:T(8,128)S(1)}, f32[128,512]{1,0:T(8,128)S(1)}, u32[]{:S(2)}, u32[]{:S(2)}) %collective-permute-start.15) | collective-permute-done | bytes 262176 | tf_op jit(solution)/shard_map/ppermute | solution.py:223
  72.7 1.9 %copy-done.9 = bf16[2992,512]{1,0:T(8,128)(2,1)S(1)} copy-done((bf16[2992,512]{1,0:T(8,128)(2,1)S(1)}, bf16[2992,512]{1,0:T(8,128)(2,1)}, u32[]{:S(2)}) %copy-start.9) | copy-done | bytes 3063832
  74.6 1.9 %copy-done.11 = bf16[2992,512]{1,0:T(8,128)(2,1)S(1)} copy-done((bf16[2992,512]{1,0:T(8,128)(2,1)S(1)}, bf16[2992,512]{1,0:T(8,128)(2,1)}, u32[]{:S(2)}) %copy-start.11) | copy-done | bytes 3063832
  76.5 5.2 %grad_features.1 = (f32[2992,128]{1,0:T(8,128)S(1)}, f32[2992,128]{1,0:T(8,128)S(1)}) custom-call(bf16[2992,512]{1,0:T(8,128)(2,1)S(1)} %copy-done.5, bf16[2992,512]{1,0:T(8,128)(2,1)S(1)} %copy-done.7, bf16[2992,512]{1,0:T(8,128)(2,1)S(1)} %copy-done.9, bf16[2992,512]{1,0:T(8,128)(2,1)S(1)} %copy-done.11, f32[128,512]{1,0:T(8,128)S(1)} %pad_maximum_fusion.refs_4_.refs_2_, ...), custom_call_target="tpu_custom_call" | custom-call | flops 4706009088 | bytes 12255232 | tf_op jit(solution)/shard_map/grad_features/pallas_call | solution.py:197
  81.8 3.8 %grad_table.2.refs_4_ = f32[2992,1024]{1,0:T(8,128)} custom-call(bf16[2992,256]{1,0:T(8,128)(2,1)S(1)} %get-tuple-element.14.refs_1_.refs_0_, bf16[2992,256]{1,0:T(8,128)(2,1)S(1)} %get-tuple-element.15.refs_2_.refs_1_, f32[128,512]{1,0:T(8,128)S(1)} %pad_maximum_fusion.refs_4_.refs_2_, f32[128,512]{1,0:T(8,128)S(1)} %collective-permute-done.12.refs_5_.refs_3_), custom_call_target="tpu_custom_call" | custom-call | flops 2353004544 | bytes 6127616 | tf_op jit(solution)/shard_map/grad_table/pallas_call | solution.py:151
  85.6 3.8 %grad_table.3 = f32[2992,1024]{1,0:T(8,128)} custom-call(bf16[2992,256]{1,0:T(8,128)(2,1)S(1)} %get-tuple-element.14.refs_1_.refs_0_, bf16[2992,256]{1,0:T(8,128)(2,1)S(1)} %get-tuple-element.15.refs_2_.refs_1_, f32[128,512]{1,0:T(8,128)S(1)} %pad_maximum_fusion.1.refs_6_.refs_2_, ...), custom_call_target="tpu_custom_call", output_to_operand_aliasing={{}: (4, {})} | custom-call | flops 2353004544 | bytes 6127616 | tf_op jit(solution)/shard_map/grad_table/pallas_call | solution.py:151
  89.4 1.3 %add_bitcast_fusion = f32[128,2992]{0,1:T(8,128)} fusion(f32[2992,128]{1,0:T(8,128)S(1)} %get-tuple-element.20, f32[2992,128]{1,0:T(8,128)S(1)} %collective-permute-done.16), kind=kLoop, calls=%fused_computation | loop fusion | flops 382976 | bytes 4595712 | tf_op jit(solution)/shard_map/transpose | solution.py:295
  (59 shorter events, 9.0 us)
Async XLA Ops:
  0.6 1.9 %copy-start.1 = (f32[256,2992]{0,1:T(8,128)S(1)}, f32[256,2992]{0,1:T(8,128)}, u32[]{:S(2)}) copy-start(f32[256,2992]{0,1:T(8,128)} %param.3) | copy-start | bytes 9191428
  7.2 1.6 %copy-start.4 = (bf16[2992,512]{1,0:T(8,128)(2,1)}, bf16[2992,512]{1,0:T(8,128)(2,1)S(1)}, u32[]{:S(2)}) copy-start(bf16[2992,512]{1,0:T(8,128)(2,1)S(1)} %get-tuple-element.12.refs_0_) | copy-start | bytes 9191428
  8.9 1.6 %copy-start.6 = (bf16[2992,512]{1,0:T(8,128)(2,1)}, bf16[2992,512]{1,0:T(8,128)(2,1)S(1)}, u32[]{:S(2)}) copy-start(bf16[2992,512]{1,0:T(8,128)(2,1)S(1)} %get-tuple-element.13.refs_1_) | copy-start | bytes 9191428
  10.5 3.7 %copy-start.3 = (f32[256,512]{1,0:T(8,128)}, f32[256,512]{1,0:T(8,128)S(1)}, u32[]{:S(2)}) copy-start(f32[256,512]{1,0:T(8,128)S(1)} %get-tuple-element.18) | copy-start | bytes 1572868
  11.2 20.0 %collective-permute-start = (f32[128,512]{1,0:T(8,128)}, f32[128,512]{1,0:T(8,128)}, u32[]{:S(2)}, u32[]{:S(2)}) collective-permute-start(f32[128,512]{1,0:T(8,128)} %slice.49), channel_id=1, source_target_pairs={{0,2},{1,5},{2,0},{3,7},{4,6},{5,1},{6,4},{7,3},{8,10},{9,13},{10,... | collective-permute-start | bytes 786440 | tf_op jit(solution)/shard_map/ppermute | solution.py:223
  14.2 4.5 %copy-start = (f32[1024,2992]{0,1:T(8,128)S(1)}, f32[1024,2992]{0,1:T(8,128)}, u32[]{:S(2)}) copy-start(f32[1024,2992]{0,1:T(8,128)} %param.4) | copy-start | bytes 36765700
  18.7 9.5 %copy-start.12 = (f32[16,1024]{1,0:T(8,128)S(1)}, f32[16,1024]{1,0:T(8,128)}, u32[]{:S(2)}) copy-start(f32[16,1024]{1,0:T(8,128)} %param.5) | copy-start | bytes 196612
  23.3 1.6 %copy-start.8 = (bf16[2992,512]{1,0:T(8,128)(2,1)}, bf16[2992,512]{1,0:T(8,128)(2,1)S(1)}, u32[]{:S(2)}) copy-start(bf16[2992,512]{1,0:T(8,128)(2,1)S(1)} %get-tuple-element.16.refs_2_) | copy-start | bytes 9191428
  24.9 1.7 %copy-start.10 = (bf16[2992,512]{1,0:T(8,128)(2,1)}, bf16[2992,512]{1,0:T(8,128)(2,1)S(1)}, u32[]{:S(2)}) copy-start(bf16[2992,512]{1,0:T(8,128)(2,1)S(1)} %get-tuple-element.17.refs_3_) | copy-start | bytes 9191428
  26.6 0.8 copy-start.2
  28.1 7.1 %collective-permute-start.4 = (f32[128,512]{1,0:T(8,128)}, f32[128,512]{1,0:T(8,128)S(1)}, u32[]{:S(2)}, u32[]{:S(2)}) collective-permute-start(f32[128,512]{1,0:T(8,128)} %slice.55), channel_id=1, source_target_pairs={{0,2},{1,5},{2,0},{3,7},{4,6},{5,1},{6,4},{7,3},{8,10},{9,13},{10,... | collective-permute-start | bytes 786440 | tf_op jit(solution)/shard_map/ppermute | solution.py:223
  28.2 24.0 %collective-permute-start.9 = (f32[16,1024]{1,0:T(8,128)S(1)}, f32[16,1024]{1,0:T(8,128)S(1)}, u32[]{:S(2)}, u32[]{:S(2)}) collective-permute-start(f32[16,1024]{1,0:T(8,128)S(1)} %copy-done.12), channel_id=1, source_target_pairs={{0,16},{2,18},{4,20},{6,22},{8,24},{10,26},{12,28},{14,30},{16,0},... | collective-permute-start | bytes 196616 | tf_op jit(solution)/shard_map/ppermute | solution.py:236
  31.3 41.5 %copy-start.7 = (bf16[2992,512]{1,0:T(8,128)(2,1)S(1)}, bf16[2992,512]{1,0:T(8,128)(2,1)}, u32[]{:S(2)}) copy-start(bf16[2992,512]{1,0:T(8,128)(2,1)} %copy-done.6) | copy-start | bytes 9191428
  32.5 5.4 %collective-permute-start.1 = (f32[64,512]{1,0:T(8,128)S(1)}, f32[64,512]{1,0:T(8,128)S(1)}, u32[]{:S(2)}, u32[]{:S(2)}) collective-permute-start(f32[64,512]{1,0:T(8,128)S(1)} %slice.65), channel_id=1, source_target_pairs={{0,4},{1,3},{2,6},{3,1},{4,0},{5,7},{6,2},{7,5},{8,12},{9,11},{10,... | collective-permute-start | bytes 393224 | tf_op jit(solution)/shard_map/ppermute | solution.py:223
  36.3 5.0 %collective-permute-start.5 = (f32[64,512]{1,0:T(8,128)S(1)}, f32[64,512]{1,0:T(8,128)S(1)}, u32[]{:S(2)}, u32[]{:S(2)}) collective-permute-start(f32[64,512]{1,0:T(8,128)S(1)} %slice.69), channel_id=1, source_target_pairs={{0,4},{1,3},{2,6},{3,1},{4,0},{5,7},{6,2},{7,5},{8,12},{9,11},{10,... | collective-permute-start | bytes 393224 | tf_op jit(solution)/shard_map/ppermute | solution.py:223
  37.9 5.1 %collective-permute-start.2 = (f32[32,512]{1,0:T(8,128)S(1)}, f32[32,512]{1,0:T(8,128)S(1)}, u32[]{:S(2)}, u32[]{:S(2)}) collective-permute-start(f32[32,512]{1,0:T(8,128)S(1)} %slice.67), channel_id=1, source_target_pairs={{0,8},{1,9},{2,10},{3,11},{4,12},{5,13},{6,14},{7,15},{8,0},{9,1},... | collective-permute-start | bytes 196616 | tf_op jit(solution)/shard_map/ppermute | solution.py:223
  41.3 5.2 %collective-permute-start.6 = (f32[32,512]{1,0:T(8,128)S(1)}, f32[32,512]{1,0:T(8,128)S(1)}, u32[]{:S(2)}, u32[]{:S(2)}) collective-permute-start(f32[32,512]{1,0:T(8,128)S(1)} %slice.71), channel_id=1, source_target_pairs={{0,8},{1,9},{2,10},{3,11},{4,12},{5,13},{6,14},{7,15},{8,0},{9,1},... | collective-permute-start | bytes 196616 | tf_op jit(solution)/shard_map/ppermute | solution.py:223
  43.0 29.7 %copy-start.5 = (bf16[2992,512]{1,0:T(8,128)(2,1)S(1)}, bf16[2992,512]{1,0:T(8,128)(2,1)}, u32[]{:S(2)}) copy-start(bf16[2992,512]{1,0:T(8,128)(2,1)} %copy-done.4) | copy-start | bytes 9191428
  43.0 6.1 %collective-permute-start.3 = (f32[32,512]{1,0:T(8,128)S(1)}, f32[32,512]{1,0:T(8,128)S(1)}, u32[]{:S(2)}, u32[]{:S(2)}) collective-permute-start(f32[32,512]{1,0:T(8,128)S(1)} %slice_add_fusion.5), channel_id=1, source_target_pairs={{0,16},{2,18},{4,20},{6,22},{8,24},{10,26},{12,28},{14,30},{16,0},... | collective-permute-start | bytes 196616 | tf_op jit(solution)/shard_map/ppermute | solution.py:229
  46.5 5.2 %collective-permute-start.7 = (f32[32,512]{1,0:T(8,128)S(1)}, f32[32,512]{1,0:T(8,128)S(1)}, u32[]{:S(2)}, u32[]{:S(2)}) collective-permute-start(f32[32,512]{1,0:T(8,128)S(1)} %slice_add_fusion.4), channel_id=1, source_target_pairs={{0,16},{2,18},{4,20},{6,22},{8,24},{10,26},{12,28},{14,30},{16,0},... | collective-permute-start | bytes 196616 | tf_op jit(solution)/shard_map/ppermute | solution.py:229
  52.1 1.2 %collective-permute-start.8 = (f32[32,2]{0,1:T(2,128)S(1)}, f32[32,2]{0,1:T(2,128)S(1)}, u32[]{:S(2)}, u32[]{:S(2)}) collective-permute-start(f32[32,2]{0,1:T(2,128)S(1)} %pad_maximum_fusion.4), channel_id=1, source_target_pairs={{0,1},{1,0},{2,3},{3,2},{4,5},{5,4},{6,7},{7,6},{8,9},{9,8},{10,11... | collective-permute-start | bytes 776 | tf_op jit(solution)/shard_map/ppermute | solution.py:271
  53.5 4.3 %collective-permute-start.10 = (f32[32,512]{1,0:T(8,128)S(1)}, f32[32,512]{1,0:T(8,128)S(1)}, u32[]{:S(2)}, u32[]{:S(2)}) collective-permute-start(f32[32,512]{1,0:T(8,128)S(1)} %get-tuple-element.25), channel_id=1, source_target_pairs={{0,8},{1,9},{2,10},{3,11},{4,12},{5,13},{6,14},{7,15},{8,0},{9,1},... | collective-permute-start | bytes 196616 | tf_op jit(solution)/shard_map/ppermute | solution.py:223
  55.3 4.5 %collective-permute-start.13 = (f32[32,512]{1,0:T(8,128)S(1)}, f32[32,512]{1,0:T(8,128)S(1)}, u32[]{:S(2)}, u32[]{:S(2)}) collective-permute-start(f32[32,512]{1,0:T(8,128)S(1)} %get-tuple-element.24), channel_id=1, source_target_pairs={{0,8},{1,9},{2,10},{3,11},{4,12},{5,13},{6,14},{7,15},{8,0},{9,1},... | collective-permute-start | bytes 196616 | tf_op jit(solution)/shard_map/ppermute | solution.py:223
  57.8 5.0 %collective-permute-start.11 = (f32[64,512]{1,0:T(8,128)S(1)}, f32[64,512]{1,0:T(8,128)S(1)}, u32[]{:S(2)}, u32[]{:S(2)}) collective-permute-start(f32[64,512]{1,0:T(8,128)S(1)} %pad_maximum_fusion.2), channel_id=1, source_target_pairs={{0,4},{1,3},{2,6},{3,1},{4,0},{5,7},{6,2},{7,5},{8,12},{9,11},{10,... | collective-permute-start | bytes 393224 | tf_op jit(solution)/shard_map/ppermute | solution.py:223
  59.8 6.4 %collective-permute-start.14 = (f32[64,512]{1,0:T(8,128)S(1)}, f32[64,512]{1,0:T(8,128)S(1)}, u32[]{:S(2)}, u32[]{:S(2)}) collective-permute-start(f32[64,512]{1,0:T(8,128)S(1)} %pad_maximum_fusion.3), channel_id=1, source_target_pairs={{0,4},{1,3},{2,6},{3,1},{4,0},{5,7},{6,2},{7,5},{8,12},{9,11},{10,... | collective-permute-start | bytes 393224 | tf_op jit(solution)/shard_map/ppermute | solution.py:223
  62.9 6.4 %collective-permute-start.12 = (f32[128,512]{1,0:T(8,128)S(1)}, f32[128,512]{1,0:T(8,128)S(1)}, u32[]{:S(2)}, u32[]{:S(2)}) collective-permute-start(f32[128,512]{1,0:T(8,128)S(1)} %pad_maximum_fusion.refs_4_.refs_2_), channel_id=1, source_target_pairs={{0,2},{1,5},{2,0},{3,7},{4,6},{5,1},{6,4},{7,3},{8,10},{9,13},{10,... | collective-permute-start | bytes 786440 | tf_op jit(solution)/shard_map/ppermute | solution.py:223
  66.3 6.4 %collective-permute-start.15 = (f32[128,512]{1,0:T(8,128)S(1)}, f32[128,512]{1,0:T(8,128)S(1)}, u32[]{:S(2)}, u32[]{:S(2)}) collective-permute-start(f32[128,512]{1,0:T(8,128)S(1)} %pad_maximum_fusion.1.refs_6_.refs_2_), channel_id=1, source_target_pairs={{0,2},{1,5},{2,0},{3,7},{4,6},{5,1},{6,4},{7,3},{8,10},{9,13},{10,... | collective-permute-start | bytes 786440 | tf_op jit(solution)/shard_map/ppermute | solution.py:223
  72.7 1.9 %copy-start.9 = (bf16[2992,512]{1,0:T(8,128)(2,1)S(1)}, bf16[2992,512]{1,0:T(8,128)(2,1)}, u32[]{:S(2)}) copy-start(bf16[2992,512]{1,0:T(8,128)(2,1)} %copy-done.8) | copy-start | bytes 9191428
  74.6 1.9 %copy-start.11 = (bf16[2992,512]{1,0:T(8,128)(2,1)S(1)}, bf16[2992,512]{1,0:T(8,128)(2,1)}, u32[]{:S(2)}) copy-start(bf16[2992,512]{1,0:T(8,128)(2,1)} %copy-done.10) | copy-start | bytes 9191428
  81.7 7.6 %collective-permute-start.16 = (f32[2992,128]{1,0:T(8,128)S(1)}, f32[2992,128]{1,0:T(8,128)S(1)}, u32[]{:S(2)}, u32[]{:S(2)}) collective-permute-start(f32[2992,128]{1,0:T(8,128)S(1)} %get-tuple-element.21), channel_id=1, source_target_pairs={{0,1},{1,0},{2,3},{3,2},{4,5},{5,4},{6,7},{7,6},{8,9},{9,8},{10,11... | collective-permute-start | bytes 4595720 | tf_op jit(solution)/shard_map/ppermute | solution.py:290

commit v3 on v2

--- a/solution.py
+++ b/solution.py
@@ -55,11 +55,11 @@
 
 def scores_kernel(g, m, cuts, first, *refs):
     if first:
-        feat, table, out, t_hi, t_lo, f_hi, f_lo, feat_v, table_v, acc, sems = refs
+        feat, table, keep, send, f_hi, f_lo, feat_v, table_v, acc, sems = refs
     else:
-        table, f_hi, f_lo, out, t_hi, t_lo, table_v, acc, sems = refs
+        table, f_hi, f_lo, keep, send, table_v, acc, sems = refs
     chunk = 0 if first else 1
-    width = t_hi.shape[1]
+    width = keep.shape[1]
     columns = pl.ds(chunk * width, width)
     copies = []
     for i, (at, size) in enumerate(cuts):
@@ -80,7 +80,6 @@
         else:
             a_hi, a_lo = f_hi[s], f_lo[s]
         b_hi, b_lo = split(table_v[s])
-        t_hi[s], t_lo[s] = b_hi, b_lo
         left = jnp.concatenate([a_hi, a_hi, a_lo], axis=0)
         right = jnp.concatenate([b_hi, b_lo, b_hi], axis=0)
         got = product(left, right, 0, 0)
@@ -89,8 +88,10 @@
         else:
             acc[...] += got
     rows = acc.shape[0] // (g * m)
+    half = g * m // 2
     for p, block in enumerate(blocks(g, m)):
-        out[p * rows:(p + 1) * rows] = acc[pl.ds(pl.multiple_of(block * rows, rows), rows)]
+        out, q = (keep, p) if p < half else (send, p - half)
+        out[q * rows:(q + 1) * rows] = acc[pl.ds(pl.multiple_of(block * rows, rows), rows)]
 
 
 def scores_call(g, m, table, feat=None, halves=None, depth=512):
@@ -99,7 +100,7 @@
     imgs = (feat if first else halves[0]).shape[1]
     width = rots // CHUNKS
     cuts = cuts_of(k, depth)
-    outs = [jax.ShapeDtypeStruct((imgs, width), F32)] + [jax.ShapeDtypeStruct((k, width), BF16)] * 2
+    outs = [jax.ShapeDtypeStruct((imgs // 2, width), F32)] * 2
     scratch = [pltpu.VMEM((k, width), F32), pltpu.VMEM((imgs, width), F32), pltpu.SemaphoreType.DMA((2, len(cuts)))]
     if first:
         outs += [jax.ShapeDtypeStruct((k, imgs), BF16)] * 2
@@ -116,9 +117,17 @@
     )(*([feat, table] if first else [table, *halves]))
 
 
+def load_all(src, dst, cuts, sems):
+    copies = [pltpu.make_async_copy(src.at[pl.ds(*cut)], dst.at[pl.ds(*cut)], sems.at[i]) for i, cut in enumerate(cuts)]
+    for copy in copies:
+        copy.start()
+    return copies
+
+
 def table_kernel(g, m, cuts, chunk, *refs):
-    f_hi, f_lo, mine, far = refs[:4]
-    out, out_v, rhs, sems = refs[-4:]
+    feat, mine, far = refs[:3]
+    out, feat_v, out_v, rhs, in_sems, out_sems = refs[-6:]
+    loads = load_all(feat, feat_v, cuts, in_sems)
     imgs, width = rhs.shape[0] // 3, rhs.shape[1]
     n = g * m
     rows = imgs // n
@@ -129,13 +138,14 @@
             rhs[pl.ds(pl.multiple_of(block * rows + j * imgs, rows), rows)] = part
     copies = []
     for i, (at, size) in enumerate(cuts):
+        loads[i].wait()
         s = slice(at, at + size)
-        a_hi = f_hi[s]
-        out_v[s] = product(jnp.concatenate([a_hi, a_hi, f_lo[s]], axis=1), rhs[...], 1, 0)
+        hi, lo = split(feat_v[s])
+        out_v[s] = product(jnp.concatenate([hi, hi, lo], axis=1), rhs[...], 1, 0)
         copy = pltpu.make_async_copy(
             out_v.at[pl.ds(at, size)],
             out.at[pl.ds(at, size), pl.ds(chunk * width, width)],
-            sems.at[i],
+            out_sems.at[i],
         )
         copy.start()
         copies.append(copy)
@@ -143,34 +153,38 @@
         copy.wait()
 
 
-def table_call(g, m, f_hi, f_lo, piece, chunk, onto=None, depth=752):
-    k, imgs = f_hi.shape
+def table_call(g, m, feat, piece, chunk, onto=None, depth=752):
+    k, imgs = feat.shape
     width = piece[0].shape[1]
     cuts = cuts_of(k, depth)
     extra = [] if onto is None else [onto]
     return pl.pallas_call(
         functools.partial(table_kernel, g, m, cuts, chunk),
         out_shape=jax.ShapeDtypeStruct((k, width * CHUNKS), F32),
-        in_specs=[VMEM] * 4 + [HBM] * len(extra),
+        in_specs=[HBM, VMEM, VMEM] + [HBM] * len(extra),
         out_specs=HBM,
         scratch_shapes=[
+            pltpu.VMEM((k, imgs), F32),
             pltpu.VMEM((k, width), F32),
             pltpu.VMEM((3 * imgs, width), BF16),
             pltpu.SemaphoreType.DMA((len(cuts),)),
+            pltpu.SemaphoreType.DMA((len(cuts),)),
         ],
-        input_output_aliases={4: 0} if extra else {},
+        input_output_aliases={3: 0} if extra else {},
         cost_estimate=pl.CostEstimate(flops=6 * k * imgs * width, bytes_accessed=4 * k * width, transcendentals=0),
         compiler_params=pltpu.CompilerParams(vmem_limit_bytes=24 << 20),
         name="grad_table",
-    )(f_hi, f_lo, *piece, *extra)
-
-
-def features_kernel(g, m, parts, *refs):
-    tables, pieces = refs[:2 * CHUNKS], refs[2 * CHUNKS:4 * CHUNKS]
-    outs, (rows_v, rhs) = refs[4 * CHUNKS:-2], refs[-2:]
+    )(feat, *piece, *extra)
+
+
+def features_kernel(g, m, cuts, parts, *refs):
+    table, pieces = refs[0], refs[1:1 + 2 * CHUNKS]
+    outs, (table_v, rows_v, rhs, sems) = refs[2 + 2 * CHUNKS:-4], refs[-4:]
+    loads = load_all(table, table_v, cuts, sems)
     n = g * m
     imgs, width = rows_v.shape
     rows = imgs // n
+    rots = width * CHUNKS
     shift = 0 if parts == 1 else (1 - lax.axis_index("rot")) * (n // 2)
     for c in range(CHUNKS):
         mine, far = pieces[2 * c:2 * c + 2]
@@ -180,32 +194,37 @@
             rows_v[pl.ds(pl.multiple_of(place * rows, rows), rows)] = src[q * rows:(q + 1) * rows]
         hi, lo = split(rows_v[...].T)
         for j, part in enumerate((hi, lo, hi)):
-            rhs[(3 * c + j) * width:(3 * c + j + 1) * width] = part
-    left = []
-    for c in range(CHUNKS):
-        hi, lo = tables[2 * c][...], tables[2 * c + 1][...]
-        left += [hi, hi, lo]
-    got = product(jnp.concatenate(left, axis=1), rhs[...], 1, 0)
+            rhs[j * rots + c * width:j * rots + (c + 1) * width] = part
     share = imgs // parts
-    for i, out in enumerate(outs):
-        out[...] = got[:, i * share:(i + 1) * share]
-
-
-def features_call(g, m, tables, pieces, parts):
-    k, width = tables[0].shape
+    for i, (at, size) in enumerate(cuts):
+        loads[i].wait()
+        s = slice(at, at + size)
+        hi, lo = split(table_v[s])
+        got = product(jnp.concatenate([hi, hi, lo], axis=1), rhs[...], 1, 0)
+        for j, out in enumerate(outs):
+            out[s] = got[:, j * share:(j + 1) * share]
+
+
+def features_call(g, m, table, pieces, parts, after, head=256, depth=912):
+    k, rots = table.shape
     imgs = 2 * pieces[0].shape[0]
+    head = min(head, k)
+    cuts = [(0, head)] + [(head + at, size) for at, size in cuts_of(k - head, depth)]
     return pl.pallas_call(
-        functools.partial(features_kernel, g, m, parts),
+        functools.partial(features_kernel, g, m, cuts, parts),
         out_shape=[jax.ShapeDtypeStruct((k, imgs // parts), F32)] * parts,
-        in_specs=[VMEM] * (len(tables) + len(pieces)),
+        in_specs=[HBM] + [VMEM] * len(pieces) + [HBM],
         out_specs=[VMEM] * parts,
-        scratch_shapes=[pltpu.VMEM((imgs, width), F32), pltpu.VMEM((3 * CHUNKS * width, imgs), BF16)],
-        cost_estimate=pl.CostEstimate(
-            flops=6 * k * imgs * width * CHUNKS, bytes_accessed=4 * k * width * CHUNKS, transcendentals=0
-        ),
-        compiler_params=pltpu.CompilerParams(vmem_limit_bytes=24 << 20),
+        scratch_shapes=[
+            pltpu.VMEM((k, rots), F32),
+            pltpu.VMEM((imgs, rots // CHUNKS), F32),
+            pltpu.VMEM((3 * rots, imgs), BF16),
+            pltpu.SemaphoreType.DMA((len(cuts),)),
+        ],
+        cost_estimate=pl.CostEstimate(flops=6 * k * imgs * rots, bytes_accessed=4 * k * rots, transcendentals=0),
+        compiler_params=pltpu.CompilerParams(vmem_limit_bytes=40 << 20),
         name="grad_features",
-    )(*tables, *pieces)
+    )(table, *pieces, after)
 
 
 def solution(mesh):
@@ -238,8 +257,9 @@
             return jnp.where(first, jnp.concatenate([x, other]), jnp.concatenate([other, x]))
         return lax.all_gather(x, "coef", axis_index_groups=outer, tiled=True)
 
-    def reduce(x):
-        for step in range(steps):
+    def reduce(keep, send):
+        x = keep + exchange(send, 0)
+        for step in range(1, steps):
             half = x.shape[0] // 2
             x = x[:half] + exchange(x[half:], step)
         return add_cubes(x)
@@ -254,14 +274,12 @@
         rots = table.shape[0]
         width = rots // CHUNKS
         scale = logit_gain / math.sqrt(k * n)
-        features, table = features.T, table.T
+        features = pltpu.with_memory_space_constraint(features.T, pltpu.HBM)
+        table = pltpu.with_memory_space_constraint(table.T, pltpu.HBM)
         goal = join_cubes(targets)
 
-        first, *rest = scores_call(g, m, table, feat=features)
-        tables, halves = rest[:2], rest[2:]
-        second, *more = scores_call(g, m, table, halves=halves)
-        tables = tables + more
-        scores = [scale * reduce(part) for part in (first, second)]
+        keep, send, *halves = scores_call(g, m, table, feat=features)
+        scores = [scale * reduce(keep, send), scale * reduce(*scores_call(g, m, table, halves=halves))]
 
         top = functools.reduce(jnp.maximum, [jnp.max(s, axis=1, keepdims=True) for s in scores])
         expo = [jnp.exp(s - top) for s in scores]
@@ -283,15 +301,15 @@
             grad = (scale * loss_scale) * (e * norm - goal[:, c * width:(c + 1) * width])
             pieces.append(gather(grad))
 
-        grad_table = table_call(g, m, *halves, pieces[0], 0)
+        grad_table = table_call(g, m, features, pieces[0], 0)
         flat = [x for piece in pieces for x in piece]
         if r == 2:
-            send, keep = features_call(g, m, tables, flat, 2)
+            send, keep = features_call(g, m, table, flat, 2, grad_table)
             grad_features = keep + lax.ppermute(send, "rot", rot_swap)
         else:
-            (whole,) = features_call(g, m, tables, flat, 1)
+            (whole,) = features_call(g, m, table, flat, 1, grad_table)
             grad_features = lax.psum_scatter(whole, "rot", scatter_dimension=1, tiled=True)
-        grad_table = table_call(g, m, *halves, pieces[1], 1, grad_table)
+        grad_table = table_call(g, m, features, pieces[1], 1, grad_table)
         return (grad_features.T, grad_table.T)
 
     return jax.shard_map(

time: 91 us -> 75.7 us (0.83)
  local copies, waits for them, and re-layouts: 19 us -> 0.04 us
  Pallas kernels: 22.1 us -> 30.6 us
  waiting for transfers between devices: 19.5 us -> 14.2 us
  starting transfers between devices: 25.1 us -> 27.5 us
  other arithmetic: 4.23 us -> 2.11 us
    unnamed x26 -> x2, local copies, waits for them, and re-layouts: 17.5 us -> 0.01 us
    pallas_call x1, Pallas kernels: 5.24 us -> 10.8 us  [features_call(): pl.pallas_call(functools.partial(features_kernel, g, m, cuts, parts), out...]
    ppermute x12, waiting for transfers between devices: 15.9 us -> 11 us  [exchange(): return lax.ppermute(x, ('coef', 'rot'), perm)]
    ppermute x12, starting transfers between devices: 15.8 us -> 19.1 us  [exchange(): return lax.ppermute(x, ('coef', 'rot'), perm)]
    pallas_call x2, Pallas kernels: 7.54 us -> 10.8 us  [table_call(): pl.pallas_call(functools.partial(table_kernel, g, m, cuts, chunk), out_sh...]
    add x6 -> x4, other arithmetic: 2.26 us -> 0.06 us  [reduce(): x = x[:half] + exchange(x[half:], step)]
    slice x6 -> x4, local copies, waits for them, and re-layouts: 1.52 us -> 0.03 us  [reduce(): x = x[:half] + exchange(x[half:], step)]
  transfers between devices with their start and end apart: 17 -> 17, of which waited for: 9 -> 9; matrix products, arithmetic and copies ran while one was open for 4% -> 1% of each run, Pallas kernels for 13% -> 20%
where the time goes in v3:
time: 75.7 us; the launch traced here: 75.3 us
  Pallas kernels  30.6 us (40%)
  starting transfers between devices  27.5 us (36%)
  waiting for transfers between devices  14.2 us (19%)
  other arithmetic  2.11 us (3%)
  between operations  0.82 us (1%)
    ppermute x12, starting transfers between devices, exchange(): return lax.ppermute(x, ('coef', 'rot'), perm)  19.1 us
    ppermute x12, waiting for transfers between devices, exchange(): return lax.ppermute(x, ('coef', 'rot'), perm)  11 us
    pallas_call x1, Pallas kernels, features_call(): pl.pallas_call(functools.partial(features_kernel, g, m, cuts, parts), out...  10.8 us
    pallas_call x2, Pallas kernels, table_call(): pl.pallas_call(functools.partial(table_kernel, g, m, cuts, chunk), out_sh...  10.8 us
    pallas_call x2, Pallas kernels, scores_call(): pl.pallas_call(functools.partial(scores_kernel, g, m, cuts, first), out_s...  9.03 us
    ppermute x2, starting transfers between devices, add_cubes(): return x + lax.ppermute(x, 'coef', swap)  5.69 us
    ppermute x1, starting transfers between devices, join_cubes(): other = lax.ppermute(x, 'coef', swap)  2.62 us
    ppermute x2, waiting for transfers between devices, add_cubes(): return x + lax.ppermute(x, 'coef', swap)  2.13 us
  transfers between devices with their start and end apart: 17, of which 9 were waited for; matrix products, arithmetic and copies ran while one was open for 1% of the time, Pallas kernels for 20%

profile of v3, /device:TPU:0, one launch (start us, length us, event | category | flops | bytes accessed | tf_op | source)
XLA Modules:
  0.0 75.3 jit_solution(11511654861183393932)
XLA Ops:
  0.6 4.6 %scores.2 = (f32[128,512]{1,0:T(8,128)S(1)}, f32[128,512]{1,0:T(8,128)S(1)}, bf16[2992,256]{1,0:T(8,128)(2,1)S(1)}, bf16[2992,256]{1,0:T(8,128)(2,1)S(1)}) custom-call(f32[2992,256]{1,0:T(8,128)} %bitcast.15, f32[2992,1024]{1,0:T(8,128)} %bitcast.11), custom_call_target="tpu_custom_call" | custom-call | flops 2353004544 | bytes 6127616 | tf_op jit(solution)/shard_map/scores/pallas_call | solution.py:108
  5.2 3.0 %collective-permute-start = (f32[128,512]{1,0:T(8,128)S(1)}, f32[128,512]{1,0:T(8,128)S(1)}, u32[]{:S(2)}, u32[]{:S(2)}) collective-permute-start(f32[128,512]{1,0:T(8,128)S(1)} %get-tuple-element.11), channel_id=1, source_target_pairs={{0,2},{1,5},{2,0},{3,7},{4,6},{5,1},{6,4},{7,3},{8,10},{9,13},{10,... | collective-permute-start | bytes 786440 | tf_op jit(solution)/shard_map/ppermute | solution.py:242
  8.2 4.5 %scores.3 = (f32[128,512]{1,0:T(8,128)S(1)}, f32[128,512]{1,0:T(8,128)S(1)}) custom-call(f32[2992,1024]{1,0:T(8,128)} %bitcast.12, bf16[2992,256]{1,0:T(8,128)(2,1)S(1)} %get-tuple-element.12.refs_1_, bf16[2992,256]{1,0:T(8,128)(2,1)S(1)} %get-tuple-element.13.refs_2_), custom_call_target="tpu_custom_call" | custom-call | flops 2353004544 | bytes 6127616 | tf_op jit(solution)/shard_map/scores/pallas_call | solution.py:108
  12.9 2.1 %collective-permute-start.1 = (f32[64,512]{1,0:T(8,128)S(1)}, f32[64,512]{1,0:T(8,128)S(1)}, u32[]{:S(2)}, u32[]{:S(2)}) collective-permute-start(f32[64,512]{1,0:T(8,128)S(1)} %slice.49), channel_id=1, source_target_pairs={{0,4},{1,3},{2,6},{3,1},{4,0},{5,7},{6,2},{7,5},{8,12},{9,11},{10,... | collective-permute-start | bytes 393224 | tf_op jit(solution)/shard_map/ppermute | solution.py:242
  14.9 2.6 %collective-permute-start.9 = (f32[16,1024]{1,0:T(8,128)S(1)}, f32[16,1024]{1,0:T(8,128)S(1)}, u32[]{:S(2)}, u32[]{:S(2)}) collective-permute-start(f32[16,1024]{1,0:T(8,128)S(1)} %copy-done), channel_id=1, source_target_pairs={{0,16},{2,18},{4,20},{6,22},{8,24},{10,26},{12,28},{14,30},{16,0},... | collective-permute-start | bytes 196616 | tf_op jit(solution)/shard_map/ppermute | solution.py:255
  17.6 1.8 %collective-permute-done.4 = f32[128,512]{1,0:T(8,128)S(1)} collective-permute-done((f32[128,512]{1,0:T(8,128)S(1)}, f32[128,512]{1,0:T(8,128)S(1)}, u32[]{:S(2)}, u32[]{:S(2)}) %collective-permute-start.4) | collective-permute-done | bytes 262176 | tf_op jit(solution)/shard_map/ppermute | solution.py:242
  19.4 1.8 %collective-permute-start.5 = (f32[64,512]{1,0:T(8,128)S(1)}, f32[64,512]{1,0:T(8,128)S(1)}, u32[]{:S(2)}, u32[]{:S(2)}) collective-permute-start(f32[64,512]{1,0:T(8,128)S(1)} %slice.53), channel_id=1, source_target_pairs={{0,4},{1,3},{2,6},{3,1},{4,0},{5,7},{6,2},{7,5},{8,12},{9,11},{10,... | collective-permute-start | bytes 393224 | tf_op jit(solution)/shard_map/ppermute | solution.py:242
  21.2 1.6 %collective-permute-start.2 = (f32[32,512]{1,0:T(8,128)S(1)}, f32[32,512]{1,0:T(8,128)S(1)}, u32[]{:S(2)}, u32[]{:S(2)}) collective-permute-start(f32[32,512]{1,0:T(8,128)S(1)} %slice.51), channel_id=1, source_target_pairs={{0,8},{1,9},{2,10},{3,11},{4,12},{5,13},{6,14},{7,15},{8,0},{9,1},... | collective-permute-start | bytes 196616 | tf_op jit(solution)/shard_map/ppermute | solution.py:242
  22.9 1.6 %collective-permute-done.5 = f32[64,512]{1,0:T(8,128)S(1)} collective-permute-done((f32[64,512]{1,0:T(8,128)S(1)}, f32[64,512]{1,0:T(8,128)S(1)}, u32[]{:S(2)}, u32[]{:S(2)}) %collective-permute-start.5) | collective-permute-done | bytes 131104 | tf_op jit(solution)/shard_map/ppermute | solution.py:242
  24.5 1.8 %collective-permute-start.6 = (f32[32,512]{1,0:T(8,128)S(1)}, f32[32,512]{1,0:T(8,128)S(1)}, u32[]{:S(2)}, u32[]{:S(2)}) collective-permute-start(f32[32,512]{1,0:T(8,128)S(1)} %slice.55), channel_id=1, source_target_pairs={{0,8},{1,9},{2,10},{3,11},{4,12},{5,13},{6,14},{7,15},{8,0},{9,1},... | collective-permute-start | bytes 196616 | tf_op jit(solution)/shard_map/ppermute | solution.py:242
  26.3 2.7 %collective-permute-start.3 = (f32[32,512]{1,0:T(8,128)S(1)}, f32[32,512]{1,0:T(8,128)S(1)}, u32[]{:S(2)}, u32[]{:S(2)}) collective-permute-start(f32[32,512]{1,0:T(8,128)S(1)} %slice_add_fusion.3), channel_id=1, source_target_pairs={{0,16},{2,18},{4,20},{6,22},{8,24},{10,26},{12,28},{14,30},{16,0},... | collective-permute-start | bytes 196616 | tf_op jit(solution)/shard_map/ppermute | solution.py:248
  29.0 3.0 %collective-permute-start.7 = (f32[32,512]{1,0:T(8,128)S(1)}, f32[32,512]{1,0:T(8,128)S(1)}, u32[]{:S(2)}, u32[]{:S(2)}) collective-permute-start(f32[32,512]{1,0:T(8,128)S(1)} %slice_add_fusion.2), channel_id=1, source_target_pairs={{0,16},{2,18},{4,20},{6,22},{8,24},{10,26},{12,28},{14,30},{16,0},... | collective-permute-start | bytes 196616 | tf_op jit(solution)/shard_map/ppermute | solution.py:248
  32.0 1.0 %collective-permute-done.3 = f32[32,512]{1,0:T(8,128)S(1)} collective-permute-done((f32[32,512]{1,0:T(8,128)S(1)}, f32[32,512]{1,0:T(8,128)S(1)}, u32[]{:S(2)}, u32[]{:S(2)}) %collective-permute-start.3) | collective-permute-done | bytes 65568 | tf_op jit(solution)/shard_map/ppermute | solution.py:248
  33.0 0.1 fusion.8
  33.1 1.2 %collective-permute-done.7 = f32[32,512]{1,0:T(8,128)S(1)} collective-permute-done((f32[32,512]{1,0:T(8,128)S(1)}, f32[32,512]{1,0:T(8,128)S(1)}, u32[]{:S(2)}, u32[]{:S(2)}) %collective-permute-start.7) | collective-permute-done | bytes 65568 | tf_op jit(solution)/shard_map/ppermute | solution.py:248
  34.3 0.1 fusion.9
  34.4 0.2 fusion.3
  34.7 1.1 %collective-permute-done.8 = f32[32,2]{0,1:T(2,128)S(1)} collective-permute-done((f32[32,2]{0,1:T(2,128)S(1)}, f32[32,2]{0,1:T(2,128)S(1)}, u32[]{:S(2)}, u32[]{:S(2)}) %collective-permute-start.8) | collective-permute-done | bytes 288 | tf_op jit(solution)/shard_map/ppermute | solution.py:289
  36.0 1.7 %collective-permute-start.10 = (f32[32,512]{1,0:T(8,128)S(1)}, f32[32,512]{1,0:T(8,128)S(1)}, u32[]{:S(2)}, u32[]{:S(2)}) collective-permute-start(f32[32,512]{1,0:T(8,128)S(1)} %get-tuple-element.21), channel_id=1, source_target_pairs={{0,8},{1,9},{2,10},{3,11},{4,12},{5,13},{6,14},{7,15},{8,0},{9,1},... | collective-permute-start | bytes 196616 | tf_op jit(solution)/shard_map/ppermute | solution.py:242
  37.7 0.4 collective-permute-start.13
  38.1 2.4 %collective-permute-done.10 = f32[32,512]{1,0:T(8,128)S(1)} collective-permute-done((f32[32,512]{1,0:T(8,128)S(1)}, f32[32,512]{1,0:T(8,128)S(1)}, u32[]{:S(2)}, u32[]{:S(2)}) %collective-permute-start.10) | collective-permute-done | bytes 65568 | tf_op jit(solution)/shard_map/ppermute | solution.py:242
  40.4 2.4 %collective-permute-start.11 = (f32[64,512]{1,0:T(8,128)S(1)}, f32[64,512]{1,0:T(8,128)S(1)}, u32[]{:S(2)}, u32[]{:S(2)}) collective-permute-start(f32[64,512]{1,0:T(8,128)S(1)} %pad_maximum_fusion.2), channel_id=1, source_target_pairs={{0,4},{1,3},{2,6},{3,1},{4,0},{5,7},{6,2},{7,5},{8,12},{9,11},{10,... | collective-permute-start | bytes 393224 | tf_op jit(solution)/shard_map/ppermute | solution.py:242
  42.9 1.1 %collective-permute-start.14 = (f32[64,512]{1,0:T(8,128)S(1)}, f32[64,512]{1,0:T(8,128)S(1)}, u32[]{:S(2)}, u32[]{:S(2)}) collective-permute-start(f32[64,512]{1,0:T(8,128)S(1)} %pad_maximum_fusion.3), channel_id=1, source_target_pairs={{0,4},{1,3},{2,6},{3,1},{4,0},{5,7},{6,2},{7,5},{8,12},{9,11},{10,... | collective-permute-start | bytes 393224 | tf_op jit(solution)/shard_map/ppermute | solution.py:242
  44.0 1.8 %collective-permute-done.11 = f32[64,512]{1,0:T(8,128)S(1)} collective-permute-done((f32[64,512]{1,0:T(8,128)S(1)}, f32[64,512]{1,0:T(8,128)S(1)}, u32[]{:S(2)}, u32[]{:S(2)}) %collective-permute-start.11) | collective-permute-done | bytes 131104 | tf_op jit(solution)/shard_map/ppermute | solution.py:242
  45.9 1.5 %collective-permute-start.12 = (f32[128,512]{1,0:T(8,128)S(1)}, f32[128,512]{1,0:T(8,128)S(1)}, u32[]{:S(2)}, u32[]{:S(2)}) collective-permute-start(f32[128,512]{1,0:T(8,128)S(1)} %pad_maximum_fusion.refs_1_), channel_id=1, source_target_pairs={{0,2},{1,5},{2,0},{3,7},{4,6},{5,1},{6,4},{7,3},{8,10},{9,13},{10,... | collective-permute-start | bytes 786440 | tf_op jit(solution)/shard_map/ppermute | solution.py:242
  47.3 2.0 %collective-permute-done.14 = f32[64,512]{1,0:T(8,128)S(1)} collective-permute-done((f32[64,512]{1,0:T(8,128)S(1)}, f32[64,512]{1,0:T(8,128)S(1)}, u32[]{:S(2)}, u32[]{:S(2)}) %collective-permute-start.14) | collective-permute-done | bytes 131104 | tf_op jit(solution)/shard_map/ppermute | solution.py:242
  49.4 1.5 %collective-permute-start.15 = (f32[128,512]{1,0:T(8,128)S(1)}, f32[128,512]{1,0:T(8,128)S(1)}, u32[]{:S(2)}, u32[]{:S(2)}) collective-permute-start(f32[128,512]{1,0:T(8,128)S(1)} %pad_maximum_fusion.1.refs_3_.refs_1_), channel_id=1, source_target_pairs={{0,2},{1,5},{2,0},{3,7},{4,6},{5,1},{6,4},{7,3},{8,10},{9,13},{10,... | collective-permute-start | bytes 786440 | tf_op jit(solution)/shard_map/ppermute | solution.py:242
  50.8 1.5 %collective-permute-done.12.refs_2_ = f32[128,512]{1,0:T(8,128)S(1)} collective-permute-done((f32[128,512]{1,0:T(8,128)S(1)}, f32[128,512]{1,0:T(8,128)S(1)}, u32[]{:S(2)}, u32[]{:S(2)}) %collective-permute-start.12) | collective-permute-done | bytes 262176 | tf_op jit(solution)/shard_map/ppermute | solution.py:242
  52.3 5.4 %grad_table.2.refs_5_.refs_3_ = f32[2992,1024]{1,0:T(8,128)} custom-call(f32[2992,256]{1,0:T(8,128)} %bitcast.16, f32[128,512]{1,0:T(8,128)S(1)} %pad_maximum_fusion.refs_1_, f32[128,512]{1,0:T(8,128)S(1)} %collective-permute-done.12.refs_2_), custom_call_target="tpu_custom_call" | custom-call | flops 2353004544 | bytes 6127616 | tf_op jit(solution)/shard_map/grad_table/pallas_call | solution.py:161
  57.7 10.8 %grad_features.1 = (f32[2992,128]{1,0:T(8,128)S(1)}, f32[2992,128]{1,0:T(8,128)S(1)}) custom-call(f32[2992,1024]{1,0:T(8,128)} %bitcast.13, f32[128,512]{1,0:T(8,128)S(1)} %pad_maximum_fusion.refs_1_, f32[128,512]{1,0:T(8,128)S(1)} %collective-permute-done.12.refs_2_, f32[128,512]{1,0:T(8,128)S(1)} %pad_maximum_fusion.1.refs_3_.refs_1_, ...), custom_call_target="tpu_custom_call" | custom-call | flops 4706009088 | bytes 12255232 | tf_op jit(solution)/shard_map/grad_features/pallas_call | solution.py:213
  68.6 5.4 %grad_table.3 = f32[2992,1024]{1,0:T(8,128)} custom-call(f32[2992,256]{1,0:T(8,128)} %bitcast.17, f32[128,512]{1,0:T(8,128)S(1)} %pad_maximum_fusion.1.refs_3_.refs_1_, f32[128,512]{1,0:T(8,128)S(1)} %collective-permute-done.15.refs_4_.refs_2_, f32[2992,1024]{1,0:T(8,128)} %grad_table.2.refs_5_.refs_3_), custom_call_target="tpu_custom_call", output_to_operand_aliasing={{}: (3, {})} | custom-call | flops 2353004544 | bytes 6127616 | tf_op jit(solution)/shard_map/grad_table/pallas_call | solution.py:161
  74.0 1.3 %add_bitcast_fusion = f32[128,2992]{0,1:T(8,128)} fusion(f32[2992,128]{1,0:T(8,128)S(1)} %get-tuple-element.16, f32[2992,128]{1,0:T(8,128)S(1)} %collective-permute-done.16), kind=kLoop, calls=%fused_computation | loop fusion | flops 382976 | bytes 4595712 | tf_op jit(solution)/shard_map/transpose | solution.py:313
  (33 shorter events, 0.6 us)
Async XLA Ops:
  5.2 7.6 %collective-permute-start = (f32[128,512]{1,0:T(8,128)S(1)}, f32[128,512]{1,0:T(8,128)S(1)}, u32[]{:S(2)}, u32[]{:S(2)}) collective-permute-start(f32[128,512]{1,0:T(8,128)S(1)} %get-tuple-element.11), channel_id=1, source_target_pairs={{0,2},{1,5},{2,0},{3,7},{4,6},{5,1},{6,4},{7,3},{8,10},{9,13},{10,... | collective-permute-start | bytes 786440 | tf_op jit(solution)/shard_map/ppermute | solution.py:242
  8.2 6.7 %copy-start = (f32[16,1024]{1,0:T(8,128)S(1)}, f32[16,1024]{1,0:T(8,128)}, u32[]{:S(2)}) copy-start(f32[16,1024]{1,0:T(8,128)} %param.5) | copy-start | bytes 196612
  12.7 6.6 %collective-permute-start.4 = (f32[128,512]{1,0:T(8,128)S(1)}, f32[128,512]{1,0:T(8,128)S(1)}, u32[]{:S(2)}, u32[]{:S(2)}) collective-permute-start(f32[128,512]{1,0:T(8,128)S(1)} %get-tuple-element.15), channel_id=1, source_target_pairs={{0,2},{1,5},{2,0},{3,7},{4,6},{5,1},{6,4},{7,3},{8,10},{9,13},{10,... | collective-permute-start | bytes 786440 | tf_op jit(solution)/shard_map/ppermute | solution.py:242
  12.9 8.3 %collective-permute-start.1 = (f32[64,512]{1,0:T(8,128)S(1)}, f32[64,512]{1,0:T(8,128)S(1)}, u32[]{:S(2)}, u32[]{:S(2)}) collective-permute-start(f32[64,512]{1,0:T(8,128)S(1)} %slice.49), channel_id=1, source_target_pairs={{0,4},{1,3},{2,6},{3,1},{4,0},{5,7},{6,2},{7,5},{8,12},{9,11},{10,... | collective-permute-start | bytes 393224 | tf_op jit(solution)/shard_map/ppermute | solution.py:242
  14.9 19.8 %collective-permute-start.9 = (f32[16,1024]{1,0:T(8,128)S(1)}, f32[16,1024]{1,0:T(8,128)S(1)}, u32[]{:S(2)}, u32[]{:S(2)}) collective-permute-start(f32[16,1024]{1,0:T(8,128)S(1)} %copy-done), channel_id=1, source_target_pairs={{0,16},{2,18},{4,20},{6,22},{8,24},{10,26},{12,28},{14,30},{16,0},... | collective-permute-start | bytes 196616 | tf_op jit(solution)/shard_map/ppermute | solution.py:255
  19.4 5.0 %collective-permute-start.5 = (f32[64,512]{1,0:T(8,128)S(1)}, f32[64,512]{1,0:T(8,128)S(1)}, u32[]{:S(2)}, u32[]{:S(2)}) collective-permute-start(f32[64,512]{1,0:T(8,128)S(1)} %slice.53), channel_id=1, source_target_pairs={{0,4},{1,3},{2,6},{3,1},{4,0},{5,7},{6,2},{7,5},{8,12},{9,11},{10,... | collective-permute-start | bytes 393224 | tf_op jit(solution)/shard_map/ppermute | solution.py:242
  21.2 5.1 %collective-permute-start.2 = (f32[32,512]{1,0:T(8,128)S(1)}, f32[32,512]{1,0:T(8,128)S(1)}, u32[]{:S(2)}, u32[]{:S(2)}) collective-permute-start(f32[32,512]{1,0:T(8,128)S(1)} %slice.51), channel_id=1, source_target_pairs={{0,8},{1,9},{2,10},{3,11},{4,12},{5,13},{6,14},{7,15},{8,0},{9,1},... | collective-permute-start | bytes 196616 | tf_op jit(solution)/shard_map/ppermute | solution.py:242
  24.5 4.5 %collective-permute-start.6 = (f32[32,512]{1,0:T(8,128)S(1)}, f32[32,512]{1,0:T(8,128)S(1)}, u32[]{:S(2)}, u32[]{:S(2)}) collective-permute-start(f32[32,512]{1,0:T(8,128)S(1)} %slice.55), channel_id=1, source_target_pairs={{0,8},{1,9},{2,10},{3,11},{4,12},{5,13},{6,14},{7,15},{8,0},{9,1},... | collective-permute-start | bytes 196616 | tf_op jit(solution)/shard_map/ppermute | solution.py:242
  26.3 6.7 %collective-permute-start.3 = (f32[32,512]{1,0:T(8,128)S(1)}, f32[32,512]{1,0:T(8,128)S(1)}, u32[]{:S(2)}, u32[]{:S(2)}) collective-permute-start(f32[32,512]{1,0:T(8,128)S(1)} %slice_add_fusion.3), channel_id=1, source_target_pairs={{0,16},{2,18},{4,20},{6,22},{8,24},{10,26},{12,28},{14,30},{16,0},... | collective-permute-start | bytes 196616 | tf_op jit(solution)/shard_map/ppermute | solution.py:248
  29.0 5.3 %collective-permute-start.7 = (f32[32,512]{1,0:T(8,128)S(1)}, f32[32,512]{1,0:T(8,128)S(1)}, u32[]{:S(2)}, u32[]{:S(2)}) collective-permute-start(f32[32,512]{1,0:T(8,128)S(1)} %slice_add_fusion.2), channel_id=1, source_target_pairs={{0,16},{2,18},{4,20},{6,22},{8,24},{10,26},{12,28},{14,30},{16,0},... | collective-permute-start | bytes 196616 | tf_op jit(solution)/shard_map/ppermute | solution.py:248
  34.6 1.2 %collective-permute-start.8 = (f32[32,2]{0,1:T(2,128)S(1)}, f32[32,2]{0,1:T(2,128)S(1)}, u32[]{:S(2)}, u32[]{:S(2)}) collective-permute-start(f32[32,2]{0,1:T(2,128)S(1)} %pad_maximum_fusion.4), channel_id=1, source_target_pairs={{0,1},{1,0},{2,3},{3,2},{4,5},{5,4},{6,7},{7,6},{8,9},{9,8},{10,11... | collective-permute-start | bytes 776 | tf_op jit(solution)/shard_map/ppermute | solution.py:289
  36.0 4.5 %collective-permute-start.10 = (f32[32,512]{1,0:T(8,128)S(1)}, f32[32,512]{1,0:T(8,128)S(1)}, u32[]{:S(2)}, u32[]{:S(2)}) collective-permute-start(f32[32,512]{1,0:T(8,128)S(1)} %get-tuple-element.21), channel_id=1, source_target_pairs={{0,8},{1,9},{2,10},{3,11},{4,12},{5,13},{6,14},{7,15},{8,0},{9,1},... | collective-permute-start | bytes 196616 | tf_op jit(solution)/shard_map/ppermute | solution.py:242
  37.7 5.2 %collective-permute-start.13 = (f32[32,512]{1,0:T(8,128)S(1)}, f32[32,512]{1,0:T(8,128)S(1)}, u32[]{:S(2)}, u32[]{:S(2)}) collective-permute-start(f32[32,512]{1,0:T(8,128)S(1)} %get-tuple-element.20), channel_id=1, source_target_pairs={{0,8},{1,9},{2,10},{3,11},{4,12},{5,13},{6,14},{7,15},{8,0},{9,1},... | collective-permute-start | bytes 196616 | tf_op jit(solution)/shard_map/ppermute | solution.py:242
  40.4 5.4 %collective-permute-start.11 = (f32[64,512]{1,0:T(8,128)S(1)}, f32[64,512]{1,0:T(8,128)S(1)}, u32[]{:S(2)}, u32[]{:S(2)}) collective-permute-start(f32[64,512]{1,0:T(8,128)S(1)} %pad_maximum_fusion.2), channel_id=1, source_target_pairs={{0,4},{1,3},{2,6},{3,1},{4,0},{5,7},{6,2},{7,5},{8,12},{9,11},{10,... | collective-permute-start | bytes 393224 | tf_op jit(solution)/shard_map/ppermute | solution.py:242
  42.9 6.4 %collective-permute-start.14 = (f32[64,512]{1,0:T(8,128)S(1)}, f32[64,512]{1,0:T(8,128)S(1)}, u32[]{:S(2)}, u32[]{:S(2)}) collective-permute-start(f32[64,512]{1,0:T(8,128)S(1)} %pad_maximum_fusion.3), channel_id=1, source_target_pairs={{0,4},{1,3},{2,6},{3,1},{4,0},{5,7},{6,2},{7,5},{8,12},{9,11},{10,... | collective-permute-start | bytes 393224 | tf_op jit(solution)/shard_map/ppermute | solution.py:242
  45.9 6.4 %collective-permute-start.12 = (f32[128,512]{1,0:T(8,128)S(1)}, f32[128,512]{1,0:T(8,128)S(1)}, u32[]{:S(2)}, u32[]{:S(2)}) collective-permute-start(f32[128,512]{1,0:T(8,128)S(1)} %pad_maximum_fusion.refs_1_), channel_id=1, source_target_pairs={{0,2},{1,5},{2,0},{3,7},{4,6},{5,1},{6,4},{7,3},{8,10},{9,13},{10,... | collective-permute-start | bytes 786440 | tf_op jit(solution)/shard_map/ppermute | solution.py:242
  49.4 8.3 %collective-permute-start.15 = (f32[128,512]{1,0:T(8,128)S(1)}, f32[128,512]{1,0:T(8,128)S(1)}, u32[]{:S(2)}, u32[]{:S(2)}) collective-permute-start(f32[128,512]{1,0:T(8,128)S(1)} %pad_maximum_fusion.1.refs_3_.refs_1_), channel_id=1, source_target_pairs={{0,2},{1,5},{2,0},{3,7},{4,6},{5,1},{6,4},{7,3},{8,10},{9,13},{10,... | collective-permute-start | bytes 786440 | tf_op jit(solution)/shard_map/ppermute | solution.py:242
  68.5 5.5 %collective-permute-start.16 = (f32[2992,128]{1,0:T(8,128)S(1)}, f32[2992,128]{1,0:T(8,128)S(1)}, u32[]{:S(2)}, u32[]{:S(2)}) collective-permute-start(f32[2992,128]{1,0:T(8,128)S(1)} %get-tuple-element.17), channel_id=1, source_target_pairs={{0,1},{1,0},{2,3},{3,2},{4,5},{5,4},{6,7},{7,6},{8,9},{9,8},{10,11... | collective-permute-start | bytes 4595720 | tf_op jit(solution)/shard_map/ppermute | solution.py:308

commit v4 on v2

--- a/solution.py
+++ b/solution.py
@@ -55,11 +55,11 @@
 
 def scores_kernel(g, m, cuts, first, *refs):
     if first:
-        feat, table, out, t_hi, t_lo, f_hi, f_lo, feat_v, table_v, acc, sems = refs
+        feat, table, keep, send, t_hi, t_lo, f_hi, f_lo, feat_v, table_v, acc, sems = refs
     else:
-        table, f_hi, f_lo, out, t_hi, t_lo, table_v, acc, sems = refs
+        table, f_hi, f_lo, keep, send, t_hi, t_lo, table_v, acc, sems = refs
     chunk = 0 if first else 1
-    width = t_hi.shape[1]
+    width = keep.shape[1]
     columns = pl.ds(chunk * width, width)
     copies = []
     for i, (at, size) in enumerate(cuts):
@@ -89,8 +89,10 @@
         else:
             acc[...] += got
     rows = acc.shape[0] // (g * m)
+    half = g * m // 2
     for p, block in enumerate(blocks(g, m)):
-        out[p * rows:(p + 1) * rows] = acc[pl.ds(pl.multiple_of(block * rows, rows), rows)]
+        out, q = (keep, p) if p < half else (send, p - half)
+        out[q * rows:(q + 1) * rows] = acc[pl.ds(pl.multiple_of(block * rows, rows), rows)]
 
 
 def scores_call(g, m, table, feat=None, halves=None, depth=512):
@@ -99,7 +101,7 @@
     imgs = (feat if first else halves[0]).shape[1]
     width = rots // CHUNKS
     cuts = cuts_of(k, depth)
-    outs = [jax.ShapeDtypeStruct((imgs, width), F32)] + [jax.ShapeDtypeStruct((k, width), BF16)] * 2
+    outs = [jax.ShapeDtypeStruct((imgs // 2, width), F32)] * 2 + [jax.ShapeDtypeStruct((k, width), BF16)] * 2
     scratch = [pltpu.VMEM((k, width), F32), pltpu.VMEM((imgs, width), F32), pltpu.SemaphoreType.DMA((2, len(cuts)))]
     if first:
         outs += [jax.ShapeDtypeStruct((k, imgs), BF16)] * 2
@@ -111,14 +113,15 @@
         out_specs=[VMEM] * len(outs),
         scratch_shapes=scratch,
         cost_estimate=pl.CostEstimate(flops=6 * k * imgs * width, bytes_accessed=4 * k * width, transcendentals=0),
-        compiler_params=pltpu.CompilerParams(vmem_limit_bytes=32 << 20),
+        compiler_params=pltpu.CompilerParams(vmem_limit_bytes=20 << 20),
         name="scores",
     )(*([feat, table] if first else [table, *halves]))
 
 
 def table_kernel(g, m, cuts, chunk, *refs):
     f_hi, f_lo, mine, far = refs[:4]
-    out, out_v, rhs, sems = refs[-4:]
+    out, token, out_v, rhs, sems = refs[-5:]
+    token[...] = jnp.zeros_like(token)
     imgs, width = rhs.shape[0] // 3, rhs.shape[1]
     n = g * m
     rows = imgs // n
@@ -150,9 +153,9 @@
     extra = [] if onto is None else [onto]
     return pl.pallas_call(
         functools.partial(table_kernel, g, m, cuts, chunk),
-        out_shape=jax.ShapeDtypeStruct((k, width * CHUNKS), F32),
+        out_shape=[jax.ShapeDtypeStruct((k, width * CHUNKS), F32), jax.ShapeDtypeStruct((8, 128), F32)],
         in_specs=[VMEM] * 4 + [HBM] * len(extra),
-        out_specs=HBM,
+        out_specs=[HBM, VMEM],
         scratch_shapes=[
             pltpu.VMEM((k, width), F32),
             pltpu.VMEM((3 * imgs, width), BF16),
@@ -167,7 +170,7 @@
 
 def features_kernel(g, m, parts, *refs):
     tables, pieces = refs[:2 * CHUNKS], refs[2 * CHUNKS:4 * CHUNKS]
-    outs, (rows_v, rhs) = refs[4 * CHUNKS:-2], refs[-2:]
+    outs, (rows_v, rhs) = refs[4 * CHUNKS + 1:-2], refs[-2:]
     n = g * m
     imgs, width = rows_v.shape
     rows = imgs // n
@@ -191,13 +194,13 @@
         out[...] = got[:, i * share:(i + 1) * share]
 
 
-def features_call(g, m, tables, pieces, parts):
+def features_call(g, m, tables, pieces, parts, after):
     k, width = tables[0].shape
     imgs = 2 * pieces[0].shape[0]
     return pl.pallas_call(
         functools.partial(features_kernel, g, m, parts),
         out_shape=[jax.ShapeDtypeStruct((k, imgs // parts), F32)] * parts,
-        in_specs=[VMEM] * (len(tables) + len(pieces)),
+        in_specs=[VMEM] * (len(tables) + len(pieces) + 1),
         out_specs=[VMEM] * parts,
         scratch_shapes=[pltpu.VMEM((imgs, width), F32), pltpu.VMEM((3 * CHUNKS * width, imgs), BF16)],
         cost_estimate=pl.CostEstimate(
@@ -205,7 +208,26 @@
         ),
         compiler_params=pltpu.CompilerParams(vmem_limit_bytes=24 << 20),
         name="grad_features",
-    )(*tables, *pieces)
+    )(*tables, *pieces, after)
+
+
+def join_kernel(g, mine, other, out):
+    rows = mine.shape[0]
+    cube = lax.div(lax.axis_index("coef"), g)
+    out[pl.ds(pl.multiple_of(cube * rows, rows), rows)] = mine[...]
+    out[pl.ds(pl.multiple_of((1 - cube) * rows, rows), rows)] = other[...]
+
+
+def join_call(g, mine, other):
+    rows, cols = mine.shape
+    return pl.pallas_call(
+        functools.partial(join_kernel, g),
+        out_shape=jax.ShapeDtypeStruct((2 * rows, cols), mine.dtype),
+        in_specs=[VMEM] * 2,
+        out_specs=VMEM,
+        compiler_params=pltpu.CompilerParams(vmem_limit_bytes=4 << 20),
+        name="join",
+    )(mine, other)
 
 
 def solution(mesh):
@@ -233,13 +255,12 @@
         if m == 1:
             return x
         if m == 2:
-            other = lax.ppermute(x, "coef", swap)
-            first = lax.axis_index("coef") < g
-            return jnp.where(first, jnp.concatenate([x, other]), jnp.concatenate([other, x]))
+            return join_call(g, x, lax.ppermute(x, "coef", swap))
         return lax.all_gather(x, "coef", axis_index_groups=outer, tiled=True)
 
-    def reduce(x):
-        for step in range(steps):
+    def reduce(keep, send):
+        x = keep + exchange(send, 0)
+        for step in range(1, steps):
             half = x.shape[0] // 2
             x = x[:half] + exchange(x[half:], step)
         return add_cubes(x)
@@ -254,14 +275,15 @@
         rots = table.shape[0]
         width = rots // CHUNKS
         scale = logit_gain / math.sqrt(k * n)
-        features, table = features.T, table.T
+        features = pltpu.with_memory_space_constraint(features.T, pltpu.HBM)
+        table = pltpu.with_memory_space_constraint(table.T, pltpu.HBM)
         goal = join_cubes(targets)
 
-        first, *rest = scores_call(g, m, table, feat=features)
+        keep, send, *rest = scores_call(g, m, table, feat=features)
         tables, halves = rest[:2], rest[2:]
-        second, *more = scores_call(g, m, table, halves=halves)
+        last_keep, last_send, *more = scores_call(g, m, table, halves=halves)
         tables = tables + more
-        scores = [scale * reduce(part) for part in (first, second)]
+        scores = [scale * reduce(keep, send), scale * reduce(last_keep, last_send)]
 
         top = functools.reduce(jnp.maximum, [jnp.max(s, axis=1, keepdims=True) for s in scores])
         expo = [jnp.exp(s - top) for s in scores]
@@ -283,15 +305,15 @@
             grad = (scale * loss_scale) * (e * norm - goal[:, c * width:(c + 1) * width])
             pieces.append(gather(grad))
 
-        grad_table = table_call(g, m, *halves, pieces[0], 0)
+        grad_table, done = table_call(g, m, *halves, pieces[0], 0)
         flat = [x for piece in pieces for x in piece]
         if r == 2:
-            send, keep = features_call(g, m, tables, flat, 2)
+            send, keep = features_call(g, m, tables, flat, 2, done)
             grad_features = keep + lax.ppermute(send, "rot", rot_swap)
         else:
-            (whole,) = features_call(g, m, tables, flat, 1)
+            (whole,) = features_call(g, m, tables, flat, 1, done)
             grad_features = lax.psum_scatter(whole, "rot", scatter_dimension=1, tiled=True)
-        grad_table = table_call(g, m, *halves, pieces[1], 1, grad_table)
+        grad_table, _ = table_call(g, m, *halves, pieces[1], 1, grad_table)
         return (grad_features.T, grad_table.T)
 
     return jax.shard_map(

time: 91 us -> 68.4 us (0.75)
  local copies, waits for them, and re-layouts: 19 us -> 0.04 us
  waiting for transfers between devices: 19.5 us -> 14.2 us
  starting transfers between devices: 25.1 us -> 27.5 us
  other arithmetic: 4.23 us -> 2.12 us
  Pallas kernels: 22.1 us -> 23.4 us
    unnamed x26 -> x2, local copies, waits for them, and re-layouts: 17.5 us -> 0.01 us
    ppermute x12, waiting for transfers between devices: 15.9 us -> 11 us  [exchange(): return lax.ppermute(x, ('coef', 'rot'), perm)]
    ppermute x12, starting transfers between devices: 15.8 us -> 19.1 us  [exchange(): return lax.ppermute(x, ('coef', 'rot'), perm)]
    add x6 -> x4, other arithmetic: 2.26 us -> 0.06 us  [reduce(): x = x[:half] + exchange(x[half:], step)]
    slice x6 -> x4, local copies, waits for them, and re-layouts: 1.52 us -> 0.03 us  [reduce(): x = x[:half] + exchange(x[half:], step)]
  transfers between devices with their start and end apart: 17 -> 17, of which waited for: 9 -> 9; matrix products, arithmetic and copies ran while one was open for 4% -> 1% of each run, Pallas kernels for 13% -> 19%
where the time goes in v4:
time: 68.4 us; the launch traced here: 68.1 us
  starting transfers between devices  27.5 us (40%)
  Pallas kernels  23.4 us (34%)
  waiting for transfers between devices  14.2 us (21%)
  other arithmetic  2.12 us (3%)
  between operations  0.82 us (1%)
    ppermute x12, starting transfers between devices, exchange(): return lax.ppermute(x, ('coef', 'rot'), perm)  19.1 us
    ppermute x12, waiting for transfers between devices, exchange(): return lax.ppermute(x, ('coef', 'rot'), perm)  11 us
    pallas_call x2, Pallas kernels, scores_call(): pl.pallas_call(functools.partial(scores_kernel, g, m, cuts, first), out_s...  9.57 us
    pallas_call x2, Pallas kernels, table_call(): pl.pallas_call(functools.partial(table_kernel, g, m, cuts, chunk), out_sh...  8.19 us
    ppermute x2, starting transfers between devices, add_cubes(): return x + lax.ppermute(x, 'coef', swap)  5.71 us
    pallas_call x1, Pallas kernels, features_call(): pl.pallas_call(functools.partial(features_kernel, g, m, parts), out_shape...  5.57 us
    ppermute x1, starting transfers between devices, join_cubes(): return join_call(g, x, lax.ppermute(x, 'coef', swap))  2.57 us
    ppermute x2, waiting for transfers between devices, add_cubes(): return x + lax.ppermute(x, 'coef', swap)  2.13 us
  transfers between devices with their start and end apart: 17, of which 9 were waited for; matrix products, arithmetic and copies ran while one was open for 1% of the time, Pallas kernels for 19%

profile of v4, /device:TPU:0, one launch (start us, length us, event | category | flops | bytes accessed | tf_op | source)
XLA Modules:
  0.0 68.1 jit_solution(11734472818965429857)
XLA Ops:
  0.6 4.9 %scores.2 = (f32[128,512]{1,0:T(8,128)S(1)}, f32[128,512]{1,0:T(8,128)S(1)}, bf16[2992,512]{1,0:T(8,128)(2,1)S(1)}, bf16[2992,512]{1,0:T(8,128)(2,1)S(1)}, bf16[...) custom-call(f32[2992,256]{1,0:T(8,128)} %bitcast.14, f32[2992,1024]{1,0:T(8,128)} %bitcast.11), custom_call_target="tpu_custom_call" | custom-call | flops 2353004544 | bytes 6127616 | tf_op jit(solution)/shard_map/scores/pallas_call | solution.py:109
  5.5 3.0 %collective-permute-start = (f32[128,512]{1,0:T(8,128)S(1)}, f32[128,512]{1,0:T(8,128)S(1)}, u32[]{:S(2)}, u32[]{:S(2)}) collective-permute-start(f32[128,512]{1,0:T(8,128)S(1)} %get-tuple-element.24), channel_id=1, source_target_pairs={{0,2},{1,5},{2,0},{3,7},{4,6},{5,1},{6,4},{7,3},{8,10},{9,13},{10,... | collective-permute-start | bytes 786440 | tf_op jit(solution)/shard_map/ppermute | solution.py:245
  8.5 4.7 %scores.3 = (f32[128,512]{1,0:T(8,128)S(1)}, f32[128,512]{1,0:T(8,128)S(1)}, bf16[2992,512]{1,0:T(8,128)(2,1)S(1)}, bf16[2992,512]{1,0:T(8,128)(2,1)S(1)}) custom-call(f32[2992,1024]{1,0:T(8,128)} %bitcast.12, bf16[2992,256]{1,0:T(8,128)(2,1)S(1)} %get-tuple-element.19.refs_1_.refs_0_, bf16[2992,256]{1,0:T(8,128)(2,1)S(1)} %get-tuple-element.20.refs_2_.refs_1_), custom_call_target="tpu_custom_call" | custom-call | flops 2353004544 | bytes 6127616 | tf_op jit(solution)/shard_map/scores/pallas_call | solution.py:109
  13.4 2.1 %collective-permute-start.1 = (f32[64,512]{1,0:T(8,128)S(1)}, f32[64,512]{1,0:T(8,128)S(1)}, u32[]{:S(2)}, u32[]{:S(2)}) collective-permute-start(f32[64,512]{1,0:T(8,128)S(1)} %slice.49), channel_id=1, source_target_pairs={{0,4},{1,3},{2,6},{3,1},{4,0},{5,7},{6,2},{7,5},{8,12},{9,11},{10,... | collective-permute-start | bytes 393224 | tf_op jit(solution)/shard_map/ppermute | solution.py:245
  15.5 2.6 %collective-permute-start.9 = (f32[16,1024]{1,0:T(8,128)S(1)}, f32[16,1024]{1,0:T(8,128)S(1)}, u32[]{:S(2)}, u32[]{:S(2)}) collective-permute-start(f32[16,1024]{1,0:T(8,128)S(1)} %copy-done), channel_id=1, source_target_pairs={{0,16},{2,18},{4,20},{6,22},{8,24},{10,26},{12,28},{14,30},{16,0},... | collective-permute-start | bytes 196616 | tf_op jit(solution)/shard_map/ppermute | solution.py:258
  18.1 1.8 %collective-permute-done.4 = f32[128,512]{1,0:T(8,128)S(1)} collective-permute-done((f32[128,512]{1,0:T(8,128)S(1)}, f32[128,512]{1,0:T(8,128)S(1)}, u32[]{:S(2)}, u32[]{:S(2)}) %collective-permute-start.4) | collective-permute-done | bytes 262176 | tf_op jit(solution)/shard_map/ppermute | solution.py:245
  19.9 1.8 %collective-permute-start.5 = (f32[64,512]{1,0:T(8,128)S(1)}, f32[64,512]{1,0:T(8,128)S(1)}, u32[]{:S(2)}, u32[]{:S(2)}) collective-permute-start(f32[64,512]{1,0:T(8,128)S(1)} %slice.53), channel_id=1, source_target_pairs={{0,4},{1,3},{2,6},{3,1},{4,0},{5,7},{6,2},{7,5},{8,12},{9,11},{10,... | collective-permute-start | bytes 393224 | tf_op jit(solution)/shard_map/ppermute | solution.py:245
  21.8 1.6 %collective-permute-start.2 = (f32[32,512]{1,0:T(8,128)S(1)}, f32[32,512]{1,0:T(8,128)S(1)}, u32[]{:S(2)}, u32[]{:S(2)}) collective-permute-start(f32[32,512]{1,0:T(8,128)S(1)} %slice.51), channel_id=1, source_target_pairs={{0,8},{1,9},{2,10},{3,11},{4,12},{5,13},{6,14},{7,15},{8,0},{9,1},... | collective-permute-start | bytes 196616 | tf_op jit(solution)/shard_map/ppermute | solution.py:245
  23.4 1.6 %collective-permute-done.5 = f32[64,512]{1,0:T(8,128)S(1)} collective-permute-done((f32[64,512]{1,0:T(8,128)S(1)}, f32[64,512]{1,0:T(8,128)S(1)}, u32[]{:S(2)}, u32[]{:S(2)}) %collective-permute-start.5) | collective-permute-done | bytes 131104 | tf_op jit(solution)/shard_map/ppermute | solution.py:245
  25.0 1.8 %collective-permute-start.6 = (f32[32,512]{1,0:T(8,128)S(1)}, f32[32,512]{1,0:T(8,128)S(1)}, u32[]{:S(2)}, u32[]{:S(2)}) collective-permute-start(f32[32,512]{1,0:T(8,128)S(1)} %slice.55), channel_id=1, source_target_pairs={{0,8},{1,9},{2,10},{3,11},{4,12},{5,13},{6,14},{7,15},{8,0},{9,1},... | collective-permute-start | bytes 196616 | tf_op jit(solution)/shard_map/ppermute | solution.py:245
  26.9 2.7 %collective-permute-start.3 = (f32[32,512]{1,0:T(8,128)S(1)}, f32[32,512]{1,0:T(8,128)S(1)}, u32[]{:S(2)}, u32[]{:S(2)}) collective-permute-start(f32[32,512]{1,0:T(8,128)S(1)} %slice_add_fusion.3), channel_id=1, source_target_pairs={{0,16},{2,18},{4,20},{6,22},{8,24},{10,26},{12,28},{14,30},{16,0},... | collective-permute-start | bytes 196616 | tf_op jit(solution)/shard_map/ppermute | solution.py:251
  29.5 3.0 %collective-permute-start.7 = (f32[32,512]{1,0:T(8,128)S(1)}, f32[32,512]{1,0:T(8,128)S(1)}, u32[]{:S(2)}, u32[]{:S(2)}) collective-permute-start(f32[32,512]{1,0:T(8,128)S(1)} %slice_add_fusion.2), channel_id=1, source_target_pairs={{0,16},{2,18},{4,20},{6,22},{8,24},{10,26},{12,28},{14,30},{16,0},... | collective-permute-start | bytes 196616 | tf_op jit(solution)/shard_map/ppermute | solution.py:251
  32.6 0.9 %collective-permute-done.3 = f32[32,512]{1,0:T(8,128)S(1)} collective-permute-done((f32[32,512]{1,0:T(8,128)S(1)}, f32[32,512]{1,0:T(8,128)S(1)}, u32[]{:S(2)}, u32[]{:S(2)}) %collective-permute-start.3) | collective-permute-done | bytes 65568 | tf_op jit(solution)/shard_map/ppermute | solution.py:251
  33.5 0.1 fusion.8
  33.6 1.2 %collective-permute-done.7 = f32[32,512]{1,0:T(8,128)S(1)} collective-permute-done((f32[32,512]{1,0:T(8,128)S(1)}, f32[32,512]{1,0:T(8,128)S(1)}, u32[]{:S(2)}, u32[]{:S(2)}) %collective-permute-start.7) | collective-permute-done | bytes 65568 | tf_op jit(solution)/shard_map/ppermute | solution.py:251
  34.8 0.1 fusion.9
  35.0 0.2 fusion.3
  35.3 1.1 %collective-permute-done.8 = f32[32,2]{0,1:T(2,128)S(1)} collective-permute-done((f32[32,2]{0,1:T(2,128)S(1)}, f32[32,2]{0,1:T(2,128)S(1)}, u32[]{:S(2)}, u32[]{:S(2)}) %collective-permute-start.8) | collective-permute-done | bytes 288 | tf_op jit(solution)/shard_map/ppermute | solution.py:293
  36.5 1.7 %collective-permute-start.10 = (f32[32,512]{1,0:T(8,128)S(1)}, f32[32,512]{1,0:T(8,128)S(1)}, u32[]{:S(2)}, u32[]{:S(2)}) collective-permute-start(f32[32,512]{1,0:T(8,128)S(1)} %get-tuple-element.35), channel_id=1, source_target_pairs={{0,8},{1,9},{2,10},{3,11},{4,12},{5,13},{6,14},{7,15},{8,0},{9,1},... | collective-permute-start | bytes 196616 | tf_op jit(solution)/shard_map/ppermute | solution.py:245
  38.3 0.4 collective-permute-start.13
  38.6 2.4 %collective-permute-done.10 = f32[32,512]{1,0:T(8,128)S(1)} collective-permute-done((f32[32,512]{1,0:T(8,128)S(1)}, f32[32,512]{1,0:T(8,128)S(1)}, u32[]{:S(2)}, u32[]{:S(2)}) %collective-permute-start.10) | collective-permute-done | bytes 65568 | tf_op jit(solution)/shard_map/ppermute | solution.py:245
  41.0 2.5 %collective-permute-start.11 = (f32[64,512]{1,0:T(8,128)S(1)}, f32[64,512]{1,0:T(8,128)S(1)}, u32[]{:S(2)}, u32[]{:S(2)}) collective-permute-start(f32[64,512]{1,0:T(8,128)S(1)} %pad_maximum_fusion.2), channel_id=1, source_target_pairs={{0,4},{1,3},{2,6},{3,1},{4,0},{5,7},{6,2},{7,5},{8,12},{9,11},{10,... | collective-permute-start | bytes 393224 | tf_op jit(solution)/shard_map/ppermute | solution.py:245
  43.5 1.1 %collective-permute-start.14 = (f32[64,512]{1,0:T(8,128)S(1)}, f32[64,512]{1,0:T(8,128)S(1)}, u32[]{:S(2)}, u32[]{:S(2)}) collective-permute-start(f32[64,512]{1,0:T(8,128)S(1)} %pad_maximum_fusion.3), channel_id=1, source_target_pairs={{0,4},{1,3},{2,6},{3,1},{4,0},{5,7},{6,2},{7,5},{8,12},{9,11},{10,... | collective-permute-start | bytes 393224 | tf_op jit(solution)/shard_map/ppermute | solution.py:245
  44.5 1.9 %collective-permute-done.11 = f32[64,512]{1,0:T(8,128)S(1)} collective-permute-done((f32[64,512]{1,0:T(8,128)S(1)}, f32[64,512]{1,0:T(8,128)S(1)}, u32[]{:S(2)}, u32[]{:S(2)}) %collective-permute-start.11) | collective-permute-done | bytes 131104 | tf_op jit(solution)/shard_map/ppermute | solution.py:245
  46.4 1.5 %collective-permute-start.12 = (f32[128,512]{1,0:T(8,128)S(1)}, f32[128,512]{1,0:T(8,128)S(1)}, u32[]{:S(2)}, u32[]{:S(2)}) collective-permute-start(f32[128,512]{1,0:T(8,128)S(1)} %pad_maximum_fusion.refs_2_.refs_4_), channel_id=1, source_target_pairs={{0,2},{1,5},{2,0},{3,7},{4,6},{5,1},{6,4},{7,3},{8,10},{9,13},{10,... | collective-permute-start | bytes 786440 | tf_op jit(solution)/shard_map/ppermute | solution.py:245
  48.0 2.0 %collective-permute-done.14 = f32[64,512]{1,0:T(8,128)S(1)} collective-permute-done((f32[64,512]{1,0:T(8,128)S(1)}, f32[64,512]{1,0:T(8,128)S(1)}, u32[]{:S(2)}, u32[]{:S(2)}) %collective-permute-start.14) | collective-permute-done | bytes 131104 | tf_op jit(solution)/shard_map/ppermute | solution.py:245
  49.9 1.5 %collective-permute-start.15 = (f32[128,512]{1,0:T(8,128)S(1)}, f32[128,512]{1,0:T(8,128)S(1)}, u32[]{:S(2)}, u32[]{:S(2)}) collective-permute-start(f32[128,512]{1,0:T(8,128)S(1)} %pad_maximum_fusion.1.refs_6_.refs_2_), channel_id=1, source_target_pairs={{0,2},{1,5},{2,0},{3,7},{4,6},{5,1},{6,4},{7,3},{8,10},{9,13},{10,... | collective-permute-start | bytes 786440 | tf_op jit(solution)/shard_map/ppermute | solution.py:245
  51.5 1.4 %collective-permute-done.12.refs_3_.refs_5_ = f32[128,512]{1,0:T(8,128)S(1)} collective-permute-done((f32[128,512]{1,0:T(8,128)S(1)}, f32[128,512]{1,0:T(8,128)S(1)}, u32[]{:S(2)}, u32[]{:S(2)}) %collective-permute-start.12) | collective-permute-done | bytes 262176 | tf_op jit(solution)/shard_map/ppermute | solution.py:245
  52.9 3.8 %grad_table.2 = (f32[2992,1024]{1,0:T(8,128)}, f32[8,128]{1,0:T(8,128)S(1)}) custom-call(bf16[2992,256]{1,0:T(8,128)(2,1)S(1)} %get-tuple-element.19.refs_1_.refs_0_, bf16[2992,256]{1,0:T(8,128)(2,1)S(1)} %get-tuple-element.20.refs_2_.refs_1_, f32[128,512]{1,0:T(8,128)S(1)} %pad_maximum_fusion.refs_2_.refs_4_, ...), custom_call_target="tpu_custom_call" | custom-call | flops 2353004544 | bytes 6127616 | tf_op jit(solution)/shard_map/grad_table/pallas_call | solution.py:154
  56.7 5.6 %grad_features.1 = (f32[2992,128]{1,0:T(8,128)S(1)}, f32[2992,128]{1,0:T(8,128)S(1)}) custom-call(bf16[2992,512]{1,0:T(8,128)(2,1)S(1)} %get-tuple-element.17.refs_0_, bf16[2992,512]{1,0:T(8,128)(2,1)S(1)} %get-tuple-element.18.refs_1_, bf16[2992,512]{1,0:T(8,128)(2,1)S(1)} %get-tuple-element.21.refs_2_, bf16[2992,512]{1,0:T(8,128)(2,1)S(1)} %get-tuple-element.22.refs_3_, ...), custom_call_target="tpu_custom_call" | custom-call | flops 4706009088 | bytes 12255232 | tf_op jit(solution)/shard_map/grad_features/pallas_call | solution.py:200
  62.3 4.4 %grad_table.3 = (f32[2992,1024]{1,0:T(8,128)}, f32[8,128]{1,0:T(8,128)}) custom-call(bf16[2992,256]{1,0:T(8,128)(2,1)S(1)} %get-tuple-element.19.refs_1_.refs_0_, bf16[2992,256]{1,0:T(8,128)(2,1)S(1)} %get-tuple-element.20.refs_2_.refs_1_, f32[128,512]{1,0:T(8,128)S(1)} %pad_maximum_fusion.1.refs_6_.refs_2_, ...), custom_call_target="tpu_custom_call", output_to_operand_aliasing={{0}: (4, {})} | custom-call | flops 2353004544 | bytes 6127616 | tf_op jit(solution)/shard_map/grad_table/pallas_call | solution.py:154
  66.8 1.3 %add_bitcast_fusion = f32[128,2992]{0,1:T(8,128)} fusion(f32[2992,128]{1,0:T(8,128)S(1)} %get-tuple-element.28, f32[2992,128]{1,0:T(8,128)S(1)} %collective-permute-done.16), kind=kLoop, calls=%fused_computation | loop fusion | flops 382976 | bytes 4595712 | tf_op jit(solution)/shard_map/transpose | solution.py:317
  (33 shorter events, 0.7 us)
Async XLA Ops:
  5.5 7.9 %collective-permute-start = (f32[128,512]{1,0:T(8,128)S(1)}, f32[128,512]{1,0:T(8,128)S(1)}, u32[]{:S(2)}, u32[]{:S(2)}) collective-permute-start(f32[128,512]{1,0:T(8,128)S(1)} %get-tuple-element.24), channel_id=1, source_target_pairs={{0,2},{1,5},{2,0},{3,7},{4,6},{5,1},{6,4},{7,3},{8,10},{9,13},{10,... | collective-permute-start | bytes 786440 | tf_op jit(solution)/shard_map/ppermute | solution.py:245
  8.5 7.0 %copy-start = (f32[16,1024]{1,0:T(8,128)S(1)}, f32[16,1024]{1,0:T(8,128)}, u32[]{:S(2)}) copy-start(f32[16,1024]{1,0:T(8,128)} %mine.1) | copy-start | bytes 196612
  13.3 6.6 %collective-permute-start.4 = (f32[128,512]{1,0:T(8,128)S(1)}, f32[128,512]{1,0:T(8,128)S(1)}, u32[]{:S(2)}, u32[]{:S(2)}) collective-permute-start(f32[128,512]{1,0:T(8,128)S(1)} %get-tuple-element.26), channel_id=1, source_target_pairs={{0,2},{1,5},{2,0},{3,7},{4,6},{5,1},{6,4},{7,3},{8,10},{9,13},{10,... | collective-permute-start | bytes 786440 | tf_op jit(solution)/shard_map/ppermute | solution.py:245
  13.4 8.3 %collective-permute-start.1 = (f32[64,512]{1,0:T(8,128)S(1)}, f32[64,512]{1,0:T(8,128)S(1)}, u32[]{:S(2)}, u32[]{:S(2)}) collective-permute-start(f32[64,512]{1,0:T(8,128)S(1)} %slice.49), channel_id=1, source_target_pairs={{0,4},{1,3},{2,6},{3,1},{4,0},{5,7},{6,2},{7,5},{8,12},{9,11},{10,... | collective-permute-start | bytes 393224 | tf_op jit(solution)/shard_map/ppermute | solution.py:245
  15.5 19.7 %collective-permute-start.9 = (f32[16,1024]{1,0:T(8,128)S(1)}, f32[16,1024]{1,0:T(8,128)S(1)}, u32[]{:S(2)}, u32[]{:S(2)}) collective-permute-start(f32[16,1024]{1,0:T(8,128)S(1)} %copy-done), channel_id=1, source_target_pairs={{0,16},{2,18},{4,20},{6,22},{8,24},{10,26},{12,28},{14,30},{16,0},... | collective-permute-start | bytes 196616 | tf_op jit(solution)/shard_map/ppermute | solution.py:258
  19.9 5.0 %collective-permute-start.5 = (f32[64,512]{1,0:T(8,128)S(1)}, f32[64,512]{1,0:T(8,128)S(1)}, u32[]{:S(2)}, u32[]{:S(2)}) collective-permute-start(f32[64,512]{1,0:T(8,128)S(1)} %slice.53), channel_id=1, source_target_pairs={{0,4},{1,3},{2,6},{3,1},{4,0},{5,7},{6,2},{7,5},{8,12},{9,11},{10,... | collective-permute-start | bytes 393224 | tf_op jit(solution)/shard_map/ppermute | solution.py:245
  21.8 5.1 %collective-permute-start.2 = (f32[32,512]{1,0:T(8,128)S(1)}, f32[32,512]{1,0:T(8,128)S(1)}, u32[]{:S(2)}, u32[]{:S(2)}) collective-permute-start(f32[32,512]{1,0:T(8,128)S(1)} %slice.51), channel_id=1, source_target_pairs={{0,8},{1,9},{2,10},{3,11},{4,12},{5,13},{6,14},{7,15},{8,0},{9,1},... | collective-permute-start | bytes 196616 | tf_op jit(solution)/shard_map/ppermute | solution.py:245
  25.0 4.5 %collective-permute-start.6 = (f32[32,512]{1,0:T(8,128)S(1)}, f32[32,512]{1,0:T(8,128)S(1)}, u32[]{:S(2)}, u32[]{:S(2)}) collective-permute-start(f32[32,512]{1,0:T(8,128)S(1)} %slice.55), channel_id=1, source_target_pairs={{0,8},{1,9},{2,10},{3,11},{4,12},{5,13},{6,14},{7,15},{8,0},{9,1},... | collective-permute-start | bytes 196616 | tf_op jit(solution)/shard_map/ppermute | solution.py:245
  26.9 6.7 %collective-permute-start.3 = (f32[32,512]{1,0:T(8,128)S(1)}, f32[32,512]{1,0:T(8,128)S(1)}, u32[]{:S(2)}, u32[]{:S(2)}) collective-permute-start(f32[32,512]{1,0:T(8,128)S(1)} %slice_add_fusion.3), channel_id=1, source_target_pairs={{0,16},{2,18},{4,20},{6,22},{8,24},{10,26},{12,28},{14,30},{16,0},... | collective-permute-start | bytes 196616 | tf_op jit(solution)/shard_map/ppermute | solution.py:251
  29.5 5.3 %collective-permute-start.7 = (f32[32,512]{1,0:T(8,128)S(1)}, f32[32,512]{1,0:T(8,128)S(1)}, u32[]{:S(2)}, u32[]{:S(2)}) collective-permute-start(f32[32,512]{1,0:T(8,128)S(1)} %slice_add_fusion.2), channel_id=1, source_target_pairs={{0,16},{2,18},{4,20},{6,22},{8,24},{10,26},{12,28},{14,30},{16,0},... | collective-permute-start | bytes 196616 | tf_op jit(solution)/shard_map/ppermute | solution.py:251
  35.2 1.2 %collective-permute-start.8 = (f32[32,2]{0,1:T(2,128)S(1)}, f32[32,2]{0,1:T(2,128)S(1)}, u32[]{:S(2)}, u32[]{:S(2)}) collective-permute-start(f32[32,2]{0,1:T(2,128)S(1)} %pad_maximum_fusion.4), channel_id=1, source_target_pairs={{0,1},{1,0},{2,3},{3,2},{4,5},{5,4},{6,7},{7,6},{8,9},{9,8},{10,11... | collective-permute-start | bytes 776 | tf_op jit(solution)/shard_map/ppermute | solution.py:293
  36.5 4.5 %collective-permute-start.10 = (f32[32,512]{1,0:T(8,128)S(1)}, f32[32,512]{1,0:T(8,128)S(1)}, u32[]{:S(2)}, u32[]{:S(2)}) collective-permute-start(f32[32,512]{1,0:T(8,128)S(1)} %get-tuple-element.35), channel_id=1, source_target_pairs={{0,8},{1,9},{2,10},{3,11},{4,12},{5,13},{6,14},{7,15},{8,0},{9,1},... | collective-permute-start | bytes 196616 | tf_op jit(solution)/shard_map/ppermute | solution.py:245
  38.3 5.2 %collective-permute-start.13 = (f32[32,512]{1,0:T(8,128)S(1)}, f32[32,512]{1,0:T(8,128)S(1)}, u32[]{:S(2)}, u32[]{:S(2)}) collective-permute-start(f32[32,512]{1,0:T(8,128)S(1)} %get-tuple-element.34), channel_id=1, source_target_pairs={{0,8},{1,9},{2,10},{3,11},{4,12},{5,13},{6,14},{7,15},{8,0},{9,1},... | collective-permute-start | bytes 196616 | tf_op jit(solution)/shard_map/ppermute | solution.py:245
  41.0 5.4 %collective-permute-start.11 = (f32[64,512]{1,0:T(8,128)S(1)}, f32[64,512]{1,0:T(8,128)S(1)}, u32[]{:S(2)}, u32[]{:S(2)}) collective-permute-start(f32[64,512]{1,0:T(8,128)S(1)} %pad_maximum_fusion.2), channel_id=1, source_target_pairs={{0,4},{1,3},{2,6},{3,1},{4,0},{5,7},{6,2},{7,5},{8,12},{9,11},{10,... | collective-permute-start | bytes 393224 | tf_op jit(solution)/shard_map/ppermute | solution.py:245
  43.5 6.4 %collective-permute-start.14 = (f32[64,512]{1,0:T(8,128)S(1)}, f32[64,512]{1,0:T(8,128)S(1)}, u32[]{:S(2)}, u32[]{:S(2)}) collective-permute-start(f32[64,512]{1,0:T(8,128)S(1)} %pad_maximum_fusion.3), channel_id=1, source_target_pairs={{0,4},{1,3},{2,6},{3,1},{4,0},{5,7},{6,2},{7,5},{8,12},{9,11},{10,... | collective-permute-start | bytes 393224 | tf_op jit(solution)/shard_map/ppermute | solution.py:245
  46.4 6.4 %collective-permute-start.12 = (f32[128,512]{1,0:T(8,128)S(1)}, f32[128,512]{1,0:T(8,128)S(1)}, u32[]{:S(2)}, u32[]{:S(2)}) collective-permute-start(f32[128,512]{1,0:T(8,128)S(1)} %pad_maximum_fusion.refs_2_.refs_4_), channel_id=1, source_target_pairs={{0,2},{1,5},{2,0},{3,7},{4,6},{5,1},{6,4},{7,3},{8,10},{9,13},{10,... | collective-permute-start | bytes 786440 | tf_op jit(solution)/shard_map/ppermute | solution.py:245
  49.9 6.7 %collective-permute-start.15 = (f32[128,512]{1,0:T(8,128)S(1)}, f32[128,512]{1,0:T(8,128)S(1)}, u32[]{:S(2)}, u32[]{:S(2)}) collective-permute-start(f32[128,512]{1,0:T(8,128)S(1)} %pad_maximum_fusion.1.refs_6_.refs_2_), channel_id=1, source_target_pairs={{0,2},{1,5},{2,0},{3,7},{4,6},{5,1},{6,4},{7,3},{8,10},{9,13},{10,... | collective-permute-start | bytes 786440 | tf_op jit(solution)/shard_map/ppermute | solution.py:245
  62.2 4.5 %collective-permute-start.16 = (f32[2992,128]{1,0:T(8,128)S(1)}, f32[2992,128]{1,0:T(8,128)S(1)}, u32[]{:S(2)}, u32[]{:S(2)}) collective-permute-start(f32[2992,128]{1,0:T(8,128)S(1)} %get-tuple-element.29), channel_id=1, source_target_pairs={{0,1},{1,0},{2,3},{3,2},{4,5},{5,4},{6,7},{7,6},{8,9},{9,8},{10,11... | collective-permute-start | bytes 4595720 | tf_op jit(solution)/shard_map/ppermute | solution.py:312

commit v5 on v4

--- a/solution.py
+++ b/solution.py
@@ -30,14 +30,19 @@
     return [(a, min(most, k - a)) for a in range(0, k, most)]
 
 
-def masks_of(g, odd):
-    bits = [1 << b for b in range(g.bit_length() - 1)]
-    if odd and len(bits) > 1:
-        bits[0], bits[1] = bits[1], bits[0]
-    return bits
-
-
-def blocks(g, m):
+ORDERS = {
+    "scores0": ((0, 2, 1), (1, 2, 0)),
+    "scores1": ((0, 1, 2), (1, 2, 0)),
+    "grads0": ((0, 1, 2), (1, 2, 0)),
+    "grads1": ((0, 1, 2), (1, 2, 0)),
+}
+
+
+def masks_of(g, use, odd):
+    return [1 << b for b in ORDERS[use][odd] if 1 << b < g]
+
+
+def blocks(g, m, use):
     me, core = lax.axis_index("coef"), lax.axis_index("rot")
     odd = lax.rem(core, 2)
     inner = lax.rem(me, g)
@@ -45,7 +50,7 @@
     for q in range(g):
         far = []
         for order in (0, 1):
-            steps = masks_of(g, order)
+            steps = masks_of(g, use, order)
             far.append(sum(bit for s, bit in enumerate(reversed(steps)) if q >> s & 1))
         flip = jnp.where(odd == 1, far[1], far[0])
         for a in range(m):
@@ -57,19 +62,18 @@
     if first:
         feat, table, keep, send, t_hi, t_lo, f_hi, f_lo, feat_v, table_v, acc, sems = refs
     else:
-        table, f_hi, f_lo, keep, send, t_hi, t_lo, table_v, acc, sems = refs
-    chunk = 0 if first else 1
+        table_v, f_hi, f_lo, keep, send, t_hi, t_lo, acc = refs
     width = keep.shape[1]
-    columns = pl.ds(chunk * width, width)
-    copies = []
-    for i, (at, size) in enumerate(cuts):
-        s = pl.ds(at, size)
-        pair = [pltpu.make_async_copy(table.at[s, columns], table_v.at[s], sems.at[0, i])]
-        if first:
-            pair.append(pltpu.make_async_copy(feat.at[s], feat_v.at[s], sems.at[1, i]))
-        for c in pair:
-            c.start()
-        copies.append(pair)
+    copies = [[] for _ in cuts]
+    if first:
+        for i, (at, size) in enumerate(cuts):
+            s = pl.ds(at, size)
+            copies[i] = [
+                pltpu.make_async_copy(table.at[s, pl.ds(0, width)], table_v.at[s], sems.at[0, i]),
+                pltpu.make_async_copy(feat.at[s], feat_v.at[s], sems.at[1, i]),
+            ]
+            for c in copies[i]:
+                c.start()
     for i, (at, size) in enumerate(cuts):
         for c in copies[i]:
             c.wait()
@@ -79,7 +83,7 @@
             f_hi[s], f_lo[s] = a_hi, a_lo
         else:
             a_hi, a_lo = f_hi[s], f_lo[s]
-        b_hi, b_lo = split(table_v[s])
+        b_hi, b_lo = split(table_v[s] if first else table_v[s, width:2 * width])
         t_hi[s], t_lo[s] = b_hi, b_lo
         left = jnp.concatenate([a_hi, a_hi, a_lo], axis=0)
         right = jnp.concatenate([b_hi, b_lo, b_hi], axis=0)
@@ -90,26 +94,27 @@
             acc[...] += got
     rows = acc.shape[0] // (g * m)
     half = g * m // 2
-    for p, block in enumerate(blocks(g, m)):
+    for p, block in enumerate(blocks(g, m, "scores0" if first else "scores1")):
         out, q = (keep, p) if p < half else (send, p - half)
         out[q * rows:(q + 1) * rows] = acc[pl.ds(pl.multiple_of(block * rows, rows), rows)]
 
 
 def scores_call(g, m, table, feat=None, halves=None, depth=512):
-    k, rots = table.shape
     first = halves is None
+    k, width = table.shape
+    width //= CHUNKS
     imgs = (feat if first else halves[0]).shape[1]
-    width = rots // CHUNKS
     cuts = cuts_of(k, depth)
     outs = [jax.ShapeDtypeStruct((imgs // 2, width), F32)] * 2 + [jax.ShapeDtypeStruct((k, width), BF16)] * 2
-    scratch = [pltpu.VMEM((k, width), F32), pltpu.VMEM((imgs, width), F32), pltpu.SemaphoreType.DMA((2, len(cuts)))]
+    scratch = [pltpu.VMEM((imgs, width), F32)]
     if first:
         outs += [jax.ShapeDtypeStruct((k, imgs), BF16)] * 2
-        scratch = [pltpu.VMEM((k, imgs), F32)] + scratch
+        scratch = [pltpu.VMEM((k, imgs), F32), pltpu.VMEM((k, width), F32)] + scratch
+        scratch += [pltpu.SemaphoreType.DMA((2, len(cuts)))]
     return pl.pallas_call(
         functools.partial(scores_kernel, g, m, cuts, first),
         out_shape=outs,
-        in_specs=[HBM, HBM] if first else [HBM, VMEM, VMEM],
+        in_specs=[HBM, HBM] if first else [VMEM] * 3,
         out_specs=[VMEM] * len(outs),
         scratch_shapes=scratch,
         cost_estimate=pl.CostEstimate(flops=6 * k * imgs * width, bytes_accessed=4 * k * width, transcendentals=0),
@@ -125,7 +130,7 @@
     imgs, width = rhs.shape[0] // 3, rhs.shape[1]
     n = g * m
     rows = imgs // n
-    for p, block in enumerate(blocks(g, m)):
+    for p, block in enumerate(blocks(g, m, f"grads{chunk}")):
         src, q = (mine, p) if p < n // 2 else (far, p - n // 2)
         hi, lo = split(src[q * rows:(q + 1) * rows])
         for j, part in enumerate((hi, lo, hi)):
@@ -177,7 +182,7 @@
     shift = 0 if parts == 1 else (1 - lax.axis_index("rot")) * (n // 2)
     for c in range(CHUNKS):
         mine, far = pieces[2 * c:2 * c + 2]
-        for p, block in enumerate(blocks(g, m)):
+        for p, block in enumerate(blocks(g, m, f"grads{c}")):
             src, q = (mine, p) if p < n // 2 else (far, p - n // 2)
             place = lax.rem(block + shift, n)
             rows_v[pl.ds(pl.multiple_of(place * rows, rows), rows)] = src[q * rows:(q + 1) * rows]
@@ -240,8 +245,8 @@
     rot_swap = [(0, 1), (1, 0)]
     steps = g.bit_length() - 1
 
-    def exchange(x, step):
-        perm = [(i * r + c, (i ^ masks_of(g, c % 2)[step]) * r + c) for i in range(n) for c in range(r)]
+    def exchange(x, use, step):
+        perm = [(i * r + c, (i ^ masks_of(g, use, c % 2)[step]) * r + c) for i in range(n) for c in range(r)]
         return lax.ppermute(x, ("coef", "rot"), perm)
 
     def add_cubes(x):
@@ -258,17 +263,17 @@
             return join_call(g, x, lax.ppermute(x, "coef", swap))
         return lax.all_gather(x, "coef", axis_index_groups=outer, tiled=True)
 
-    def reduce(keep, send):
-        x = keep + exchange(send, 0)
+    def reduce(use, keep, send):
+        x = keep + exchange(send, use, 0)
         for step in range(1, steps):
             half = x.shape[0] // 2
-            x = x[:half] + exchange(x[half:], step)
+            x = x[:half] + exchange(x[half:], use, step)
         return add_cubes(x)
 
-    def gather(x):
+    def gather(use, x):
         for step in reversed(range(1, steps)):
-            x = jnp.concatenate([x, exchange(x, step)])
-        return x, exchange(x, 0)
+            x = jnp.concatenate([x, exchange(x, use, step)])
+        return x, exchange(x, use, 0)
 
     def on_device(features, table, targets):
         imgs, k = features.shape
@@ -276,14 +281,15 @@
         width = rots // CHUNKS
         scale = logit_gain / math.sqrt(k * n)
         features = pltpu.with_memory_space_constraint(features.T, pltpu.HBM)
+        later = table.T
         table = pltpu.with_memory_space_constraint(table.T, pltpu.HBM)
         goal = join_cubes(targets)
 
         keep, send, *rest = scores_call(g, m, table, feat=features)
         tables, halves = rest[:2], rest[2:]
-        last_keep, last_send, *more = scores_call(g, m, table, halves=halves)
+        last_keep, last_send, *more = scores_call(g, m, later, halves=halves)
         tables = tables + more
-        scores = [scale * reduce(keep, send), scale * reduce(last_keep, last_send)]
+        scores = [scale * reduce("scores0", keep, send), scale * reduce("scores1", last_keep, last_send)]
 
         top = functools.reduce(jnp.maximum, [jnp.max(s, axis=1, keepdims=True) for s in scores])
         expo = [jnp.exp(s - top) for s in scores]
@@ -303,7 +309,7 @@
         pieces = []
         for c, e in enumerate(expo):
             grad = (scale * loss_scale) * (e * norm - goal[:, c * width:(c + 1) * width])
-            pieces.append(gather(grad))
+            pieces.append(gather(f"grads{c}", grad))
 
         grad_table, done = table_call(g, m, *halves, pieces[0], 0)
         flat = [x for piece in pieces for x in piece]

time: 68.4 us -> 66.4 us (0.971)
  Pallas kernels: 23.4 us -> 21.7 us
  waiting for transfers between devices: 14.2 us -> 12.9 us
  starting transfers between devices: 27.5 us -> 28.6 us
    pallas_call x2, Pallas kernels: 9.57 us -> 7.9 us  [scores_call(): pl.pallas_call(functools.partial(scores_kernel, g, m, cuts, first), out_s...]
    ppermute x12, waiting for transfers between devices: 11 us -> 9.44 us  [exchange(): return lax.ppermute(x, ('coef', 'rot'), perm)]
    ppermute x12, starting transfers between devices: 19.1 us -> 20.6 us  [exchange(): return lax.ppermute(x, ('coef', 'rot'), perm)]
  transfers between devices with their start and end apart: 17 -> 17, of which waited for: 9 -> 10; matrix products, arithmetic and copies ran while one was open for 1% -> 1% of each run, Pallas kernels for 19% -> 17%
where the time goes in v5:
time: 66.4 us; the launch traced here: 66.3 us
  starting transfers between devices  28.6 us (43%)
  Pallas kernels  21.7 us (33%)
  waiting for transfers between devices  12.9 us (19%)
  other arithmetic  2.12 us (3%)
  between operations  0.83 us (1%)
    ppermute x12, starting transfers between devices, exchange(): return lax.ppermute(x, ('coef', 'rot'), perm)  20.6 us
    ppermute x12, waiting for transfers between devices, exchange(): return lax.ppermute(x, ('coef', 'rot'), perm)  9.44 us
    pallas_call x2, Pallas kernels, table_call(): pl.pallas_call(functools.partial(table_kernel, g, m, cuts, chunk), out_sh...  8.19 us
    pallas_call x2, Pallas kernels, scores_call(): pl.pallas_call(functools.partial(scores_kernel, g, m, cuts, first), out_s...  7.9 us
    pallas_call x1, Pallas kernels, features_call(): pl.pallas_call(functools.partial(features_kernel, g, m, parts), out_shape...  5.58 us
    ppermute x2, starting transfers between devices, add_cubes(): return x + lax.ppermute(x, 'coef', swap)  5.37 us
    ppermute x1, starting transfers between devices, join_cubes(): return join_call(g, x, lax.ppermute(x, 'coef', swap))  2.59 us
    ppermute x2, waiting for transfers between devices, add_cubes(): return x + lax.ppermute(x, 'coef', swap)  2.4 us
  transfers between devices with their start and end apart: 17, of which 10 were waited for; matrix products, arithmetic and copies ran while one was open for 1% of the time, Pallas kernels for 17%

profile of v5, /device:TPU:0, one launch (start us, length us, event | category | flops | bytes accessed | tf_op | source)
XLA Modules:
  0.0 66.3 jit_solution(541942077127447259)
XLA Ops:
  0.6 5.0 %scores.2 = (f32[128,512]{1,0:T(8,128)S(1)}, f32[128,512]{1,0:T(8,128)S(1)}, bf16[2992,512]{1,0:T(8,128)(2,1)S(1)}, bf16[2992,512]{1,0:T(8,128)(2,1)S(1)}, bf16[...) custom-call(f32[2992,256]{1,0:T(8,128)} %bitcast.14, f32[2992,1024]{1,0:T(8,128)} %bitcast.11), custom_call_target="tpu_custom_call" | custom-call | flops 2353004544 | bytes 6127616 | tf_op jit(solution)/shard_map/scores/pallas_call | solution.py:114
  5.7 3.0 %collective-permute-start = (f32[128,512]{1,0:T(8,128)S(1)}, f32[128,512]{1,0:T(8,128)S(1)}, u32[]{:S(2)}, u32[]{:S(2)}) collective-permute-start(f32[128,512]{1,0:T(8,128)S(1)} %get-tuple-element.24), channel_id=1, source_target_pairs={{0,2},{1,5},{2,0},{3,7},{4,6},{5,1},{6,4},{7,3},{8,10},{9,13},{10,... | collective-permute-start | bytes 786440 | tf_op jit(solution)/shard_map/ppermute | solution.py:250
  8.7 2.9 %scores.3 = (f32[128,512]{1,0:T(8,128)S(1)}, f32[128,512]{1,0:T(8,128)S(1)}, bf16[2992,512]{1,0:T(8,128)(2,1)S(1)}, bf16[2992,512]{1,0:T(8,128)(2,1)S(1)}) custom-call(f32[2992,1024]{1,0:T(8,128)S(1)} %bitcast.12, bf16[2992,256]{1,0:T(8,128)(2,1)S(1)} %get-tuple-element.19.refs_1_.refs_0_, bf16[2992,256]{1,0:T(8,128)(2,1)S(1)} %get-tuple-element.20.refs_2_.refs_1_), custom_call_target="tpu_custom_call" | custom-call | flops 2353004544 | bytes 6127616 | tf_op jit(solution)/shard_map/scores/pallas_call | solution.py:114
  11.6 2.2 %collective-permute-start.4 = (f32[128,512]{1,0:T(8,128)S(1)}, f32[128,512]{1,0:T(8,128)S(1)}, u32[]{:S(2)}, u32[]{:S(2)}) collective-permute-start(f32[128,512]{1,0:T(8,128)S(1)} %get-tuple-element.26), channel_id=1, source_target_pairs={{0,2},{1,5},{2,0},{3,7},{4,6},{5,1},{6,4},{7,3},{8,10},{9,13},{10,... | collective-permute-start | bytes 786440 | tf_op jit(solution)/shard_map/ppermute | solution.py:250
  13.8 1.6 %collective-permute-start.1 = (f32[64,512]{1,0:T(8,128)S(1)}, f32[64,512]{1,0:T(8,128)S(1)}, u32[]{:S(2)}, u32[]{:S(2)}) collective-permute-start(f32[64,512]{1,0:T(8,128)S(1)} %slice.49), channel_id=1, source_target_pairs={{0,8},{1,9},{2,10},{3,11},{4,12},{5,13},{6,14},{7,15},{8,0},{9,1},... | collective-permute-start | bytes 393224 | tf_op jit(solution)/shard_map/ppermute | solution.py:250
  15.4 2.6 %collective-permute-start.9 = (f32[16,1024]{1,0:T(8,128)S(1)}, f32[16,1024]{1,0:T(8,128)S(1)}, u32[]{:S(2)}, u32[]{:S(2)}) collective-permute-start(f32[16,1024]{1,0:T(8,128)S(1)} %copy-done.1), channel_id=1, source_target_pairs={{0,16},{2,18},{4,20},{6,22},{8,24},{10,26},{12,28},{14,30},{16,0},... | collective-permute-start | bytes 196616 | tf_op jit(solution)/shard_map/ppermute | solution.py:263
  18.1 2.1 %collective-permute-start.5 = (f32[64,512]{1,0:T(8,128)S(1)}, f32[64,512]{1,0:T(8,128)S(1)}, u32[]{:S(2)}, u32[]{:S(2)}) collective-permute-start(f32[64,512]{1,0:T(8,128)S(1)} %slice.53), channel_id=1, source_target_pairs={{0,4},{1,9},{2,6},{3,11},{4,0},{5,13},{6,2},{7,15},{8,12},{9,1},{1... | collective-permute-start | bytes 393224 | tf_op jit(solution)/shard_map/ppermute | solution.py:250
  20.3 0.8 %collective-permute-start.2 = (f32[32,512]{1,0:T(8,128)S(1)}, f32[32,512]{1,0:T(8,128)S(1)}, u32[]{:S(2)}, u32[]{:S(2)}) collective-permute-start(f32[32,512]{1,0:T(8,128)S(1)} %slice.51), channel_id=1, source_target_pairs={{0,4},{1,3},{2,6},{3,1},{4,0},{5,7},{6,2},{7,5},{8,12},{9,11},{10,... | collective-permute-start | bytes 196616 | tf_op jit(solution)/shard_map/ppermute | solution.py:250
  21.1 2.1 %collective-permute-done.5 = f32[64,512]{1,0:T(8,128)S(1)} collective-permute-done((f32[64,512]{1,0:T(8,128)S(1)}, f32[64,512]{1,0:T(8,128)S(1)}, u32[]{:S(2)}, u32[]{:S(2)}) %collective-permute-start.5) | collective-permute-done | bytes 131104 | tf_op jit(solution)/shard_map/ppermute | solution.py:250
  23.2 2.1 %collective-permute-start.6 = (f32[32,512]{1,0:T(8,128)S(1)}, f32[32,512]{1,0:T(8,128)S(1)}, u32[]{:S(2)}, u32[]{:S(2)}) collective-permute-start(f32[32,512]{1,0:T(8,128)S(1)} %slice.55), channel_id=1, source_target_pairs={{0,8},{1,3},{2,10},{3,1},{4,12},{5,7},{6,14},{7,5},{8,0},{9,11},{1... | collective-permute-start | bytes 196616 | tf_op jit(solution)/shard_map/ppermute | solution.py:250
  25.4 2.7 %collective-permute-start.3 = (f32[32,512]{1,0:T(8,128)S(1)}, f32[32,512]{1,0:T(8,128)S(1)}, u32[]{:S(2)}, u32[]{:S(2)}) collective-permute-start(f32[32,512]{1,0:T(8,128)S(1)} %slice_add_fusion.3), channel_id=1, source_target_pairs={{0,16},{2,18},{4,20},{6,22},{8,24},{10,26},{12,28},{14,30},{16,0},... | collective-permute-start | bytes 196616 | tf_op jit(solution)/shard_map/ppermute | solution.py:256
  28.1 0.2 collective-permute-done.6
  28.3 2.7 %collective-permute-start.7 = (f32[32,512]{1,0:T(8,128)S(1)}, f32[32,512]{1,0:T(8,128)S(1)}, u32[]{:S(2)}, u32[]{:S(2)}) collective-permute-start(f32[32,512]{1,0:T(8,128)S(1)} %slice_add_fusion.2), channel_id=1, source_target_pairs={{0,16},{2,18},{4,20},{6,22},{8,24},{10,26},{12,28},{14,30},{16,0},... | collective-permute-start | bytes 196616 | tf_op jit(solution)/shard_map/ppermute | solution.py:256
  31.0 1.0 %collective-permute-done.3 = f32[32,512]{1,0:T(8,128)S(1)} collective-permute-done((f32[32,512]{1,0:T(8,128)S(1)}, f32[32,512]{1,0:T(8,128)S(1)}, u32[]{:S(2)}, u32[]{:S(2)}) %collective-permute-start.3) | collective-permute-done | bytes 65568 | tf_op jit(solution)/shard_map/ppermute | solution.py:256
  32.0 0.1 fusion.8
  32.1 1.4 %collective-permute-done.7 = f32[32,512]{1,0:T(8,128)S(1)} collective-permute-done((f32[32,512]{1,0:T(8,128)S(1)}, f32[32,512]{1,0:T(8,128)S(1)}, u32[]{:S(2)}, u32[]{:S(2)}) %collective-permute-start.7) | collective-permute-done | bytes 65568 | tf_op jit(solution)/shard_map/ppermute | solution.py:256
  33.6 0.2 fusion.3
  34.0 1.1 %collective-permute-done.8 = f32[32,2]{0,1:T(2,128)S(1)} collective-permute-done((f32[32,2]{0,1:T(2,128)S(1)}, f32[32,2]{0,1:T(2,128)S(1)}, u32[]{:S(2)}, u32[]{:S(2)}) %collective-permute-start.8) | collective-permute-done | bytes 288 | tf_op jit(solution)/shard_map/ppermute | solution.py:299
  35.2 1.5 %collective-permute-start.10 = (f32[32,512]{1,0:T(8,128)S(1)}, f32[32,512]{1,0:T(8,128)S(1)}, u32[]{:S(2)}, u32[]{:S(2)}) collective-permute-start(f32[32,512]{1,0:T(8,128)S(1)} %get-tuple-element.35), channel_id=1, source_target_pairs={{0,8},{1,3},{2,10},{3,1},{4,12},{5,7},{6,14},{7,5},{8,0},{9,11},{1... | collective-permute-start | bytes 196616 | tf_op jit(solution)/shard_map/ppermute | solution.py:250
  36.7 0.6 collective-permute-start.13
  37.3 2.2 %collective-permute-done.10 = f32[32,512]{1,0:T(8,128)S(1)} collective-permute-done((f32[32,512]{1,0:T(8,128)S(1)}, f32[32,512]{1,0:T(8,128)S(1)}, u32[]{:S(2)}, u32[]{:S(2)}) %collective-permute-start.10) | collective-permute-done | bytes 65568 | tf_op jit(solution)/shard_map/ppermute | solution.py:250
  39.5 1.4 %collective-permute-start.11 = (f32[64,512]{1,0:T(8,128)S(1)}, f32[64,512]{1,0:T(8,128)S(1)}, u32[]{:S(2)}, u32[]{:S(2)}) collective-permute-start(f32[64,512]{1,0:T(8,128)S(1)} %pad_maximum_fusion.2), channel_id=1, source_target_pairs={{0,4},{1,9},{2,6},{3,11},{4,0},{5,13},{6,2},{7,15},{8,12},{9,1},{1... | collective-permute-start | bytes 393224 | tf_op jit(solution)/shard_map/ppermute | solution.py:250
  41.0 1.6 %collective-permute-start.14 = (f32[64,512]{1,0:T(8,128)S(1)}, f32[64,512]{1,0:T(8,128)S(1)}, u32[]{:S(2)}, u32[]{:S(2)}) collective-permute-start(f32[64,512]{1,0:T(8,128)S(1)} %pad_maximum_fusion.3), channel_id=1, source_target_pairs={{0,4},{1,9},{2,6},{3,11},{4,0},{5,13},{6,2},{7,15},{8,12},{9,1},{1... | collective-permute-start | bytes 393224 | tf_op jit(solution)/shard_map/ppermute | solution.py:250
  42.6 2.0 %collective-permute-done.11 = f32[64,512]{1,0:T(8,128)S(1)} collective-permute-done((f32[64,512]{1,0:T(8,128)S(1)}, f32[64,512]{1,0:T(8,128)S(1)}, u32[]{:S(2)}, u32[]{:S(2)}) %collective-permute-start.11) | collective-permute-done | bytes 131104 | tf_op jit(solution)/shard_map/ppermute | solution.py:250
  44.6 1.6 %collective-permute-start.12 = (f32[128,512]{1,0:T(8,128)S(1)}, f32[128,512]{1,0:T(8,128)S(1)}, u32[]{:S(2)}, u32[]{:S(2)}) collective-permute-start(f32[128,512]{1,0:T(8,128)S(1)} %pad_maximum_fusion.refs_2_.refs_4_), channel_id=1, source_target_pairs={{0,2},{1,5},{2,0},{3,7},{4,6},{5,1},{6,4},{7,3},{8,10},{9,13},{10,... | collective-permute-start | bytes 786440 | tf_op jit(solution)/shard_map/ppermute | solution.py:250
  46.2 0.7 %collective-permute-done.14 = f32[64,512]{1,0:T(8,128)S(1)} collective-permute-done((f32[64,512]{1,0:T(8,128)S(1)}, f32[64,512]{1,0:T(8,128)S(1)}, u32[]{:S(2)}, u32[]{:S(2)}) %collective-permute-start.14) | collective-permute-done | bytes 131104 | tf_op jit(solution)/shard_map/ppermute | solution.py:250
  46.9 1.9 %collective-permute-start.15 = (f32[128,512]{1,0:T(8,128)S(1)}, f32[128,512]{1,0:T(8,128)S(1)}, u32[]{:S(2)}, u32[]{:S(2)}) collective-permute-start(f32[128,512]{1,0:T(8,128)S(1)} %pad_maximum_fusion.1.refs_6_.refs_2_), channel_id=1, source_target_pairs={{0,2},{1,5},{2,0},{3,7},{4,6},{5,1},{6,4},{7,3},{8,10},{9,13},{10,... | collective-permute-start | bytes 786440 | tf_op jit(solution)/shard_map/ppermute | solution.py:250
  48.8 2.2 %collective-permute-done.12.refs_3_.refs_5_ = f32[128,512]{1,0:T(8,128)S(1)} collective-permute-done((f32[128,512]{1,0:T(8,128)S(1)}, f32[128,512]{1,0:T(8,128)S(1)}, u32[]{:S(2)}, u32[]{:S(2)}) %collective-permute-start.12) | collective-permute-done | bytes 262176 | tf_op jit(solution)/shard_map/ppermute | solution.py:250
  51.0 3.8 %grad_table.2 = (f32[2992,1024]{1,0:T(8,128)}, f32[8,128]{1,0:T(8,128)S(1)}) custom-call(bf16[2992,256]{1,0:T(8,128)(2,1)S(1)} %get-tuple-element.19.refs_1_.refs_0_, bf16[2992,256]{1,0:T(8,128)(2,1)S(1)} %get-tuple-element.20.refs_2_.refs_1_, f32[128,512]{1,0:T(8,128)S(1)} %pad_maximum_fusion.refs_2_.refs_4_, ...), custom_call_target="tpu_custom_call" | custom-call | flops 2353004544 | bytes 6127616 | tf_op jit(solution)/shard_map/grad_table/pallas_call | solution.py:159
  54.8 5.6 %grad_features.1 = (f32[2992,128]{1,0:T(8,128)S(1)}, f32[2992,128]{1,0:T(8,128)S(1)}) custom-call(bf16[2992,512]{1,0:T(8,128)(2,1)S(1)} %get-tuple-element.17.refs_0_, bf16[2992,512]{1,0:T(8,128)(2,1)S(1)} %get-tuple-element.18.refs_1_, bf16[2992,512]{1,0:T(8,128)(2,1)S(1)} %get-tuple-element.21.refs_2_, bf16[2992,512]{1,0:T(8,128)(2,1)S(1)} %get-tuple-element.22.refs_3_, ...), custom_call_target="tpu_custom_call" | custom-call | flops 4706009088 | bytes 12255232 | tf_op jit(solution)/shard_map/grad_features/pallas_call | solution.py:205
  60.5 4.4 %grad_table.3 = (f32[2992,1024]{1,0:T(8,128)}, f32[8,128]{1,0:T(8,128)}) custom-call(bf16[2992,256]{1,0:T(8,128)(2,1)S(1)} %get-tuple-element.19.refs_1_.refs_0_, bf16[2992,256]{1,0:T(8,128)(2,1)S(1)} %get-tuple-element.20.refs_2_.refs_1_, f32[128,512]{1,0:T(8,128)S(1)} %pad_maximum_fusion.1.refs_6_.refs_2_, ...), custom_call_target="tpu_custom_call", output_to_operand_aliasing={{0}: (4, {})} | custom-call | flops 2353004544 | bytes 6127616 | tf_op jit(solution)/shard_map/grad_table/pallas_call | solution.py:159
  64.9 1.3 %add_bitcast_fusion = f32[128,2992]{0,1:T(8,128)} fusion(f32[2992,128]{1,0:T(8,128)S(1)} %get-tuple-element.28, f32[2992,128]{1,0:T(8,128)S(1)} %collective-permute-done.16), kind=kLoop, calls=%fused_computation | loop fusion | flops 382976 | bytes 4595712 | tf_op jit(solution)/shard_map/transpose | solution.py:323
  (35 shorter events, 0.7 us)
Async XLA Ops:
  0.6 8.0 %copy-start = (f32[1024,2992]{0,1:T(8,128)S(1)}, f32[1024,2992]{0,1:T(8,128)}, u32[]{:S(2)}) copy-start(f32[1024,2992]{0,1:T(8,128)} %param.4) | copy-start | bytes 36765700
  5.7 8.1 %collective-permute-start = (f32[128,512]{1,0:T(8,128)S(1)}, f32[128,512]{1,0:T(8,128)S(1)}, u32[]{:S(2)}, u32[]{:S(2)}) collective-permute-start(f32[128,512]{1,0:T(8,128)S(1)} %get-tuple-element.24), channel_id=1, source_target_pairs={{0,2},{1,5},{2,0},{3,7},{4,6},{5,1},{6,4},{7,3},{8,10},{9,13},{10,... | collective-permute-start | bytes 786440 | tf_op jit(solution)/shard_map/ppermute | solution.py:250
  8.7 6.8 %copy-start.1 = (f32[16,1024]{1,0:T(8,128)S(1)}, f32[16,1024]{1,0:T(8,128)}, u32[]{:S(2)}) copy-start(f32[16,1024]{1,0:T(8,128)} %mine.1) | copy-start | bytes 196612
  11.6 6.5 %collective-permute-start.4 = (f32[128,512]{1,0:T(8,128)S(1)}, f32[128,512]{1,0:T(8,128)S(1)}, u32[]{:S(2)}, u32[]{:S(2)}) collective-permute-start(f32[128,512]{1,0:T(8,128)S(1)} %get-tuple-element.26), channel_id=1, source_target_pairs={{0,2},{1,5},{2,0},{3,7},{4,6},{5,1},{6,4},{7,3},{8,10},{9,13},{10,... | collective-permute-start | bytes 786440 | tf_op jit(solution)/shard_map/ppermute | solution.py:250
  13.8 6.5 %collective-permute-start.1 = (f32[64,512]{1,0:T(8,128)S(1)}, f32[64,512]{1,0:T(8,128)S(1)}, u32[]{:S(2)}, u32[]{:S(2)}) collective-permute-start(f32[64,512]{1,0:T(8,128)S(1)} %slice.49), channel_id=1, source_target_pairs={{0,8},{1,9},{2,10},{3,11},{4,12},{5,13},{6,14},{7,15},{8,0},{9,1},... | collective-permute-start | bytes 393224 | tf_op jit(solution)/shard_map/ppermute | solution.py:250
  15.4 18.5 %collective-permute-start.9 = (f32[16,1024]{1,0:T(8,128)S(1)}, f32[16,1024]{1,0:T(8,128)S(1)}, u32[]{:S(2)}, u32[]{:S(2)}) collective-permute-start(f32[16,1024]{1,0:T(8,128)S(1)} %copy-done.1), channel_id=1, source_target_pairs={{0,16},{2,18},{4,20},{6,22},{8,24},{10,26},{12,28},{14,30},{16,0},... | collective-permute-start | bytes 196616 | tf_op jit(solution)/shard_map/ppermute | solution.py:263
  18.1 5.1 %collective-permute-start.5 = (f32[64,512]{1,0:T(8,128)S(1)}, f32[64,512]{1,0:T(8,128)S(1)}, u32[]{:S(2)}, u32[]{:S(2)}) collective-permute-start(f32[64,512]{1,0:T(8,128)S(1)} %slice.53), channel_id=1, source_target_pairs={{0,4},{1,9},{2,6},{3,11},{4,0},{5,13},{6,2},{7,15},{8,12},{9,1},{1... | collective-permute-start | bytes 393224 | tf_op jit(solution)/shard_map/ppermute | solution.py:250
  20.3 5.1 %collective-permute-start.2 = (f32[32,512]{1,0:T(8,128)S(1)}, f32[32,512]{1,0:T(8,128)S(1)}, u32[]{:S(2)}, u32[]{:S(2)}) collective-permute-start(f32[32,512]{1,0:T(8,128)S(1)} %slice.51), channel_id=1, source_target_pairs={{0,4},{1,3},{2,6},{3,1},{4,0},{5,7},{6,2},{7,5},{8,12},{9,11},{10,... | collective-permute-start | bytes 196616 | tf_op jit(solution)/shard_map/ppermute | solution.py:250
  23.2 5.0 %collective-permute-start.6 = (f32[32,512]{1,0:T(8,128)S(1)}, f32[32,512]{1,0:T(8,128)S(1)}, u32[]{:S(2)}, u32[]{:S(2)}) collective-permute-start(f32[32,512]{1,0:T(8,128)S(1)} %slice.55), channel_id=1, source_target_pairs={{0,8},{1,3},{2,10},{3,1},{4,12},{5,7},{6,14},{7,5},{8,0},{9,11},{1... | collective-permute-start | bytes 196616 | tf_op jit(solution)/shard_map/ppermute | solution.py:250
  25.4 6.6 %collective-permute-start.3 = (f32[32,512]{1,0:T(8,128)S(1)}, f32[32,512]{1,0:T(8,128)S(1)}, u32[]{:S(2)}, u32[]{:S(2)}) collective-permute-start(f32[32,512]{1,0:T(8,128)S(1)} %slice_add_fusion.3), channel_id=1, source_target_pairs={{0,16},{2,18},{4,20},{6,22},{8,24},{10,26},{12,28},{14,30},{16,0},... | collective-permute-start | bytes 196616 | tf_op jit(solution)/shard_map/ppermute | solution.py:256
  28.3 5.2 %collective-permute-start.7 = (f32[32,512]{1,0:T(8,128)S(1)}, f32[32,512]{1,0:T(8,128)S(1)}, u32[]{:S(2)}, u32[]{:S(2)}) collective-permute-start(f32[32,512]{1,0:T(8,128)S(1)} %slice_add_fusion.2), channel_id=1, source_target_pairs={{0,16},{2,18},{4,20},{6,22},{8,24},{10,26},{12,28},{14,30},{16,0},... | collective-permute-start | bytes 196616 | tf_op jit(solution)/shard_map/ppermute | solution.py:256
  33.8 1.2 %collective-permute-start.8 = (f32[32,2]{0,1:T(2,128)S(1)}, f32[32,2]{0,1:T(2,128)S(1)}, u32[]{:S(2)}, u32[]{:S(2)}) collective-permute-start(f32[32,2]{0,1:T(2,128)S(1)} %pad_maximum_fusion.4), channel_id=1, source_target_pairs={{0,1},{1,0},{2,3},{3,2},{4,5},{5,4},{6,7},{7,6},{8,9},{9,8},{10,11... | collective-permute-start | bytes 776 | tf_op jit(solution)/shard_map/ppermute | solution.py:299
  35.2 4.3 %collective-permute-start.10 = (f32[32,512]{1,0:T(8,128)S(1)}, f32[32,512]{1,0:T(8,128)S(1)}, u32[]{:S(2)}, u32[]{:S(2)}) collective-permute-start(f32[32,512]{1,0:T(8,128)S(1)} %get-tuple-element.35), channel_id=1, source_target_pairs={{0,8},{1,3},{2,10},{3,1},{4,12},{5,7},{6,14},{7,5},{8,0},{9,11},{1... | collective-permute-start | bytes 196616 | tf_op jit(solution)/shard_map/ppermute | solution.py:250
  36.7 4.3 %collective-permute-start.13 = (f32[32,512]{1,0:T(8,128)S(1)}, f32[32,512]{1,0:T(8,128)S(1)}, u32[]{:S(2)}, u32[]{:S(2)}) collective-permute-start(f32[32,512]{1,0:T(8,128)S(1)} %get-tuple-element.34), channel_id=1, source_target_pairs={{0,8},{1,3},{2,10},{3,1},{4,12},{5,7},{6,14},{7,5},{8,0},{9,11},{1... | collective-permute-start | bytes 196616 | tf_op jit(solution)/shard_map/ppermute | solution.py:250
  39.5 5.0 %collective-permute-start.11 = (f32[64,512]{1,0:T(8,128)S(1)}, f32[64,512]{1,0:T(8,128)S(1)}, u32[]{:S(2)}, u32[]{:S(2)}) collective-permute-start(f32[64,512]{1,0:T(8,128)S(1)} %pad_maximum_fusion.2), channel_id=1, source_target_pairs={{0,4},{1,9},{2,6},{3,11},{4,0},{5,13},{6,2},{7,15},{8,12},{9,1},{1... | collective-permute-start | bytes 393224 | tf_op jit(solution)/shard_map/ppermute | solution.py:250
  41.0 5.9 %collective-permute-start.14 = (f32[64,512]{1,0:T(8,128)S(1)}, f32[64,512]{1,0:T(8,128)S(1)}, u32[]{:S(2)}, u32[]{:S(2)}) collective-permute-start(f32[64,512]{1,0:T(8,128)S(1)} %pad_maximum_fusion.3), channel_id=1, source_target_pairs={{0,4},{1,9},{2,6},{3,11},{4,0},{5,13},{6,2},{7,15},{8,12},{9,1},{1... | collective-permute-start | bytes 393224 | tf_op jit(solution)/shard_map/ppermute | solution.py:250
  44.6 6.4 %collective-permute-start.12 = (f32[128,512]{1,0:T(8,128)S(1)}, f32[128,512]{1,0:T(8,128)S(1)}, u32[]{:S(2)}, u32[]{:S(2)}) collective-permute-start(f32[128,512]{1,0:T(8,128)S(1)} %pad_maximum_fusion.refs_2_.refs_4_), channel_id=1, source_target_pairs={{0,2},{1,5},{2,0},{3,7},{4,6},{5,1},{6,4},{7,3},{8,10},{9,13},{10,... | collective-permute-start | bytes 786440 | tf_op jit(solution)/shard_map/ppermute | solution.py:250
  46.9 7.9 %collective-permute-start.15 = (f32[128,512]{1,0:T(8,128)S(1)}, f32[128,512]{1,0:T(8,128)S(1)}, u32[]{:S(2)}, u32[]{:S(2)}) collective-permute-start(f32[128,512]{1,0:T(8,128)S(1)} %pad_maximum_fusion.1.refs_6_.refs_2_), channel_id=1, source_target_pairs={{0,2},{1,5},{2,0},{3,7},{4,6},{5,1},{6,4},{7,3},{8,10},{9,13},{10,... | collective-permute-start | bytes 786440 | tf_op jit(solution)/shard_map/ppermute | solution.py:250
  60.4 4.5 %collective-permute-start.16 = (f32[2992,128]{1,0:T(8,128)S(1)}, f32[2992,128]{1,0:T(8,128)S(1)}, u32[]{:S(2)}, u32[]{:S(2)}) collective-permute-start(f32[2992,128]{1,0:T(8,128)S(1)} %get-tuple-element.29), channel_id=1, source_target_pairs={{0,1},{1,0},{2,3},{3,2},{4,5},{5,4},{6,7},{7,6},{8,9},{9,8},{10,11... | collective-permute-start | bytes 4595720 | tf_op jit(solution)/shard_map/ppermute | solution.py:318

commit v6 on v5

--- a/solution.py
+++ b/solution.py
@@ -32,7 +32,7 @@
 
 ORDERS = {
     "scores0": ((0, 2, 1), (1, 2, 0)),
-    "scores1": ((0, 1, 2), (1, 2, 0)),
+    "scores1": ((0, 2, 1), (1, 2, 0)),
     "grads0": ((0, 1, 2), (1, 2, 0)),
     "grads1": ((0, 1, 2), (1, 2, 0)),
 }

time: 66.4 us -> 66.2 us (level)
  transfers between devices with their start and end apart: 17 -> 17, of which waited for: 10 -> 9; matrix products, arithmetic and copies ran while one was open for 1% -> 1% of each run, Pallas kernels for 17% -> 17%
where the time goes in v6:
time: 66.2 us; the launch traced here: 66 us
  starting transfers between devices  28.8 us (44%)
  Pallas kernels  21.7 us (33%)
  waiting for transfers between devices  12.5 us (19%)
  other arithmetic  2.12 us (3%)
  between operations  0.83 us (1%)
    ppermute x12, starting transfers between devices, exchange(): return lax.ppermute(x, ('coef', 'rot'), perm)  20.7 us
    ppermute x12, waiting for transfers between devices, exchange(): return lax.ppermute(x, ('coef', 'rot'), perm)  9.01 us
    pallas_call x2, Pallas kernels, table_call(): pl.pallas_call(functools.partial(table_kernel, g, m, cuts, chunk), out_sh...  8.2 us
    pallas_call x2, Pallas kernels, scores_call(): pl.pallas_call(functools.partial(scores_kernel, g, m, cuts, first), out_s...  7.9 us
    pallas_call x1, Pallas kernels, features_call(): pl.pallas_call(functools.partial(features_kernel, g, m, parts), out_shape...  5.58 us
    ppermute x2, starting transfers between devices, add_cubes(): return x + lax.ppermute(x, 'coef', swap)  5.38 us
    ppermute x1, starting transfers between devices, join_cubes(): return join_call(g, x, lax.ppermute(x, 'coef', swap))  2.59 us
    ppermute x2, waiting for transfers between devices, add_cubes(): return x + lax.ppermute(x, 'coef', swap)  2.39 us
  transfers between devices with their start and end apart: 17, of which 9 were waited for; matrix products, arithmetic and copies ran while one was open for 1% of the time, Pallas kernels for 17%

profile of v6, /device:TPU:0, one launch (start us, length us, event | category | flops | bytes accessed | tf_op | source)
XLA Modules:
  0.0 66.0 jit_solution(17557767084020440562)
XLA Ops:
  0.6 5.0 %scores.2 = (f32[128,512]{1,0:T(8,128)S(1)}, f32[128,512]{1,0:T(8,128)S(1)}, bf16[2992,512]{1,0:T(8,128)(2,1)S(1)}, bf16[2992,512]{1,0:T(8,128)(2,1)S(1)}, bf16[...) custom-call(f32[2992,256]{1,0:T(8,128)} %bitcast.14, f32[2992,1024]{1,0:T(8,128)} %bitcast.11), custom_call_target="tpu_custom_call" | custom-call | flops 2353004544 | bytes 6127616 | tf_op jit(solution)/shard_map/scores/pallas_call | solution.py:114
  5.7 3.0 %collective-permute-start = (f32[128,512]{1,0:T(8,128)S(1)}, f32[128,512]{1,0:T(8,128)S(1)}, u32[]{:S(2)}, u32[]{:S(2)}) collective-permute-start(f32[128,512]{1,0:T(8,128)S(1)} %get-tuple-element.24), channel_id=1, source_target_pairs={{0,2},{1,5},{2,0},{3,7},{4,6},{5,1},{6,4},{7,3},{8,10},{9,13},{10,... | collective-permute-start | bytes 786440 | tf_op jit(solution)/shard_map/ppermute | solution.py:250
  8.7 2.9 %scores.3 = (f32[128,512]{1,0:T(8,128)S(1)}, f32[128,512]{1,0:T(8,128)S(1)}, bf16[2992,512]{1,0:T(8,128)(2,1)S(1)}, bf16[2992,512]{1,0:T(8,128)(2,1)S(1)}) custom-call(f32[2992,1024]{1,0:T(8,128)S(1)} %bitcast.12, bf16[2992,256]{1,0:T(8,128)(2,1)S(1)} %get-tuple-element.19.refs_1_.refs_0_, bf16[2992,256]{1,0:T(8,128)(2,1)S(1)} %get-tuple-element.20.refs_2_.refs_1_), custom_call_target="tpu_custom_call" | custom-call | flops 2353004544 | bytes 6127616 | tf_op jit(solution)/shard_map/scores/pallas_call | solution.py:114
  11.6 2.2 %collective-permute-start.4 = (f32[128,512]{1,0:T(8,128)S(1)}, f32[128,512]{1,0:T(8,128)S(1)}, u32[]{:S(2)}, u32[]{:S(2)}) collective-permute-start(f32[128,512]{1,0:T(8,128)S(1)} %get-tuple-element.26), channel_id=1, source_target_pairs={{0,2},{1,5},{2,0},{3,7},{4,6},{5,1},{6,4},{7,3},{8,10},{9,13},{10,... | collective-permute-start | bytes 786440 | tf_op jit(solution)/shard_map/ppermute | solution.py:250
  13.8 1.6 %collective-permute-start.1 = (f32[64,512]{1,0:T(8,128)S(1)}, f32[64,512]{1,0:T(8,128)S(1)}, u32[]{:S(2)}, u32[]{:S(2)}) collective-permute-start(f32[64,512]{1,0:T(8,128)S(1)} %slice.49), channel_id=1, source_target_pairs={{0,8},{1,9},{2,10},{3,11},{4,12},{5,13},{6,14},{7,15},{8,0},{9,1},... | collective-permute-start | bytes 393224 | tf_op jit(solution)/shard_map/ppermute | solution.py:250
  15.4 2.6 %collective-permute-start.9 = (f32[16,1024]{1,0:T(8,128)S(1)}, f32[16,1024]{1,0:T(8,128)S(1)}, u32[]{:S(2)}, u32[]{:S(2)}) collective-permute-start(f32[16,1024]{1,0:T(8,128)S(1)} %copy-done.1), channel_id=1, source_target_pairs={{0,16},{2,18},{4,20},{6,22},{8,24},{10,26},{12,28},{14,30},{16,0},... | collective-permute-start | bytes 196616 | tf_op jit(solution)/shard_map/ppermute | solution.py:263
  18.1 2.2 %collective-permute-start.5 = (f32[64,512]{1,0:T(8,128)S(1)}, f32[64,512]{1,0:T(8,128)S(1)}, u32[]{:S(2)}, u32[]{:S(2)}) collective-permute-start(f32[64,512]{1,0:T(8,128)S(1)} %slice.53), channel_id=1, source_target_pairs={{0,8},{1,9},{2,10},{3,11},{4,12},{5,13},{6,14},{7,15},{8,0},{9,1},... | collective-permute-start | bytes 393224 | tf_op jit(solution)/shard_map/ppermute | solution.py:250
  20.4 1.6 %collective-permute-start.2 = (f32[32,512]{1,0:T(8,128)S(1)}, f32[32,512]{1,0:T(8,128)S(1)}, u32[]{:S(2)}, u32[]{:S(2)}) collective-permute-start(f32[32,512]{1,0:T(8,128)S(1)} %slice.51), channel_id=1, source_target_pairs={{0,4},{1,3},{2,6},{3,1},{4,0},{5,7},{6,2},{7,5},{8,12},{9,11},{10,... | collective-permute-start | bytes 196616 | tf_op jit(solution)/shard_map/ppermute | solution.py:250
  21.9 1.6 %collective-permute-done.5 = f32[64,512]{1,0:T(8,128)S(1)} collective-permute-done((f32[64,512]{1,0:T(8,128)S(1)}, f32[64,512]{1,0:T(8,128)S(1)}, u32[]{:S(2)}, u32[]{:S(2)}) %collective-permute-start.5) | collective-permute-done | bytes 131104 | tf_op jit(solution)/shard_map/ppermute | solution.py:250
  23.6 1.8 %collective-permute-start.6 = (f32[32,512]{1,0:T(8,128)S(1)}, f32[32,512]{1,0:T(8,128)S(1)}, u32[]{:S(2)}, u32[]{:S(2)}) collective-permute-start(f32[32,512]{1,0:T(8,128)S(1)} %slice.55), channel_id=1, source_target_pairs={{0,4},{1,3},{2,6},{3,1},{4,0},{5,7},{6,2},{7,5},{8,12},{9,11},{10,... | collective-permute-start | bytes 196616 | tf_op jit(solution)/shard_map/ppermute | solution.py:250
  25.4 2.7 %collective-permute-start.3 = (f32[32,512]{1,0:T(8,128)S(1)}, f32[32,512]{1,0:T(8,128)S(1)}, u32[]{:S(2)}, u32[]{:S(2)}) collective-permute-start(f32[32,512]{1,0:T(8,128)S(1)} %slice_add_fusion.3), channel_id=1, source_target_pairs={{0,16},{2,18},{4,20},{6,22},{8,24},{10,26},{12,28},{14,30},{16,0},... | collective-permute-start | bytes 196616 | tf_op jit(solution)/shard_map/ppermute | solution.py:256
  28.0 2.7 %collective-permute-start.7 = (f32[32,512]{1,0:T(8,128)S(1)}, f32[32,512]{1,0:T(8,128)S(1)}, u32[]{:S(2)}, u32[]{:S(2)}) collective-permute-start(f32[32,512]{1,0:T(8,128)S(1)} %slice_add_fusion.2), channel_id=1, source_target_pairs={{0,16},{2,18},{4,20},{6,22},{8,24},{10,26},{12,28},{14,30},{16,0},... | collective-permute-start | bytes 196616 | tf_op jit(solution)/shard_map/ppermute | solution.py:256
  30.7 1.4 %collective-permute-done.3 = f32[32,512]{1,0:T(8,128)S(1)} collective-permute-done((f32[32,512]{1,0:T(8,128)S(1)}, f32[32,512]{1,0:T(8,128)S(1)}, u32[]{:S(2)}, u32[]{:S(2)}) %collective-permute-start.3) | collective-permute-done | bytes 65568 | tf_op jit(solution)/shard_map/ppermute | solution.py:256
  32.1 0.1 fusion.8
  32.2 1.0 %collective-permute-done.7 = f32[32,512]{1,0:T(8,128)S(1)} collective-permute-done((f32[32,512]{1,0:T(8,128)S(1)}, f32[32,512]{1,0:T(8,128)S(1)}, u32[]{:S(2)}, u32[]{:S(2)}) %collective-permute-start.7) | collective-permute-done | bytes 65568 | tf_op jit(solution)/shard_map/ppermute | solution.py:256
  33.3 0.1 fusion.9
  33.4 0.2 fusion.3
  33.7 1.1 %collective-permute-done.8 = f32[32,2]{0,1:T(2,128)S(1)} collective-permute-done((f32[32,2]{0,1:T(2,128)S(1)}, f32[32,2]{0,1:T(2,128)S(1)}, u32[]{:S(2)}, u32[]{:S(2)}) %collective-permute-start.8) | collective-permute-done | bytes 288 | tf_op jit(solution)/shard_map/ppermute | solution.py:299
  35.0 1.7 %collective-permute-start.10 = (f32[32,512]{1,0:T(8,128)S(1)}, f32[32,512]{1,0:T(8,128)S(1)}, u32[]{:S(2)}, u32[]{:S(2)}) collective-permute-start(f32[32,512]{1,0:T(8,128)S(1)} %get-tuple-element.35), channel_id=1, source_target_pairs={{0,8},{1,3},{2,10},{3,1},{4,12},{5,7},{6,14},{7,5},{8,0},{9,11},{1... | collective-permute-start | bytes 196616 | tf_op jit(solution)/shard_map/ppermute | solution.py:250
  36.7 0.4 collective-permute-start.13
  37.0 2.2 %collective-permute-done.10 = f32[32,512]{1,0:T(8,128)S(1)} collective-permute-done((f32[32,512]{1,0:T(8,128)S(1)}, f32[32,512]{1,0:T(8,128)S(1)}, u32[]{:S(2)}, u32[]{:S(2)}) %collective-permute-start.10) | collective-permute-done | bytes 65568 | tf_op jit(solution)/shard_map/ppermute | solution.py:250
  39.3 1.7 %collective-permute-start.11 = (f32[64,512]{1,0:T(8,128)S(1)}, f32[64,512]{1,0:T(8,128)S(1)}, u32[]{:S(2)}, u32[]{:S(2)}) collective-permute-start(f32[64,512]{1,0:T(8,128)S(1)} %pad_maximum_fusion.2), channel_id=1, source_target_pairs={{0,4},{1,9},{2,6},{3,11},{4,0},{5,13},{6,2},{7,15},{8,12},{9,1},{1... | collective-permute-start | bytes 393224 | tf_op jit(solution)/shard_map/ppermute | solution.py:250
  41.0 1.6 %collective-permute-start.14 = (f32[64,512]{1,0:T(8,128)S(1)}, f32[64,512]{1,0:T(8,128)S(1)}, u32[]{:S(2)}, u32[]{:S(2)}) collective-permute-start(f32[64,512]{1,0:T(8,128)S(1)} %pad_maximum_fusion.3), channel_id=1, source_target_pairs={{0,4},{1,9},{2,6},{3,11},{4,0},{5,13},{6,2},{7,15},{8,12},{9,1},{1... | collective-permute-start | bytes 393224 | tf_op jit(solution)/shard_map/ppermute | solution.py:250
  42.5 1.8 %collective-permute-done.11 = f32[64,512]{1,0:T(8,128)S(1)} collective-permute-done((f32[64,512]{1,0:T(8,128)S(1)}, f32[64,512]{1,0:T(8,128)S(1)}, u32[]{:S(2)}, u32[]{:S(2)}) %collective-permute-start.11) | collective-permute-done | bytes 131104 | tf_op jit(solution)/shard_map/ppermute | solution.py:250
  44.4 1.6 %collective-permute-start.12 = (f32[128,512]{1,0:T(8,128)S(1)}, f32[128,512]{1,0:T(8,128)S(1)}, u32[]{:S(2)}, u32[]{:S(2)}) collective-permute-start(f32[128,512]{1,0:T(8,128)S(1)} %pad_maximum_fusion.refs_2_.refs_4_), channel_id=1, source_target_pairs={{0,2},{1,5},{2,0},{3,7},{4,6},{5,1},{6,4},{7,3},{8,10},{9,13},{10,... | collective-permute-start | bytes 786440 | tf_op jit(solution)/shard_map/ppermute | solution.py:250
  46.0 1.1 %collective-permute-done.14 = f32[64,512]{1,0:T(8,128)S(1)} collective-permute-done((f32[64,512]{1,0:T(8,128)S(1)}, f32[64,512]{1,0:T(8,128)S(1)}, u32[]{:S(2)}, u32[]{:S(2)}) %collective-permute-start.14) | collective-permute-done | bytes 131104 | tf_op jit(solution)/shard_map/ppermute | solution.py:250
  47.2 1.5 %collective-permute-start.15 = (f32[128,512]{1,0:T(8,128)S(1)}, f32[128,512]{1,0:T(8,128)S(1)}, u32[]{:S(2)}, u32[]{:S(2)}) collective-permute-start(f32[128,512]{1,0:T(8,128)S(1)} %pad_maximum_fusion.1.refs_6_.refs_2_), channel_id=1, source_target_pairs={{0,2},{1,5},{2,0},{3,7},{4,6},{5,1},{6,4},{7,3},{8,10},{9,13},{10,... | collective-permute-start | bytes 786440 | tf_op jit(solution)/shard_map/ppermute | solution.py:250
  48.6 2.2 %collective-permute-done.12.refs_3_.refs_5_ = f32[128,512]{1,0:T(8,128)S(1)} collective-permute-done((f32[128,512]{1,0:T(8,128)S(1)}, f32[128,512]{1,0:T(8,128)S(1)}, u32[]{:S(2)}, u32[]{:S(2)}) %collective-permute-start.12) | collective-permute-done | bytes 262176 | tf_op jit(solution)/shard_map/ppermute | solution.py:250
  50.8 3.8 %grad_table.2 = (f32[2992,1024]{1,0:T(8,128)}, f32[8,128]{1,0:T(8,128)S(1)}) custom-call(bf16[2992,256]{1,0:T(8,128)(2,1)S(1)} %get-tuple-element.19.refs_1_.refs_0_, bf16[2992,256]{1,0:T(8,128)(2,1)S(1)} %get-tuple-element.20.refs_2_.refs_1_, f32[128,512]{1,0:T(8,128)S(1)} %pad_maximum_fusion.refs_2_.refs_4_, ...), custom_call_target="tpu_custom_call" | custom-call | flops 2353004544 | bytes 6127616 | tf_op jit(solution)/shard_map/grad_table/pallas_call | solution.py:159
  54.6 5.6 %grad_features.1 = (f32[2992,128]{1,0:T(8,128)S(1)}, f32[2992,128]{1,0:T(8,128)S(1)}) custom-call(bf16[2992,512]{1,0:T(8,128)(2,1)S(1)} %get-tuple-element.17.refs_0_, bf16[2992,512]{1,0:T(8,128)(2,1)S(1)} %get-tuple-element.18.refs_1_, bf16[2992,512]{1,0:T(8,128)(2,1)S(1)} %get-tuple-element.21.refs_2_, bf16[2992,512]{1,0:T(8,128)(2,1)S(1)} %get-tuple-element.22.refs_3_, ...), custom_call_target="tpu_custom_call" | custom-call | flops 4706009088 | bytes 12255232 | tf_op jit(solution)/shard_map/grad_features/pallas_call | solution.py:205
  60.3 4.4 %grad_table.3 = (f32[2992,1024]{1,0:T(8,128)}, f32[8,128]{1,0:T(8,128)}) custom-call(bf16[2992,256]{1,0:T(8,128)(2,1)S(1)} %get-tuple-element.19.refs_1_.refs_0_, bf16[2992,256]{1,0:T(8,128)(2,1)S(1)} %get-tuple-element.20.refs_2_.refs_1_, f32[128,512]{1,0:T(8,128)S(1)} %pad_maximum_fusion.1.refs_6_.refs_2_, ...), custom_call_target="tpu_custom_call", output_to_operand_aliasing={{0}: (4, {})} | custom-call | flops 2353004544 | bytes 6127616 | tf_op jit(solution)/shard_map/grad_table/pallas_call | solution.py:159
  64.7 1.3 %add_bitcast_fusion = f32[128,2992]{0,1:T(8,128)} fusion(f32[2992,128]{1,0:T(8,128)S(1)} %get-tuple-element.28, f32[2992,128]{1,0:T(8,128)S(1)} %collective-permute-done.16), kind=kLoop, calls=%fused_computation | loop fusion | flops 382976 | bytes 4595712 | tf_op jit(solution)/shard_map/transpose | solution.py:323
  (35 shorter events, 0.6 us)
Async XLA Ops:
  0.6 8.0 %copy-start = (f32[1024,2992]{0,1:T(8,128)S(1)}, f32[1024,2992]{0,1:T(8,128)}, u32[]{:S(2)}) copy-start(f32[1024,2992]{0,1:T(8,128)} %param.4) | copy-start | bytes 36765700
  5.7 8.1 %collective-permute-start = (f32[128,512]{1,0:T(8,128)S(1)}, f32[128,512]{1,0:T(8,128)S(1)}, u32[]{:S(2)}, u32[]{:S(2)}) collective-permute-start(f32[128,512]{1,0:T(8,128)S(1)} %get-tuple-element.24), channel_id=1, source_target_pairs={{0,2},{1,5},{2,0},{3,7},{4,6},{5,1},{6,4},{7,3},{8,10},{9,13},{10,... | collective-permute-start | bytes 786440 | tf_op jit(solution)/shard_map/ppermute | solution.py:250
  8.7 6.8 %copy-start.1 = (f32[16,1024]{1,0:T(8,128)S(1)}, f32[16,1024]{1,0:T(8,128)}, u32[]{:S(2)}) copy-start(f32[16,1024]{1,0:T(8,128)} %mine.1) | copy-start | bytes 196612
  11.6 6.5 %collective-permute-start.4 = (f32[128,512]{1,0:T(8,128)S(1)}, f32[128,512]{1,0:T(8,128)S(1)}, u32[]{:S(2)}, u32[]{:S(2)}) collective-permute-start(f32[128,512]{1,0:T(8,128)S(1)} %get-tuple-element.26), channel_id=1, source_target_pairs={{0,2},{1,5},{2,0},{3,7},{4,6},{5,1},{6,4},{7,3},{8,10},{9,13},{10,... | collective-permute-start | bytes 786440 | tf_op jit(solution)/shard_map/ppermute | solution.py:250
  13.8 6.5 %collective-permute-start.1 = (f32[64,512]{1,0:T(8,128)S(1)}, f32[64,512]{1,0:T(8,128)S(1)}, u32[]{:S(2)}, u32[]{:S(2)}) collective-permute-start(f32[64,512]{1,0:T(8,128)S(1)} %slice.49), channel_id=1, source_target_pairs={{0,8},{1,9},{2,10},{3,11},{4,12},{5,13},{6,14},{7,15},{8,0},{9,1},... | collective-permute-start | bytes 393224 | tf_op jit(solution)/shard_map/ppermute | solution.py:250
  15.4 18.3 %collective-permute-start.9 = (f32[16,1024]{1,0:T(8,128)S(1)}, f32[16,1024]{1,0:T(8,128)S(1)}, u32[]{:S(2)}, u32[]{:S(2)}) collective-permute-start(f32[16,1024]{1,0:T(8,128)S(1)} %copy-done.1), channel_id=1, source_target_pairs={{0,16},{2,18},{4,20},{6,22},{8,24},{10,26},{12,28},{14,30},{16,0},... | collective-permute-start | bytes 196616 | tf_op jit(solution)/shard_map/ppermute | solution.py:263
  18.1 5.4 %collective-permute-start.5 = (f32[64,512]{1,0:T(8,128)S(1)}, f32[64,512]{1,0:T(8,128)S(1)}, u32[]{:S(2)}, u32[]{:S(2)}) collective-permute-start(f32[64,512]{1,0:T(8,128)S(1)} %slice.53), channel_id=1, source_target_pairs={{0,8},{1,9},{2,10},{3,11},{4,12},{5,13},{6,14},{7,15},{8,0},{9,1},... | collective-permute-start | bytes 393224 | tf_op jit(solution)/shard_map/ppermute | solution.py:250
  20.4 5.0 %collective-permute-start.2 = (f32[32,512]{1,0:T(8,128)S(1)}, f32[32,512]{1,0:T(8,128)S(1)}, u32[]{:S(2)}, u32[]{:S(2)}) collective-permute-start(f32[32,512]{1,0:T(8,128)S(1)} %slice.51), channel_id=1, source_target_pairs={{0,4},{1,3},{2,6},{3,1},{4,0},{5,7},{6,2},{7,5},{8,12},{9,11},{10,... | collective-permute-start | bytes 196616 | tf_op jit(solution)/shard_map/ppermute | solution.py:250
  23.6 4.4 %collective-permute-start.6 = (f32[32,512]{1,0:T(8,128)S(1)}, f32[32,512]{1,0:T(8,128)S(1)}, u32[]{:S(2)}, u32[]{:S(2)}) collective-permute-start(f32[32,512]{1,0:T(8,128)S(1)} %slice.55), channel_id=1, source_target_pairs={{0,4},{1,3},{2,6},{3,1},{4,0},{5,7},{6,2},{7,5},{8,12},{9,11},{10,... | collective-permute-start | bytes 196616 | tf_op jit(solution)/shard_map/ppermute | solution.py:250
  25.4 6.8 %collective-permute-start.3 = (f32[32,512]{1,0:T(8,128)S(1)}, f32[32,512]{1,0:T(8,128)S(1)}, u32[]{:S(2)}, u32[]{:S(2)}) collective-permute-start(f32[32,512]{1,0:T(8,128)S(1)} %slice_add_fusion.3), channel_id=1, source_target_pairs={{0,16},{2,18},{4,20},{6,22},{8,24},{10,26},{12,28},{14,30},{16,0},... | collective-permute-start | bytes 196616 | tf_op jit(solution)/shard_map/ppermute | solution.py:256
  28.0 5.2 %collective-permute-start.7 = (f32[32,512]{1,0:T(8,128)S(1)}, f32[32,512]{1,0:T(8,128)S(1)}, u32[]{:S(2)}, u32[]{:S(2)}) collective-permute-start(f32[32,512]{1,0:T(8,128)S(1)} %slice_add_fusion.2), channel_id=1, source_target_pairs={{0,16},{2,18},{4,20},{6,22},{8,24},{10,26},{12,28},{14,30},{16,0},... | collective-permute-start | bytes 196616 | tf_op jit(solution)/shard_map/ppermute | solution.py:256
  33.6 1.2 %collective-permute-start.8 = (f32[32,2]{0,1:T(2,128)S(1)}, f32[32,2]{0,1:T(2,128)S(1)}, u32[]{:S(2)}, u32[]{:S(2)}) collective-permute-start(f32[32,2]{0,1:T(2,128)S(1)} %pad_maximum_fusion.4), channel_id=1, source_target_pairs={{0,1},{1,0},{2,3},{3,2},{4,5},{5,4},{6,7},{7,6},{8,9},{9,8},{10,11... | collective-permute-start | bytes 776 | tf_op jit(solution)/shard_map/ppermute | solution.py:299
  35.0 4.3 %collective-permute-start.10 = (f32[32,512]{1,0:T(8,128)S(1)}, f32[32,512]{1,0:T(8,128)S(1)}, u32[]{:S(2)}, u32[]{:S(2)}) collective-permute-start(f32[32,512]{1,0:T(8,128)S(1)} %get-tuple-element.35), channel_id=1, source_target_pairs={{0,8},{1,3},{2,10},{3,1},{4,12},{5,7},{6,14},{7,5},{8,0},{9,11},{1... | collective-permute-start | bytes 196616 | tf_op jit(solution)/shard_map/ppermute | solution.py:250
  36.7 4.3 %collective-permute-start.13 = (f32[32,512]{1,0:T(8,128)S(1)}, f32[32,512]{1,0:T(8,128)S(1)}, u32[]{:S(2)}, u32[]{:S(2)}) collective-permute-start(f32[32,512]{1,0:T(8,128)S(1)} %get-tuple-element.34), channel_id=1, source_target_pairs={{0,8},{1,3},{2,10},{3,1},{4,12},{5,7},{6,14},{7,5},{8,0},{9,11},{1... | collective-permute-start | bytes 196616 | tf_op jit(solution)/shard_map/ppermute | solution.py:250
  39.3 5.0 %collective-permute-start.11 = (f32[64,512]{1,0:T(8,128)S(1)}, f32[64,512]{1,0:T(8,128)S(1)}, u32[]{:S(2)}, u32[]{:S(2)}) collective-permute-start(f32[64,512]{1,0:T(8,128)S(1)} %pad_maximum_fusion.2), channel_id=1, source_target_pairs={{0,4},{1,9},{2,6},{3,11},{4,0},{5,13},{6,2},{7,15},{8,12},{9,1},{1... | collective-permute-start | bytes 393224 | tf_op jit(solution)/shard_map/ppermute | solution.py:250
  41.0 6.2 %collective-permute-start.14 = (f32[64,512]{1,0:T(8,128)S(1)}, f32[64,512]{1,0:T(8,128)S(1)}, u32[]{:S(2)}, u32[]{:S(2)}) collective-permute-start(f32[64,512]{1,0:T(8,128)S(1)} %pad_maximum_fusion.3), channel_id=1, source_target_pairs={{0,4},{1,9},{2,6},{3,11},{4,0},{5,13},{6,2},{7,15},{8,12},{9,1},{1... | collective-permute-start | bytes 393224 | tf_op jit(solution)/shard_map/ppermute | solution.py:250
  44.4 6.4 %collective-permute-start.12 = (f32[128,512]{1,0:T(8,128)S(1)}, f32[128,512]{1,0:T(8,128)S(1)}, u32[]{:S(2)}, u32[]{:S(2)}) collective-permute-start(f32[128,512]{1,0:T(8,128)S(1)} %pad_maximum_fusion.refs_2_.refs_4_), channel_id=1, source_target_pairs={{0,2},{1,5},{2,0},{3,7},{4,6},{5,1},{6,4},{7,3},{8,10},{9,13},{10,... | collective-permute-start | bytes 786440 | tf_op jit(solution)/shard_map/ppermute | solution.py:250
  47.2 7.4 %collective-permute-start.15 = (f32[128,512]{1,0:T(8,128)S(1)}, f32[128,512]{1,0:T(8,128)S(1)}, u32[]{:S(2)}, u32[]{:S(2)}) collective-permute-start(f32[128,512]{1,0:T(8,128)S(1)} %pad_maximum_fusion.1.refs_6_.refs_2_), channel_id=1, source_target_pairs={{0,2},{1,5},{2,0},{3,7},{4,6},{5,1},{6,4},{7,3},{8,10},{9,13},{10,... | collective-permute-start | bytes 786440 | tf_op jit(solution)/shard_map/ppermute | solution.py:250
  60.2 4.5 %collective-permute-start.16 = (f32[2992,128]{1,0:T(8,128)S(1)}, f32[2992,128]{1,0:T(8,128)S(1)}, u32[]{:S(2)}, u32[]{:S(2)}) collective-permute-start(f32[2992,128]{1,0:T(8,128)S(1)} %get-tuple-element.29), channel_id=1, source_target_pairs={{0,1},{1,0},{2,3},{3,2},{4,5},{5,4},{6,7},{7,6},{8,9},{9,8},{10,11... | collective-permute-start | bytes 4595720 | tf_op jit(solution)/shard_map/ppermute | solution.py:318
